TPU v7x, 32 devices: a whole 2x2x4 slice. The times are simulated.
32 devices in a mesh: tile: 8 (over z, y), src: 4 (over x, core).
Axes of the slice: x: 2, y: 2, z: 4, core: 2. Of those that a mesh axis runs over, the one named last changes fastest.
Arguments:
- excitation: bfloat16 [2, 512, 8192], P(None, 'src', 'tile'), may hold values from -6 to 6
- near_blocks: bfloat16 [16, 3, 2, 512, 512], P('tile'), may hold values from -0.02734375 to 0.02734375
- source_basis: bfloat16 [16, 2, 24, 512], P('tile'), may hold values from -0.1875 to 0.1875
- target_basis: bfloat16 [16, 2, 24, 512], P('tile'), may hold values from -0.625 to 0.625
- coupling: bfloat16 [2, 384, 384], P(None, None, 'tile'), may hold values from -0.109375 to 0.109375
- pair_rank: int32 [16, 16], P(None, 'tile'), may hold values from 2 to 24
- far_link: int32 [16, 16], P(None, 'tile'), may hold values 0 or 1
- focal_kernel: bfloat16 [2, 64, 8192], P(None, None, 'tile'), may hold values from -0.046875 to 0.046875
- focal_target: float32 [64], replicated, may hold values from 0.3 to 0.9
- focal_owner: int32 [64], replicated, may hold values from 0 to 63, each once
Outputs:
- field: float32 [2, 512, 8192], P(None, 'src', 'tile')
- focal_residual: float32 [64], P('tile')
- adjoint: float32 [2, 512, 8192], P(None, 'src', 'tile')
Inputs may be any that keep to these rules, and one draw needn't show every extreme that they name: `focal_owner`: each focal point has its own slot; slot k belongs to index k // 8 of tile.
All inputs are finite; a program needn't handle non-finite values. No bound on the sum of `far_link` on one device may be relied on, other than what follows from the above.
Results may differ from a plain program's by a relative error of at most 0.006.
Values may be sent and summed in bfloat16 or wider, within the bound.
No kernel may reach another device: no remote copies, remote signals or barrier semaphores. Data moves between devices by JAX's collectives and lax.ppermute only.
A program may use at most 64 MiB of HBM per device.

v0:
```python
import jax
import jax.numpy as jnp
from jax import lax
from jax.sharding import PartitionSpec as P

TILE = 512
RANK = 24


DAMPING = 0.8


def extended(x, sides, width):
    for axis, dim in sides:
        size, length = (lax.axis_size(axis), x.shape[dim])
        up = [(i, (i + 1) % size) for i in range(size)]
        down = [(j, i) for i, j in up]
        last = lax.slice_in_dim(x, length - width, length, axis=dim)
        initial = lax.slice_in_dim(x, 0, width, axis=dim)
        before = lax.ppermute(last, axis, up)
        after = lax.ppermute(initial, axis, down)
        x = jnp.concatenate([before, x, after], axis=dim)
    return x


def plain_dot(left, right, contract):
    return lax.dot_general(
        left, right, (((1,), (contract,)), ((), ())), preferred_element_type=jnp.float32
    )


def complex_dot(left_re, left_im, right_re, right_im, contract):
    real_part = plain_dot(left_re, right_re, contract) - plain_dot(left_im, right_im, contract)
    imag_part = plain_dot(left_re, right_im, contract) + plain_dot(left_im, right_re, contract)
    return (real_part, imag_part)


def per_device(
    excitation,
    near_blocks,
    source_basis,
    target_basis,
    coupling,
    pair_rank,
    far_link,
    focal_kernel,
    focal_target,
    focal_owner,
):
    tile_count = near_blocks.shape[0]
    src_rows = excitation.shape[1]
    tiles = pair_rank.shape[0]
    focal_count = focal_target.shape[0]
    first_tile = lax.axis_index("tile") * tile_count
    global_tiles = first_tile + jnp.arange(tile_count)
    source_tiles = jnp.arange(tiles)[:, None]
    distance = (global_tiles[None, :] - source_tiles) % tiles
    far_pairs = (far_link == 1) & (distance != 0) & (distance != 1) & (distance != tiles - 1)
    levels = jnp.arange(RANK)
    rank_limit = pair_rank[:, None, :, None]
    rank_mask = (
        far_pairs[:, None, :, None]
        & (levels[None, :, None, None] < rank_limit)
        & (levels[None, None, None, :] < rank_limit)
    )
    rank_mask = rank_mask.reshape(tiles * RANK, tile_count * RANK)
    masked = coupling * rank_mask.astype(coupling.dtype)
    flipped = lax.all_to_all(masked, "tile", split_axis=1, concat_axis=2, tiled=True)

    def apply_transpose(field):
        field_bf = field.astype(jnp.bfloat16)
        moved_re = [[], [], []]
        moved_im = [[], [], []]
        proj_re = []
        proj_im = []
        for tile_here in range(tile_count):
            own = field_bf[:, :, tile_here * TILE : (tile_here + 1) * TILE]
            for offset in range(3):
                part_re, part_im = complex_dot(
                    own[0],
                    own[1],
                    near_blocks[tile_here, offset, 0],
                    near_blocks[tile_here, offset, 1],
                    1,
                )
                moved_re[offset].append(part_re)
                moved_im[offset].append(part_im)
            part_re, part_im = complex_dot(
                own[0], own[1], target_basis[tile_here, 0], target_basis[tile_here, 1], 1
            )
            proj_re.append(part_re)
            proj_im.append(part_im)
        moved = [
            jnp.stack([jnp.concatenate(moved_re[k], axis=1), jnp.concatenate(moved_im[k], axis=1)])
            for k in range(3)
        ]
        width = tile_count * TILE
        edges = jnp.concatenate([moved[0][:, :, 0:TILE], moved[2][:, :, width - TILE :]], axis=2)
        arrived = extended(edges.astype(jnp.bfloat16), (("tile", 2),), TILE).astype(edges.dtype)
        from_left = jnp.concatenate(
            [arrived[:, :, 0:TILE], moved[2][:, :, 0 : width - TILE]], axis=2
        )
        from_right = jnp.concatenate(
            [moved[0][:, :, TILE:], arrived[:, :, 3 * TILE : 4 * TILE]], axis=2
        )
        near_part = moved[1] + from_left + from_right
        projected = jnp.stack(
            [jnp.concatenate(proj_re, axis=1), jnp.concatenate(proj_im, axis=1)]
        ).astype(jnp.bfloat16)
        shard_piece = lax.all_gather(projected, "tile", axis=2, tiled=True)
        term_re, term_im = complex_dot(shard_piece[0], shard_piece[1], flipped[0], flipped[1], 1)
        summed_back = jnp.stack([term_re, term_im]).astype(jnp.bfloat16)
        far_re = []
        far_im = []
        for tile_here in range(tile_count):
            piece = summed_back[:, :, tile_here * RANK : (tile_here + 1) * RANK]
            part_re, part_im = complex_dot(
                piece[0], piece[1], source_basis[tile_here, 0], source_basis[tile_here, 1], 0
            )
            far_re.append(part_re)
            far_im.append(part_im)
        far_part = jnp.stack([jnp.concatenate(far_re, axis=1), jnp.concatenate(far_im, axis=1)])
        return field + near_part + far_part

    right_side = excitation.astype(jnp.float32)
    field = right_side
    for update in range(2):
        apply_field_bf = field.astype(jnp.bfloat16)
        padded = extended(apply_field_bf, (("tile", 2),), TILE)
        coeff_re = []
        coeff_im = []
        for apply_tile_here in range(tile_count):
            apply_own = apply_field_bf[:, :, apply_tile_here * TILE : (apply_tile_here + 1) * TILE]
            apply_part_re, apply_part_im = complex_dot(
                apply_own[0],
                apply_own[1],
                source_basis[apply_tile_here, 0],
                source_basis[apply_tile_here, 1],
                1,
            )
            coeff_re.append(apply_part_re)
            coeff_im.append(apply_part_im)
        coeff = jnp.stack(
            [jnp.concatenate(coeff_re, axis=1), jnp.concatenate(coeff_im, axis=1)]
        ).astype(jnp.bfloat16)
        fold_shard_piece = lax.all_gather(coeff, "tile", axis=2, tiled=True)
        fold_term_re, fold_term_im = complex_dot(
            fold_shard_piece[0], fold_shard_piece[1], masked[0], masked[1], 0
        )
        coupled = jnp.stack([fold_term_re, fold_term_im]).astype(jnp.bfloat16)
        out_re = []
        out_im = []
        for apply_tile_here in range(tile_count):
            total_re = jnp.zeros((src_rows, TILE), jnp.float32)
            total_im = jnp.zeros((src_rows, TILE), jnp.float32)
            for apply_offset in range(3):
                window = padded[
                    :,
                    :,
                    (apply_tile_here + apply_offset)
                    * TILE : (apply_tile_here + apply_offset + 1)
                    * TILE,
                ]
                apply_part_re, apply_part_im = complex_dot(
                    window[0],
                    window[1],
                    near_blocks[apply_tile_here, apply_offset, 0],
                    near_blocks[apply_tile_here, apply_offset, 1],
                    0,
                )
                total_re = total_re + apply_part_re
                total_im = total_im + apply_part_im
            apply_piece = coupled[:, :, apply_tile_here * RANK : (apply_tile_here + 1) * RANK]
            apply_part_re, apply_part_im = complex_dot(
                apply_piece[0],
                apply_piece[1],
                target_basis[apply_tile_here, 0],
                target_basis[apply_tile_here, 1],
                0,
            )
            out_re.append(total_re + apply_part_re)
            out_im.append(total_im + apply_part_im)
        added = jnp.stack([jnp.concatenate(out_re, axis=1), jnp.concatenate(out_im, axis=1)])
        field = field + DAMPING * (right_side - (field + added))
    field_bf = field.astype(jnp.bfloat16)
    focal_re, focal_im = complex_dot(field_bf[0], field_bf[1], focal_kernel[0], focal_kernel[1], 1)
    slots_here = focal_count // lax.axis_size("tile")
    first_slot = lax.axis_index("tile") * slots_here
    sources = src_rows * lax.axis_size("src")
    permute = (focal_owner[:, None] == jnp.arange(focal_count)[None, :]).astype(jnp.float32)
    summed_focal = lax.psum(jnp.stack([focal_re, focal_im]), "tile")
    intensity = lax.psum(
        jnp.sum(summed_focal[0] * summed_focal[0] + summed_focal[1] * summed_focal[1], axis=0),
        "src",
    )
    residual_part = jnp.tanh(intensity / (2.0 * sources)) - focal_target
    weights_re = (residual_part * summed_focal[0]).astype(jnp.bfloat16)
    weights_im = (-residual_part * summed_focal[1]).astype(jnp.bfloat16)
    residual_slots = jnp.dot(residual_part, permute, precision=lax.Precision.HIGHEST)
    residual_out = lax.dynamic_slice_in_dim(residual_slots, first_slot, slots_here)
    scale_factor = (tiles * TILE / focal_count) ** 0.5
    term_re, term_im = complex_dot(weights_re, weights_im, focal_kernel[0], focal_kernel[1], 0)
    source_term = jnp.stack([term_re, term_im]) * scale_factor
    adjoint = source_term + DAMPING * (source_term - apply_transpose(source_term))
    return (field, residual_out, adjoint)


def solution(mesh):
    return jax.shard_map(
        per_device,
        mesh=mesh,
        in_specs=(
            P(None, "src", "tile"),
            P("tile", None, None, None, None),
            P("tile", None, None, None),
            P("tile", None, None, None),
            P(None, None, "tile"),
            P(None, "tile"),
            P(None, "tile"),
            P(None, None, "tile"),
            P(),
            P(),
        ),
        out_specs=(P(None, "src", "tile"), P("tile"), P(None, "src", "tile")),
        check_vma=False,
    )
```

profile of v0, /device:TPU:6, one launch (start us, length us, event | category | flops | bytes accessed | tf_op | source)
XLA Modules:
  0.0 288.4 jit_solution(17563514672564382302)
XLA Ops:
  7.2 2.0 fusion.459
  9.1 0.5 collective-permute-start.1
  9.7 2.4 collective-permute-start
  12.1 0.7 iota_compare_fusion.2
  12.8 0.8 compare_and_fusion
  13.5 0.8 fusion.400
  14.7 0.9 broadcast_multiply_fusion
  15.8 0.9 reshape.84
  16.7 8.1 %all-to-all-start = ((bf16[8,2,2304]{2,1,0:T(2,128)(2,1)}), bf16[8,2,2304]{2,1,0:T(2,128)(2,1)S(1)}, u32[]{:S(2)}, u32[]{:S(2)}) async-start(bf16[8,2,2304]{2,1,0:T(2,128)(2,1)} %reshape.84), calls=%async_computation | async-start | bytes 147456 | tf_op jit(solution)/shard_map/all_to_all | solution.py:68
  24.8 1.2 fusion.274
  26.0 1.3 fusion.288
  27.3 1.1 fusion.272
  28.4 1.1 fusion.286
  29.4 1.1 fusion.41
  30.5 1.1 fusion.40
  31.6 1.1 fusion.43
  32.6 1.1 fusion.42
  33.7 30.7 %all_gather.9 = bf16[2,128,384]{1,2,0:T(8,128)(2,1)S(1)} all-gather(bf16[2,128,48]{1,2,0:T(8,128)(2,1)S(1)} %pad_maximum_fusion.6), channel_id=1, replica_groups=mesh['tile'=8,'src'=4] {'tile'}, dimensions={2}, use_global_device_ids=true | all-gather | bytes 221184 | tf_op jit(solution)/shard_map/all_gather | solution.py:146
  64.7 1.3 fusion.94
  66.1 1.3 fusion.112
  68.0 1.3 fusion.130
  69.3 1.3 fusion.148
  72.1 0.9 convolution_add_fusion.23
  73.3 1.0 convolution_add_fusion.16
  74.3 0.9 convolution_add_fusion.17
  75.2 0.9 convolution_subtract_fusion.23
  76.3 0.9 convolution_subtract_fusion.16
  77.3 0.9 convolution_subtract_fusion.17
  78.2 0.9 fusion.6
  79.2 0.9 fusion.3
  80.6 0.9 reshape.85
  81.5 1.2 copy.22
  82.7 1.8 fusion.85
  84.5 1.3 fusion.175
  85.8 1.5 fusion.20
  87.3 1.5 fusion.22
  88.9 1.3 fusion.77
  90.2 1.1 fusion.167
  91.4 1.1 fusion.23
  92.6 1.2 fusion.25
  95.3 30.6 %all_gather.10 = bf16[2,128,384]{1,2,0:T(8,128)(2,1)S(1)} all-gather(bf16[2,128,48]{1,2,0:T(8,128)(2,1)S(1)} %pad_maximum_fusion.7), channel_id=1, replica_groups=mesh['tile'=8,'src'=4] {'tile'}, dimensions={2}, use_global_device_ids=true | all-gather | bytes 221184 | tf_op jit(solution)/shard_map/all_gather | solution.py:146
  129.3 0.8 collective-permute-start.3
  131.0 2.3 collective-permute-start.2
  135.1 1.5 collective-permute-done.3
  136.9 2.6 collective-permute-done.2
  141.3 1.3 fusion.456
  143.5 0.6 pad_maximum_fusion.5
  144.4 70.5 %all-reduce.2.cloned.1.call-done = f32[2,128,64]{1,2,0:T(8,128)} async-done(((f32[2,128,64]{1,2,0:T(8,128)}), f32[2,128,64]{1,2,0:T(8,128)}) %all-reduce.2.cloned.1.call-update) | async-done | bytes 65552 | tf_op jit(solution)/shard_map/psum | solution.py:191
  214.9 0.9 add_reduce_fusion
  215.8 6.1 %psum.15 = f32[64]{0:T(128)S(1)} all-reduce(f32[64]{0:T(128)S(1)} %add_reduce_fusion), channel_id=1, replica_groups=mesh['tile'=8,'src'=4] {'src'}, use_global_device_ids=true, to_apply=%region_2.3 | all-reduce | flops 64 | bytes 512 | tf_op jit(solution)/shard_map/psum | solution.py:192
  221.9 1.2 fusion.253
  223.2 1.1 fusion.259
  224.3 1.1 fusion
  225.4 1.1 fusion.1
  226.6 1.3 fusion.106
  227.9 1.4 fusion.160
  229.3 1.3 fusion.116
  234.8 29.8 %all_gather.11 = bf16[2,128,384]{1,2,0:T(8,128)(2,1)S(1)} all-gather(bf16[2,128,48]{1,2,0:T(8,128)(2,1)S(1)} %pad_maximum_fusion.8), channel_id=1, replica_groups=mesh['tile'=8,'src'=4] {'tile'}, dimensions={2}, use_global_device_ids=true | all-gather | bytes 221184 | tf_op jit(solution)/shard_map/all_gather | solution.py:110
  269.8 1.6 collective-permute-start.5
  271.5 1.4 collective-permute-start.4
  274.3 0.6 dynamic_slice.3
  274.9 2.3 collective-permute-done.5
  277.2 2.7 collective-permute-done.4
  280.0 1.6 fusion.61
  (179 shorter events, 25.1 us)
Async XLA Ops:
  7.2 60.9 %copy-start.1 = (bf16[2,128,1024]{2,1,0:T(8,128)(2,1)S(1)}, bf16[2,128,1024]{2,1,0:T(8,128)(2,1)}, u32[]{:S(2)}) copy-start(bf16[2,128,1024]{2,1,0:T(8,128)(2,1)} %param.10) | copy-start | bytes 1572868
  7.2 60.4 %copy-start.2 = (bf16[2,2,24,512]{3,2,1,0:T(8,128)(2,1)S(1)}, bf16[2,2,24,512]{3,2,1,0:T(8,128)(2,1)}, u32[]{:S(2)}) copy-start(bf16[2,2,24,512]{3,2,1,0:T(8,128)(2,1)} %param.13) | copy-start | bytes 294916
  9.1 73.5 %collective-permute-start.1 = (bf16[2,128,512]{2,1,0:T(8,128)(2,1)}, bf16[2,128,512]{2,1,0:T(8,128)(2,1)}, u32[]{:S(2)}, u32[]{:S(2)}) collective-permute-start(bf16[2,128,512]{2,1,0:T(8,128)(2,1)} %get-tuple-element.12), channel_id=1, source_target_pairs={{4,0},{8,4},{12,8},{16,12},{20,16},{24,20},{28,24},{0,28},{5,1},{9... | collective-permute-start | bytes 786440 | tf_op jit(solution)/shard_map/ppermute | solution.py:21
  9.7 74.8 %collective-permute-start = (bf16[2,128,512]{2,1,0:T(8,128)(2,1)}, bf16[2,128,512]{2,1,0:T(8,128)(2,1)}, u32[]{:S(2)}, u32[]{:S(2)}) collective-permute-start(bf16[2,128,512]{2,1,0:T(8,128)(2,1)} %get-tuple-element.11), channel_id=1, source_target_pairs={{0,4},{4,8},{8,12},{12,16},{16,20},{20,24},{24,28},{28,0},{1,5},{5... | collective-permute-start | bytes 786440 | tf_op jit(solution)/shard_map/ppermute | solution.py:20
  16.7 63.9 %all-to-all-start = ((bf16[8,2,2304]{2,1,0:T(2,128)(2,1)}), bf16[8,2,2304]{2,1,0:T(2,128)(2,1)S(1)}, u32[]{:S(2)}, u32[]{:S(2)}) async-start(bf16[8,2,2304]{2,1,0:T(2,128)(2,1)} %reshape.84), calls=%async_computation | async-start | bytes 147456 | tf_op jit(solution)/shard_map/all_to_all | solution.py:68
  24.8 190.1 %all-reduce.2.cloned.1.call-start = ((), (), s32[]{:S(2)}) async-start(), calls=%async_computation.1 | async-start | bytes 131072 | tf_op jit(solution)/shard_map/psum | solution.py:191
  24.8 46.0 %copy-start = (bf16[2,3,2,512,512]{4,3,2,1,0:T(8,128)(2,1)S(1)}, bf16[2,3,2,512,512]{4,3,2,1,0:T(8,128)(2,1)}, u32[]{:S(2)}) copy-start(bf16[2,3,2,512,512]{4,3,2,1,0:T(8,128)(2,1)} %param.11) | copy-start | bytes 18874372
  76.1 14.1 %slice-start = ((s8[6291456]{0:T(1024)(128)(4,1)}), s8[2097152]{0:T(1024)(128)(4,1)S(1)}, s32[]{:S(2)}) async-start(s8[6291456]{0:T(1024)(128)(4,1)} %bitcast.613), calls=%async_computation.2 | async-start | bytes 4194304
  81.5 9.9 %copy-start.6 = (f32[128,512]{1,0:T(8,128)S(1)}, f32[128,512]{1,0:T(8,128)}, u32[]{:S(2)}) copy-start(f32[128,512]{1,0:T(8,128)} %convolution_subtract_fusion.23) | copy-start | bytes 786436
  81.5 9.9 %copy-start.7 = (f32[128,512]{1,0:T(8,128)S(1)}, f32[128,512]{1,0:T(8,128)}, u32[]{:S(2)}) copy-start(f32[128,512]{1,0:T(8,128)} %fusion.3) | copy-start | bytes 786436
  81.5 11.1 %copy-start.4 = (f32[128,512]{1,0:T(8,128)S(1)}, f32[128,512]{1,0:T(8,128)}, u32[]{:S(2)}) copy-start(f32[128,512]{1,0:T(8,128)} %convolution_subtract_fusion.16) | copy-start | bytes 786436
  81.5 11.1 %copy-start.5 = (f32[128,512]{1,0:T(8,128)S(1)}, f32[128,512]{1,0:T(8,128)}, u32[]{:S(2)}) copy-start(f32[128,512]{1,0:T(8,128)} %convolution_subtract_fusion.17) | copy-start | bytes 786436
  81.5 8.8 %slice-start.1 = ((s8[6291456]{0:T(1024)(128)(4,1)}), s8[4194304]{0:T(1024)(128)(4,1)S(1)}, s32[]{:S(2)}) async-start(s8[6291456]{0:T(1024)(128)(4,1)} %bitcast.613), calls=%async_computation.3 | async-start | bytes 8388608
  85.8 8.2 %copy-start.8 = (bf16[2,2,24,512]{3,2,1,0:T(8,128)(2,1)S(1)}, bf16[2,2,24,512]{3,2,1,0:T(8,128)(2,1)}, u32[]{:S(2)}) copy-start(bf16[2,2,24,512]{3,2,1,0:T(8,128)(2,1)} %param.12) | copy-start | bytes 294916
  129.3 7.3 %collective-permute-start.3 = (bf16[2,128,512]{2,1,0:T(8,128)(2,1)S(1)}, bf16[2,128,512]{2,1,0:T(8,128)(2,1)S(1)}, u32[]{:S(2)}, u32[]{:S(2)}) collective-permute-start(bf16[2,128,512]{2,1,0:T(8,128)(2,1)S(1)} %get-tuple-element.10), channel_id=1, source_target_pairs={{4,0},{8,4},{12,8},{16,12},{20,16},{24,20},{28,24},{0,28},{5,1},{9... | collective-permute-start | bytes 786440 | tf_op jit(solution)/shard_map/ppermute | solution.py:21
  131.0 8.4 %collective-permute-start.2 = (bf16[2,128,512]{2,1,0:T(8,128)(2,1)S(1)}, bf16[2,128,512]{2,1,0:T(8,128)(2,1)S(1)}, u32[]{:S(2)}, u32[]{:S(2)}) collective-permute-start(bf16[2,128,512]{2,1,0:T(8,128)(2,1)S(1)} %get-tuple-element.9), channel_id=1, source_target_pairs={{0,4},{4,8},{8,12},{12,16},{16,20},{20,24},{24,28},{28,0},{1,5},{5... | collective-permute-start | bytes 786440 | tf_op jit(solution)/shard_map/ppermute | solution.py:20
  140.2 2.4 copy-start.3
  140.5 81.4 %copy-start.10 = (f32[64]{0:T(128)S(1)}, f32[64]{0:T(128)}, u32[]{:S(2)}) copy-start(f32[64]{0:T(128)} %param.18) | copy-start | bytes 772
  141.3 89.4 %slice-start.2 = ((s8[6291456]{0:T(1024)(128)(4,1)}), s8[2097152]{0:T(1024)(128)(4,1)S(1)}, s32[]{:S(2)}) async-start(s8[6291456]{0:T(1024)(128)(4,1)} %bitcast.615), calls=%async_computation.4 | async-start | bytes 4194304
  221.9 8.7 %slice-start.3 = ((s8[6291456]{0:T(1024)(128)(4,1)}), s8[4194304]{0:T(1024)(128)(4,1)S(1)}, s32[]{:S(2)}) async-start(s8[6291456]{0:T(1024)(128)(4,1)} %bitcast.615), calls=%async_computation.5 | async-start | bytes 8388608
  227.9 37.1 %copy-start.9 = (bf16[2,2,24,512]{3,2,1,0:T(8,128)(2,1)S(1)}, bf16[2,2,24,512]{3,2,1,0:T(8,128)(2,1)}, u32[]{:S(2)}) copy-start(bf16[2,2,24,512]{3,2,1,0:T(8,128)(2,1)} %param.12) | copy-start | bytes 294916
  269.3 4.7 %copy-start.11 = (s32[64]{0:T(128)S(1)}, s32[64]{0:T(128)}, u32[]{:S(2)}) copy-start(s32[64]{0:T(128)} %param.19) | copy-start | bytes 772
  269.8 7.4 %collective-permute-start.5 = (bf16[2,128,512]{2,1,0:T(8,128)(2,1)S(1)}, bf16[2,128,512]{2,1,0:T(8,128)(2,1)S(1)}, u32[]{:S(2)}, u32[]{:S(2)}) collective-permute-start(bf16[2,128,512]{2,1,0:T(8,128)(2,1)S(1)} %fusion.67), channel_id=1, source_target_pairs={{4,0},{8,4},{12,8},{16,12},{20,16},{24,20},{28,24},{0,28},{5,1},{9... | collective-permute-start | bytes 786440 | tf_op jit(solution)/shard_map/ppermute | solution.py:21
  271.5 8.4 %collective-permute-start.4 = (bf16[2,128,512]{2,1,0:T(8,128)(2,1)S(1)}, bf16[2,128,512]{2,1,0:T(8,128)(2,1)S(1)}, u32[]{:S(2)}, u32[]{:S(2)}) collective-permute-start(bf16[2,128,512]{2,1,0:T(8,128)(2,1)S(1)} %fusion.69), channel_id=1, source_target_pairs={{0,4},{4,8},{8,12},{12,16},{16,20},{20,24},{24,28},{28,0},{1,5},{5... | collective-permute-start | bytes 786440 | tf_op jit(solution)/shard_map/ppermute | solution.py:20
Sparse Core Ops, SparseCore 0:
  144.3 70.5 all-reduce.1
where the time goes:
time: 294 us; the launch traced here: 288 us
  blocking collectives  97.2 us (33%)
  waiting for transfers between devices  79.6 us (27%)
  matrix products  64.2 us (22%)
  starting transfers between devices  17.1 us (6%)
  between operations  15.3 us (5%)
  other arithmetic  8.67 us (3%)
  local copies, waits for them, and re-layouts  6.31 us (2%)
    psum x1, waiting for transfers between devices, per_device(): summed_focal = lax.psum(jnp.stack([focal_re, focal_im]), 'tile')  70.5 us
    dot_general x140, matrix products, plain_dot(): lax.dot_general(left, right, (((1,), (contract,)), ((), ())), preferred_e...  64.1 us
    all_gather x2, blocking collectives, per_device(): fold_shard_piece = lax.all_gather(coeff, 'tile', axis=2, tiled=True)  61.3 us
    all_gather x1, blocking collectives, apply_transpose(): shard_piece = lax.all_gather(projected, 'tile', axis=2, tiled=True)  29.8 us
    all_to_all x1, starting transfers between devices, per_device(): lax.all_to_all(masked, 'tile', split_axis=1, concat_axis=2, tiled=True)  8.13 us
    ppermute x3, starting transfers between devices, extended(): before = lax.ppermute(last, axis, up)  6.11 us
    psum x1, blocking collectives, per_device(): lax.psum(jnp.sum(summed_focal[0] * summed_focal[0] + summed_focal[1] * su...  6.11 us
  transfers between devices with their start and end apart: 8, of which 5 were waited for; matrix products, arithmetic and copies ran while one was open for 13% of the time, Pallas kernels for 0%

commit v1 on v0

v1 whole, which is shorter than its diff:
```python
import functools

import jax
import jax.numpy as jnp
from jax import lax
from jax.experimental import pallas as pl
from jax.experimental.pallas import tpu as pltpu
from jax.sharding import PartitionSpec as P

DAMPING = 0.8
F32 = jnp.float32
BF16 = jnp.bfloat16


def nn(a, b):
    return lax.dot_general(a, b, (((1,), (0,)), ((), ())), preferred_element_type=F32)


def nt(a, b):
    return lax.dot_general(a, b, (((1,), (1,)), ((), ())), preferred_element_type=F32)


def tn(a, b):
    return lax.dot_general(a, b, (((0,), (0,)), ((), ())), preferred_element_type=F32)


def rows_join(p, q):
    h = p.shape[0] // 2
    return jnp.concatenate([p[:h] - q[h:], p[h:] + q[:h]], axis=0)


def lanes_join(p, q):
    h = p.shape[1] // 2
    return jnp.concatenate([p[:, :h] - q[:, h:], p[:, h:] + q[:, :h]], axis=1)


def lanes_turn(x):
    h = x.shape[1] // 2
    return jnp.concatenate([-x[:, h:], x[:, :h]], axis=1)


def stacked(x):
    return x.reshape(x.shape[0] * x.shape[1], x.shape[2])


def project(basis, field, tile):
    tc = basis.shape[0]
    parts = []
    for i in range(tc):
        v = field[:, i * tile : (i + 1) * tile]
        parts.append(lanes_join(nt(basis[i, 0], v), nt(basis[i, 1], v)))
    return jnp.concatenate(parts, axis=0)


def expand(coeff_t, basis, i):
    rank = basis.shape[2]
    c = coeff_t[i * rank : (i + 1) * rank]
    return tn(c.astype(BF16), basis[i, 0]) + tn(lanes_turn(c).astype(BF16), basis[i, 1])


def first_kernel(first_ref, e_ref, s_ref, t_ref, k_ref, c_ref, pr_ref, fl_ref, out_ref, m_ref):
    tiles, tc = pr_ref.shape
    rank, tile = s_ref.shape[2:]
    lanes = tc * rank
    n = out_ref.shape[0]
    width = out_ref.shape[2]
    rows = 2 * e_ref.shape[1]
    j = lax.broadcasted_iota(jnp.int32, (tiles, tc), 0)
    i = lax.broadcasted_iota(jnp.int32, (tiles, tc), 1) + first_ref[0, 0]
    distance = i - j
    distance = jnp.where(distance < 0, distance + tiles, distance)
    far = (fl_ref[...] == 1) & (distance != 0) & (distance != 1) & (distance != tiles - 1)
    limit = jnp.where(far, pr_ref[...], 0)
    lane = lax.broadcasted_iota(jnp.int32, (tiles, lanes), 1)
    level = lax.broadcasted_iota(jnp.int32, (rank, lanes), 1)
    wide = jnp.broadcast_to(limit[:, 0:1], (tiles, lanes))
    for a in range(1, tc):
        wide = jnp.where(lane >= a * rank, limit[:, a : a + 1], wide)
        level = jnp.where(level >= rank, level - rank, level)
    above = lax.broadcasted_iota(jnp.int32, (rank, lanes), 0)
    top = jnp.maximum(above, level)
    mask = jnp.concatenate(
        [jnp.where(top < wide[a : a + 1], 1.0, 0.0).astype(F32) for a in range(tiles)], axis=0
    )
    m_re = (c_ref[0].astype(F32) * mask).astype(BF16)
    m_im = (c_ref[1].astype(F32) * mask).astype(BF16)
    m_ref[0] = m_re
    m_ref[1] = m_im
    coeff = project(s_ref, stacked(e_ref[...]), tile).astype(BF16)
    proj = project(t_ref, stacked(k_ref[...]), tile)
    back = nn(m_re, proj.astype(BF16)) + nn(m_im, lanes_turn(proj).astype(BF16))
    for d in range(n):
        out_ref[d, :, 0:rows] = coeff
        out_ref[d, :, rows:width] = back[d * lanes : (d + 1) * lanes].astype(BF16)


def kernel_side(k_ref, nb_ref, loc_ref, gl_ref, gr_ref):
    tc, _, _, tile, _ = nb_ref.shape
    k = stacked(k_ref[...])

    def moved(i, o):
        own = k[:, i * tile : (i + 1) * tile]
        return rows_join(nt(own, nb_ref[i, o, 0]), nt(own, nb_ref[i, o, 1]))

    gl_ref[...] = moved(0, 0).astype(BF16)
    gr_ref[...] = moved(tc - 1, 2).astype(BF16)
    for m in range(tc):
        total = None
        for o in range(3):
            i = m + 1 - o
            if 0 <= i < tc:
                part = moved(i, o)
                total = part if total is None else total + part
        loc_ref[:, m * tile : (m + 1) * tile] = total


def near_inside(v_ref, nb_ref, loc_ref):
    tc, _, _, tile, _ = nb_ref.shape
    v = v_ref[...]
    for i in range(tc):
        p = q = None
        for o in range(3):
            j = i + o - 1
            if 0 <= j < tc:
                own = v[:, j * tile : (j + 1) * tile]
                pp, qq = nn(own, nb_ref[i, o, 0]), nn(own, nb_ref[i, o, 1])
                p, q = (pp, qq) if p is None else (p + pp, q + qq)
        loc_ref[:, i * tile : (i + 1) * tile] = rows_join(p, q)


def applied(i, near_ref, hl_ref, hr_ref, nb_ref, coupled, t_ref):
    tc, _, _, tile, _ = nb_ref.shape
    total = near_ref[:, i * tile : (i + 1) * tile] + expand(coupled, t_ref, i)
    if i == 0:
        total = total + rows_join(nn(hl_ref[...], nb_ref[0, 0, 0]), nn(hl_ref[...], nb_ref[0, 0, 1]))
    if i == tc - 1:
        total = total + rows_join(nn(hr_ref[...], nb_ref[i, 2, 0]), nn(hr_ref[...], nb_ref[i, 2, 1]))
    return total


def coupled_of(gathered, m_ref):
    turned = lanes_turn(gathered)
    coupled = tn(m_ref[0], gathered) + tn(m_ref[1], turned)
    return coupled.astype(BF16).astype(F32)


def middle_kernel(
    e_ref, near_ref, hl_ref, hr_ref, nb_ref, got_ref, m_ref, s_ref, t_ref, k_ref, loc_ref, gl_ref, gr_ref,
    base_ref, f1_ref, fl_ref, fr_ref, out_ref, r_ref,
):
    tc, _, _, tile, _ = nb_ref.shape
    n, lanes, _ = got_ref.shape
    rows, width = f1_ref.shape
    focal2 = gl_ref.shape[0]
    focal = focal2 // 2
    e = stacked(e_ref[...])
    coupled = coupled_of(got_ref[:, :, 0:rows].reshape(n * lanes, rows), m_ref)
    mixes = []
    for i in range(tc):
        cut = slice(i * tile, (i + 1) * tile)
        start = e[:, cut].astype(F32)
        field = start - DAMPING * applied(i, near_ref, hl_ref, hr_ref, nb_ref, coupled, t_ref)
        rounded = field.astype(BF16)
        f1_ref[:, cut] = rounded
        if i == 0:
            fl_ref[...] = rounded
        if i == tc - 1:
            fr_ref[...] = rounded
        mix = (1.0 - DAMPING) * field + DAMPING * start
        base_ref[:, cut] = mix
        mixes.append(mix.astype(BF16))
    f1 = f1_ref[...]
    back = jnp.sum(got_ref[:, :, rows:].astype(F32), axis=0).astype(BF16).astype(F32)
    k = stacked(k_ref[...])
    r_ref[0:focal2] = k
    for i in range(tc):
        cut = slice(i * tile, (i + 1) * tile)
        total = loc_ref[:, cut] + expand(back, s_ref, i)
        if i == 0:
            total = total + gr_ref[...].astype(F32)
        if i == tc - 1:
            total = total + gl_ref[...].astype(F32)
        r_ref[focal2:, cut] = (-DAMPING * total).astype(BF16)
    p = nt(k, jnp.concatenate(mixes, axis=1)) + nt(r_ref[focal2:], f1)
    half = rows // 2
    part = jnp.concatenate(
        [p[:focal, :half] - p[focal:, half:], p[:focal, half:] + p[focal:, :half]], axis=1
    ).astype(BF16)
    coeff = project(s_ref, f1, tile).astype(BF16)
    for d in range(n):
        out_ref[d, 0:focal] = part
        out_ref[d, focal:] = coeff


def sum_kernel(got_ref, foc_ref, int_ref):
    focal = foc_ref.shape[0]
    half = foc_ref.shape[1] // 2
    foc = jnp.sum(got_ref[:, 0:focal].astype(F32), axis=0)
    foc_ref[...] = foc
    power = foc[:, :half] * foc[:, :half] + foc[:, half:] * foc[:, half:]
    column = jnp.sum(power, axis=1, keepdims=True)
    int_ref[...] = jnp.sum(jnp.where(eye(focal), column, 0.0), axis=0, keepdims=True)


def eye(n):
    return lax.broadcasted_iota(jnp.int32, (n, n), 0) == lax.broadcasted_iota(jnp.int32, (n, n), 1)


def last_kernel(first_ref, foc_ref, int_ref, target_ref, owner_ref, r_ref, adj_ref, res_ref, *, sources, scale):
    focal = foc_ref.shape[0]
    half = foc_ref.shape[1] // 2
    row = jnp.tanh(int_ref[...] / (2.0 * sources)) - target_ref[...]
    diagonal = eye(focal)
    column = jnp.sum(jnp.where(diagonal, row, 0.0), axis=1, keepdims=True)
    owner = jnp.sum(jnp.where(diagonal, owner_ref[...], 0), axis=1, keepdims=True)
    slots = res_ref.shape[1]
    slot = lax.broadcasted_iota(jnp.int32, (focal, slots), 1) + first_ref[0, 1]
    res_ref[...] = jnp.sum(jnp.where(owner == slot, column, 0.0), axis=0, keepdims=True)
    re = column * foc_ref[:, :half]
    im = -column * foc_ref[:, half:]
    w = jnp.concatenate([re, im], axis=1).astype(BF16)
    turned = jnp.concatenate([-im, re], axis=1).astype(BF16)
    out = scale * tn(jnp.concatenate([w, turned, w, turned], axis=0), r_ref[...])
    adj_ref[0] = out[:half]
    adj_ref[1] = out[half:]


def field_kernel(base_ref, near_ref, hl_ref, hr_ref, nb_ref, got_ref, m_ref, t_ref, out_ref):
    tc, _, _, tile, _ = nb_ref.shape
    n, total, rows = got_ref.shape
    lanes = m_ref.shape[2]
    half = rows // 2
    coupled = coupled_of(got_ref[:, total - lanes :].reshape(n * lanes, rows), m_ref)
    for i in range(tc):
        cut = slice(i * tile, (i + 1) * tile)
        field = base_ref[:, cut] - DAMPING * applied(i, near_ref, hl_ref, hr_ref, nb_ref, coupled, t_ref)
        out_ref[0, :, cut] = field[:half]
        out_ref[1, :, cut] = field[half:]


VM = pl.BlockSpec(memory_space=pltpu.VMEM)
SM = pl.BlockSpec(memory_space=pltpu.SMEM)


def call(kernel, name, outs, *args, scalars=0):
    return pl.pallas_call(
        kernel,
        out_shape=[jax.ShapeDtypeStruct(s, d) for s, d in outs],
        in_specs=[SM] * scalars + [VM] * (len(args) - scalars),
        out_specs=[VM] * len(outs),
        name=name,
    )(*args)


def per_device(e, nb, sb, tb, coupling, pair_rank, far_link, fk, target, owner):
    tc, _, _, tile, _ = nb.shape
    rank = sb.shape[2]
    lanes = tc * rank
    rows = 2 * e.shape[1]
    width = e.shape[2]
    tiles = pair_rank.shape[0]
    focal = target.shape[0]
    n = lax.axis_size("tile")
    slots = focal // n
    sources = e.shape[1] * lax.axis_size("src")
    up = [(i, (i + 1) % n) for i in range(n)]
    down = [(j, i) for i, j in up]

    def exchange(to_left, to_right):
        return lax.ppermute(to_right, "tile", up), lax.ppermute(to_left, "tile", down)

    here = lax.axis_index("tile")
    first = jnp.stack([here * tc, here * slots]).astype(jnp.int32)[None]
    flat = stacked(e)
    hl, hr = exchange(flat[:, :tile], flat[:, width - tile :])
    send, masked = call(
        first_kernel, "first",
        [((n, lanes, rows + 2 * focal), BF16), ((2, tiles * rank, lanes), BF16)],
        first, e, sb, tb, fk, coupling, pair_rank, far_link, scalars=1,
    )
    got = lax.all_to_all(send, "tile", split_axis=0, concat_axis=0, tiled=True)
    loc, gl, gr = call(
        kernel_side, "kernel_side",
        [((2 * focal, width), F32), ((2 * focal, tile), BF16), ((2 * focal, tile), BF16)],
        fk, nb,
    )
    from_left, from_right = exchange(gl, gr)
    (near,) = call(near_inside, "near_inside", [((rows, width), F32)], flat, nb)
    base, f1, fl, fr, send1, r4 = call(
        middle_kernel, "middle",
        [
            ((rows, width), F32),
            ((rows, width), BF16),
            ((rows, tile), BF16),
            ((rows, tile), BF16),
            ((n, focal + lanes, rows), BF16),
            ((4 * focal, width), BF16),
        ],
        e, near, hl, hr, nb, got, masked, sb, tb, fk, loc, from_right, from_left,
    )
    got1 = lax.all_to_all(send1, "tile", split_axis=0, concat_axis=0, tiled=True)
    hl1, hr1 = exchange(fl, fr)
    (near1,) = call(near_inside, "near_inside_again", [((rows, width), F32)], f1, nb)
    foc, part = call(sum_kernel, "focal_sum", [((focal, rows), F32), ((1, focal), F32)], got1)
    intensity = lax.psum(part, "src")
    adjoint, residual = call(
        functools.partial(last_kernel, sources=sources, scale=(tiles * tile / focal) ** 0.5),
        "adjoint",
        [((2, rows // 2, width), F32), ((1, slots), F32)],
        first, foc, intensity, target[None], owner[None], r4, scalars=1,
    )
    (field,) = call(
        field_kernel, "field", [((2, rows // 2, width), F32)],
        base, near1, hl1, hr1, nb, got1, masked, tb,
    )
    return field, residual[0], adjoint


def solution(mesh):
    return jax.shard_map(
        per_device,
        mesh=mesh,
        in_specs=(
            P(None, "src", "tile"),
            P("tile", None, None, None, None),
            P("tile", None, None, None),
            P("tile", None, None, None),
            P(None, None, "tile"),
            P(None, "tile"),
            P(None, "tile"),
            P(None, None, "tile"),
            P(),
            P(),
        ),
        out_specs=(P(None, "src", "tile"), P("tile"), P(None, "src", "tile")),
        check_vma=False,
    )
```

time: 294 us -> 87 us (0.30); the launches traced: 288 us -> 86.4 us
  blocking collectives: 97.2 us -> 6.58 us
  matrix products: 64.2 us -> 0 us
  waiting for transfers between devices: 79.6 us -> 15.6 us
  Pallas kernels: 0 us -> 36.1 us
  between operations: 15.3 us -> 0.72 us
  other arithmetic: 8.67 us -> 0.61 us
    all_gather x3 -> x0, blocking collectives: 91.1 us -> none  [the longest x2 61.3 us: per_device(): fold_shard_piece = lax.all_gather(coeff, 'tile', axis=2, tiled=True)]
    psum x1 -> x0, waiting for transfers between devices: 70.5 us -> none  [per_device(): summed_focal = lax.psum(jnp.stack([focal_re, focal_im]), 'tile')]
    dot_general x141 -> x0, matrix products: 64.2 us -> none  [the longest x140 64.1 us: plain_dot(): lax.dot_general(left, right, (((1,), (contract,)), ((), ())), preferred_e...]
    pallas_call x0 -> x8, Pallas kernels: none -> 36.1 us  [call(): pl.pallas_call(kernel, out_shape=[jax.ShapeDtypeStruct(s, d) for s, d in...]
    all_to_all x1 -> x2, waiting for transfers between devices: 0.01 us -> 10.5 us  [the longest x1 10.5 us: per_device(): lax.all_to_all(send1, 'tile', split_axis=0, concat_axis=0, tiled=True)]
    unnamed x34 -> x19, local copies, waits for them, and re-layouts: 1.9 us -> 6.89 us
    ppermute x6, waiting for transfers between devices: 9.08 us -> 5.09 us  [the longest x3 5.08 us: exchange(): lax.ppermute(to_right, 'tile', up)]
    all_to_all x1 -> x2, starting transfers between devices: 8.13 us -> 10.9 us  [the longest x1 6.34 us: per_device(): got = lax.all_to_all(send, 'tile', split_axis=0, concat_axis=0, tiled=True)]
  transfers between devices with their start and end apart: 8 -> 8, of which waited for: 5 -> 2; matrix products, arithmetic and copies ran while one was open for 13% -> 1% of each run, Pallas kernels for 0% -> 24%
where the time goes in v1:
time: 87 us; the launch traced here: 86.4 us
  Pallas kernels  36.1 us (41%)
  starting transfers between devices  18.8 us (22%)
  waiting for transfers between devices  15.6 us (18%)
  local copies, waits for them, and re-layouts  7.95 us (9%)
  blocking collectives  6.58 us (8%)
    pallas_call x8, Pallas kernels, call(): pl.pallas_call(kernel, out_shape=[jax.ShapeDtypeStruct(s, d) for s, d in...  36.1 us
    all_to_all x1, waiting for transfers between devices, per_device(): lax.all_to_all(send1, 'tile', split_axis=0, concat_axis=0, tiled=True)  10.5 us
    unnamed x19, local copies, waits for them, and re-layouts  6.89 us
    psum x1, blocking collectives, per_device(): intensity = lax.psum(part, 'src')  6.58 us
    all_to_all x1, starting transfers between devices, per_device(): got = lax.all_to_all(send, 'tile', split_axis=0, concat_axis=0, tiled=True)  6.34 us
    ppermute x3, starting transfers between devices, exchange(): lax.ppermute(to_right, 'tile', up)  5.5 us
    ppermute x3, waiting for transfers between devices, exchange(): lax.ppermute(to_right, 'tile', up)  5.08 us
    all_to_all x1, starting transfers between devices, per_device(): lax.all_to_all(send1, 'tile', split_axis=0, concat_axis=0, tiled=True)  4.58 us
  transfers between devices with their start and end apart: 8, of which 2 were waited for; matrix products, arithmetic and copies ran while one was open for 1% of the time, Pallas kernels for 24%

profile of v1, /device:TPU:6, one launch (start us, length us, event | category | flops | bytes accessed | tf_op | source)
XLA Modules:
  0.0 86.4 jit_solution(18105550044275088919)
XLA Ops:
  0.6 1.4 %copy.14.pr_ref = s32[16,2]{1,0:T(8,128)} copy(s32[16,2]{0,1:T(2,128)} %param.15) | data formatting | bytes 256 | tf_op args[5]
  2.0 1.3 %copy.15.fl_ref = s32[16,2]{1,0:T(8,128)} copy(s32[16,2]{0,1:T(2,128)} %param.16) | data formatting | bytes 256 | tf_op args[6]
  3.3 1.7 %copy.13.c_ref = bf16[2,384,48]{2,1,0:T(8,128)(2,1)} copy(bf16[2,384,48]{1,2,0:T(8,128)(2,1)} %param.14) | data formatting | bytes 147456 | tf_op args[4]
  5.0 0.6 add_bitcast_fusion.first_ref
  5.6 2.9 %first.1 = (bf16[8,48,384]{2,1,0:T(8,128)(2,1)}, bf16[2,384,48]{2,1,0:T(8,128)(2,1)}) custom-call(s32[1,2]{1,0:T(1,128)} %add_bitcast_fusion.first_ref, bf16[2,128,1024]{2,1,0:T(8,128)(2,1)} %e_ref.3, bf16[2,2,24,512]{3,2,1,0:T(8,128)(2,1)} %s_ref.3, bf16[2,2,24,512]{3,2,1,0:T(8,128)(2,1)} %t_ref.5, bf16[2,64,1024]{2,1,0:T(8,128)(2,1)} %k_ref.5, ...), custom_call_target="tpu_custom_call" | custom-call | tf_op jit(solution)/shard_map/first/pallas_call | solution.py:246
  8.5 6.3 %all-to-all-start = ((bf16[8,48,384]{2,1,0:T(8,128)(2,1)}), bf16[8,48,384]{2,1,0:T(8,128)(2,1)S(1)}, u32[]{:S(2)}, u32[]{:S(2)}) async-start(bf16[8,48,384]{2,1,0:T(8,128)(2,1)} %get-tuple-element.18), calls=%async_computation | async-start | bytes 589824 | tf_op jit(solution)/shard_map/all_to_all | solution.py:281
  14.9 1.1 %fusion = (bf16[256,512]{1,0:T(8,128)(2,1)S(1)}, bf16[256,512]{1,0:T(8,128)(2,1)S(1)}) fusion(bf16[256,1024]{1,0:T(8,128)(2,1)} %bitcast.8), kind=kLoop, calls=%fused_computation.1 | loop fusion | bytes 1048576 | tf_op jit(solution)/shard_map/slice | solution.py:275
  15.9 0.1 collective-permute-start.1
  16.0 2.9 %collective-permute-start = (bf16[256,512]{1,0:T(8,128)(2,1)S(1)}, bf16[256,512]{1,0:T(8,128)(2,1)S(1)}, u32[]{:S(2)}, u32[]{:S(2)}) collective-permute-start(bf16[256,512]{1,0:T(8,128)(2,1)S(1)} %get-tuple-element.34), channel_id=1, source_target_pairs={{0,4},{4,8},{8,12},{12,16},{16,20},{20,24},{24,28},{28,0},{1,5},{5... | collective-permute-start | bytes 786440 | tf_op jit(solution)/shard_map/ppermute | solution.py:270
  18.9 5.8 %kernel_side.1 = (f32[128,1024]{1,0:T(8,128)}, bf16[128,512]{1,0:T(8,128)(2,1)}, bf16[128,512]{1,0:T(8,128)(2,1)}) custom-call(bf16[2,64,1024]{2,1,0:T(8,128)(2,1)} %k_ref.5, bf16[2,3,2,512,512]{4,3,2,1,0:T(8,128)(2,1)} %nb_ref.9), custom_call_target="tpu_custom_call" | custom-call | tf_op jit(solution)/shard_map/kernel_side/pallas_call | solution.py:246
  24.7 1.8 %collective-permute-start.2 = (bf16[128,512]{1,0:T(8,128)(2,1)}, bf16[128,512]{1,0:T(8,128)(2,1)S(1)}, u32[]{:S(2)}, u32[]{:S(2)}) collective-permute-start(bf16[128,512]{1,0:T(8,128)(2,1)} %get-tuple-element.21), channel_id=1, source_target_pairs={{4,0},{8,4},{12,8},{16,12},{20,16},{24,20},{28,24},{0,28},{5,1},{9... | collective-permute-start | bytes 393224 | tf_op jit(solution)/shard_map/ppermute | solution.py:270
  26.5 1.1 %collective-permute-start.3 = (bf16[128,512]{1,0:T(8,128)(2,1)}, bf16[128,512]{1,0:T(8,128)(2,1)S(1)}, u32[]{:S(2)}, u32[]{:S(2)}) collective-permute-start(bf16[128,512]{1,0:T(8,128)(2,1)} %get-tuple-element.22), channel_id=1, source_target_pairs={{0,4},{4,8},{8,12},{12,16},{16,20},{20,24},{24,28},{28,0},{1,5},{5... | collective-permute-start | bytes 393224 | tf_op jit(solution)/shard_map/ppermute | solution.py:270
  27.7 5.2 %near_inside.1.near_ref = f32[256,1024]{1,0:T(8,128)} custom-call(bf16[256,1024]{1,0:T(8,128)(2,1)} %bitcast.9, bf16[2,3,2,512,512]{4,3,2,1,0:T(8,128)(2,1)} %nb_ref.9), custom_call_target="tpu_custom_call" | custom-call | tf_op jit(solution)/shard_map/near_inside/pallas_call | solution.py:246
  32.8 0.0 collective-permute-done.2.gl_ref
  32.8 0.0 copy-start.6
  32.8 5.1 %collective-permute-done.3.gr_ref = bf16[128,512]{1,0:T(8,128)(2,1)S(1)} collective-permute-done((bf16[128,512]{1,0:T(8,128)(2,1)}, bf16[128,512]{1,0:T(8,128)(2,1)S(1)}, u32[]{:S(2)}, u32[]{:S(2)}) %collective-permute-start.3) | collective-permute-done | bytes 131104 | tf_op jit(solution)/shard_map/ppermute | solution.py:270
  37.9 0.0 copy-start.7
  37.9 0.0 collective-permute-done.1.hr_ref
  37.9 0.0 copy-start.2
  37.9 0.0 collective-permute-done.hl_ref
  37.9 0.0 copy-start.3
  38.0 0.0 all-to-all-done.got_ref
  38.0 0.0 copy-start.1
  38.0 0.0 copy-done.6
  38.0 0.6 copy-done.7
  38.6 0.1 copy-done.2
  38.7 0.1 copy-done.3
  38.8 0.1 copy-done.1
  38.9 6.8 %middle.1 = (f32[256,1024]{1,0:T(8,128)}, bf16[256,1024]{1,0:T(8,128)(2,1)}, bf16[256,512]{1,0:T(8,128)(2,1)}, bf16[256,512]{1,0:T(8,128)(2,1)}, bf16[8,112,256]...) custom-call(bf16[2,128,1024]{2,1,0:T(8,128)(2,1)} %e_ref.3, f32[256,1024]{1,0:T(8,128)} %near_inside.1.near_ref, ...), custom_call_target="tpu_custom_call" | custom-call | tf_op jit(solution)/shard_map/middle/pallas_call | solution.py:246
  45.7 4.6 %all-to-all-start.1 = ((bf16[8,112,256]{2,1,0:T(8,128)(2,1)}), bf16[8,112,256]{2,1,0:T(8,128)(2,1)S(1)}, u32[]{:S(2)}, u32[]{:S(2)}) async-start(bf16[8,112,256]{2,1,0:T(8,128)(2,1)} %get-tuple-element.27), calls=%async_computation.1 | async-start | bytes 917504 | tf_op jit(solution)/shard_map/all_to_all | solution.py:301
  50.3 1.5 %collective-permute-start.4 = (bf16[256,512]{1,0:T(8,128)(2,1)}, bf16[256,512]{1,0:T(8,128)(2,1)S(1)}, u32[]{:S(2)}, u32[]{:S(2)}) collective-permute-start(bf16[256,512]{1,0:T(8,128)(2,1)} %get-tuple-element.25), channel_id=1, source_target_pairs={{0,4},{4,8},{8,12},{12,16},{16,20},{20,24},{24,28},{28,0},{1,5},{5... | collective-permute-start | bytes 786440 | tf_op jit(solution)/shard_map/ppermute | solution.py:270
  51.8 0.6 collective-permute-start.5
  52.3 5.2 %near_inside_again.1.near_ref = f32[256,1024]{1,0:T(8,128)} custom-call(bf16[256,1024]{1,0:T(8,128)(2,1)} %get-tuple-element.24.v_ref, bf16[2,3,2,512,512]{4,3,2,1,0:T(8,128)(2,1)} %nb_ref.9), custom_call_target="tpu_custom_call" | custom-call | tf_op jit(solution)/shard_map/near_inside_again/pallas_call | solution.py:246
  57.5 10.5 %all-to-all-done.1.got_ref = bf16[8,112,256]{2,1,0:T(8,128)(2,1)S(1)} async-done(((bf16[8,112,256]{2,1,0:T(8,128)(2,1)}), bf16[8,112,256]{2,1,0:T(8,128)(2,1)S(1)}, u32[]{:S(2)}, u32[]{:S(2)}) %all-to-all-start.1) | async-done | bytes 458784 | tf_op jit(solution)/shard_map/all_to_all | solution.py:301
  68.0 0.0 copy-start
  68.0 0.8 copy-done
  68.8 1.7 %focal_sum.1 = (f32[64,256]{1,0:T(8,128)}, f32[1,64]{1,0:T(1,128)}) custom-call(bf16[8,112,256]{2,1,0:T(8,128)(2,1)} %copy-done), custom_call_target="tpu_custom_call" | custom-call | tf_op jit(solution)/shard_map/focal_sum/pallas_call | solution.py:246
  70.5 6.6 %psum.7.int_ref = f32[1,64]{1,0:T(1,128)} all-reduce(f32[1,64]{1,0:T(1,128)} %get-tuple-element.29), channel_id=1, replica_groups=mesh['tile'=8,'src'=4] {'src'}, use_global_device_ids=true, to_apply=%region_0.0 | all-reduce | flops 64 | bytes 512 | tf_op jit(solution)/shard_map/psum | solution.py:305
  77.1 2.5 %adjoint.1 = (f32[2,128,1024]{2,1,0:T(8,128)}, f32[1,8]{1,0:T(1,128)}) custom-call(s32[1,2]{1,0:T(1,128)} %add_bitcast_fusion.first_ref, f32[64,256]{1,0:T(8,128)} %get-tuple-element.28.foc_ref, f32[1,64]{1,0:T(1,128)} %psum.7.int_ref, f32[1,64]{1,0:T(1,128)} %bitcast.10, s32[1,64]{1,0:T(1,128)} %bitcast.11, bf16[256,1024]{1,0:T(8,128)(2,1)} %get-tuple-element.30.r_ref), custom_call_target="tpu_custom_call" | custom-call | tf_op jit(solution)/shard_map/adjoint/pallas_call | solution.py:246
  79.6 0.0 collective-permute-done.4.hl_ref
  79.6 0.0 copy-start.4
  79.6 0.0 collective-permute-done.5.hr_ref
  79.6 0.0 copy-start.5
  79.6 0.7 copy-done.4
  80.3 0.1 copy-done.5
  80.4 6.0 %field.1 = f32[2,128,1024]{2,1,0:T(8,128)} custom-call(f32[256,1024]{1,0:T(8,128)} %get-tuple-element.23.base_ref, f32[256,1024]{1,0:T(8,128)} %near_inside_again.1.near_ref, bf16[256,512]{1,0:T(8,128)(2,1)} %copy-done.4, bf16[256,512]{1,0:T(8,128)(2,1)} %copy-done.5, bf16[2,3,2,512,512]{4,3,2,1,0:T(8,128)(2,1)} %nb_ref.9, bf16[8,112,256]{2,1,0:T(8,128)(2,1)} %copy-done, ...), custom_call_target="tpu_custom_call" | custom-call | tf_op jit(solution)/shard_map/field/pallas_call | solution.py:246
Async XLA Ops:
  8.5 29.4 %all-to-all-start = ((bf16[8,48,384]{2,1,0:T(8,128)(2,1)}), bf16[8,48,384]{2,1,0:T(8,128)(2,1)S(1)}, u32[]{:S(2)}, u32[]{:S(2)}) async-start(bf16[8,48,384]{2,1,0:T(8,128)(2,1)} %get-tuple-element.18), calls=%async_computation | async-start | bytes 589824 | tf_op jit(solution)/shard_map/all_to_all | solution.py:281
  15.9 22.0 %collective-permute-start.1 = (bf16[256,512]{1,0:T(8,128)(2,1)S(1)}, bf16[256,512]{1,0:T(8,128)(2,1)S(1)}, u32[]{:S(2)}, u32[]{:S(2)}) collective-permute-start(bf16[256,512]{1,0:T(8,128)(2,1)S(1)} %get-tuple-element.33), channel_id=1, source_target_pairs={{4,0},{8,4},{12,8},{16,12},{20,16},{24,20},{28,24},{0,28},{5,1},{9... | collective-permute-start | bytes 786440 | tf_op jit(solution)/shard_map/ppermute | solution.py:270
  16.0 21.9 %collective-permute-start = (bf16[256,512]{1,0:T(8,128)(2,1)S(1)}, bf16[256,512]{1,0:T(8,128)(2,1)S(1)}, u32[]{:S(2)}, u32[]{:S(2)}) collective-permute-start(bf16[256,512]{1,0:T(8,128)(2,1)S(1)} %get-tuple-element.34), channel_id=1, source_target_pairs={{0,4},{4,8},{8,12},{12,16},{16,20},{20,24},{24,28},{28,0},{1,5},{5... | collective-permute-start | bytes 786440 | tf_op jit(solution)/shard_map/ppermute | solution.py:270
  24.7 8.1 %collective-permute-start.2 = (bf16[128,512]{1,0:T(8,128)(2,1)}, bf16[128,512]{1,0:T(8,128)(2,1)S(1)}, u32[]{:S(2)}, u32[]{:S(2)}) collective-permute-start(bf16[128,512]{1,0:T(8,128)(2,1)} %get-tuple-element.21), channel_id=1, source_target_pairs={{4,0},{8,4},{12,8},{16,12},{20,16},{24,20},{28,24},{0,28},{5,1},{9... | collective-permute-start | bytes 393224 | tf_op jit(solution)/shard_map/ppermute | solution.py:270
  26.5 11.4 %collective-permute-start.3 = (bf16[128,512]{1,0:T(8,128)(2,1)}, bf16[128,512]{1,0:T(8,128)(2,1)S(1)}, u32[]{:S(2)}, u32[]{:S(2)}) collective-permute-start(bf16[128,512]{1,0:T(8,128)(2,1)} %get-tuple-element.22), channel_id=1, source_target_pairs={{0,4},{4,8},{8,12},{12,16},{16,20},{20,24},{24,28},{28,0},{1,5},{5... | collective-permute-start | bytes 393224 | tf_op jit(solution)/shard_map/ppermute | solution.py:270
  32.8 5.1 %copy-start.6 = (bf16[128,512]{1,0:T(8,128)(2,1)}, bf16[128,512]{1,0:T(8,128)(2,1)S(1)}, u32[]{:S(2)}) copy-start(bf16[128,512]{1,0:T(8,128)(2,1)S(1)} %collective-permute-done.2.gl_ref) | copy-start | bytes 393220
  37.9 0.7 copy-start.7
  37.9 0.7 copy-start.2
  37.9 0.8 copy-start.3
  38.0 1.0 %copy-start.1 = (bf16[8,48,384]{2,1,0:T(8,128)(2,1)}, bf16[8,48,384]{2,1,0:T(8,128)(2,1)S(1)}, u32[]{:S(2)}) copy-start(bf16[8,48,384]{2,1,0:T(8,128)(2,1)S(1)} %all-to-all-done.got_ref) | copy-start | bytes 884740
  45.7 22.3 %all-to-all-start.1 = ((bf16[8,112,256]{2,1,0:T(8,128)(2,1)}), bf16[8,112,256]{2,1,0:T(8,128)(2,1)S(1)}, u32[]{:S(2)}, u32[]{:S(2)}) async-start(bf16[8,112,256]{2,1,0:T(8,128)(2,1)} %get-tuple-element.27), calls=%async_computation.1 | async-start | bytes 917504 | tf_op jit(solution)/shard_map/all_to_all | solution.py:301
  50.3 29.3 %collective-permute-start.4 = (bf16[256,512]{1,0:T(8,128)(2,1)}, bf16[256,512]{1,0:T(8,128)(2,1)S(1)}, u32[]{:S(2)}, u32[]{:S(2)}) collective-permute-start(bf16[256,512]{1,0:T(8,128)(2,1)} %get-tuple-element.25), channel_id=1, source_target_pairs={{0,4},{4,8},{8,12},{12,16},{16,20},{20,24},{24,28},{28,0},{1,5},{5... | collective-permute-start | bytes 786440 | tf_op jit(solution)/shard_map/ppermute | solution.py:270
  51.8 27.8 %collective-permute-start.5 = (bf16[256,512]{1,0:T(8,128)(2,1)}, bf16[256,512]{1,0:T(8,128)(2,1)S(1)}, u32[]{:S(2)}, u32[]{:S(2)}) collective-permute-start(bf16[256,512]{1,0:T(8,128)(2,1)} %get-tuple-element.26), channel_id=1, source_target_pairs={{4,0},{8,4},{12,8},{16,12},{20,16},{24,20},{28,24},{0,28},{5,1},{9... | collective-permute-start | bytes 786440 | tf_op jit(solution)/shard_map/ppermute | solution.py:270
  68.0 0.8 copy-start
  79.6 0.7 copy-start.4
  79.6 0.8 copy-start.5

commit v2 on v1

v2 whole, which is shorter than its diff:
```python
import functools
import math

import jax
import jax.numpy as jnp
from jax import lax
from jax.experimental import pallas as pl
from jax.experimental.pallas import tpu as pltpu
from jax.sharding import PartitionSpec as P


DAMPING = 0.8
F32 = jnp.float32
BF16 = jnp.bfloat16


def nn(a, b):
    return lax.dot_general(a, b, (((1,), (0,)), ((), ())), preferred_element_type=F32)


def nt(a, b):
    return lax.dot_general(a, b, (((1,), (1,)), ((), ())), preferred_element_type=F32)


def tn(a, b):
    return lax.dot_general(a, b, (((0,), (0,)), ((), ())), preferred_element_type=F32)


def rows_join(p, q):
    h = p.shape[0] // 2
    return jnp.concatenate([p[:h] - q[h:], p[h:] + q[:h]], axis=0)


def lanes_join(p, q):
    h = p.shape[1] // 2
    return jnp.concatenate([p[:, :h] - q[:, h:], p[:, h:] + q[:, :h]], axis=1)


def lanes_turn(x):
    h = x.shape[1] // 2
    return jnp.concatenate([-x[:, h:], x[:, :h]], axis=1)


def stacked(x):
    return x.reshape(x.shape[0] * x.shape[1], x.shape[2])


class Operand:
    def __init__(self, copy, ref):
        self.copy, self.ref = copy, ref

    def get(self):
        if self.copy is not None:
            self.copy.wait()
            self.copy = None
        return self.ref

    def __getitem__(self, index):
        return self.get()[index]


class Blocks:
    def __init__(self, operands):
        self.operands = operands

    def __getitem__(self, index):
        return self.operands[index[:2]][index[2:] + (slice(None),) * (3 - len(index[2:]))]


class Result:
    def __init__(self, ref, out=None, sems=None):
        self.ref, self.out, self.sems, self.copies = ref, out, sems, []

    def send(self, *index):
        if self.out is None:
            return
        view = (lambda r: r.at[index]) if index else (lambda r: r)
        copy = pltpu.make_async_copy(view(self.ref), view(self.out), self.sems.at[len(self.copies)])
        copy.start()
        self.copies.append(copy)


def project(basis, fields):
    parts = []
    for i, v in enumerate(fields):
        parts.append(lanes_join(nt(basis[i, 0], v), nt(basis[i, 1], v)))
    return jnp.concatenate(parts, axis=0)


def expand(coeff_t, basis, i):
    rank = basis.shape[2]
    c = coeff_t[i * rank : (i + 1) * rank]
    return tn(c.astype(BF16), basis[i, 0]) + tn(lanes_turn(c).astype(BF16), basis[i, 1])


def first_kernel(e_ref, k_ref, s_ref, t_ref, c_ref, pr_ref, fl_ref, nb_ref, out, kept, left, right):
    tc, tiles = pr_ref.ref.shape
    rank, tile = s_ref.ref.shape[2:]
    lanes = tc * rank
    n = out.ref.shape[0]
    width = out.ref.shape[2]
    rows = 2 * e_ref.ref.shape[1]
    columns = tiles * rank
    source = lax.broadcasted_iota(jnp.int32, (tiles, columns), 1) - rank * lax.broadcasted_iota(
        jnp.int32, (tiles, columns), 0
    )
    spread = jnp.where((source >= 0) & (source < rank), 1.0, 0.0).astype(F32)
    lane = lax.broadcasted_iota(jnp.int32, (rank, columns), 1).astype(F32)
    level = lane - rank * jnp.floor((lane + 0.5) / rank)
    top = jnp.maximum(level, lax.broadcasted_iota(jnp.int32, (rank, columns), 0).astype(F32))
    j = lax.broadcasted_iota(jnp.int32, (tc, tiles), 1)
    i = lax.broadcasted_iota(jnp.int32, (tc, tiles), 0) + lax.axis_index("tile") * tc
    distance = i - j
    distance = jnp.where(distance < 0, distance + tiles, distance)
    far = (fl_ref[...] == 1) & (distance != 0) & (distance != 1) & (distance != tiles - 1)
    limit = jnp.where(far, pr_ref[...], 0).astype(F32)
    wide = nn(limit, spread)
    mask = jnp.concatenate([jnp.where(top < wide[a : a + 1], 1.0, 0.0) for a in range(tc)], axis=0)
    m_re = (c_ref[0].astype(F32) * mask).astype(BF16)
    m_im = (c_ref[1].astype(F32) * mask).astype(BF16)
    kept.ref[0] = m_re
    kept.ref[1] = m_im
    kept.send()
    e = stacked(e_ref[...])
    coeff = project(s_ref.get(), [e[:, i * tile : (i + 1) * tile] for i in range(tc)]).astype(BF16)
    k = stacked(k_ref[...])
    proj = project(t_ref.get(), [k[:, i * tile : (i + 1) * tile] for i in range(tc)])
    back = tn(m_re, proj.astype(BF16)) + tn(m_im, lanes_turn(proj).astype(BF16))
    for d in range(n):
        out.ref[d, :, 0:rows] = coeff
        out.ref[d, :, rows:width] = back[d * lanes : (d + 1) * lanes].astype(BF16)
    out.send()
    left.ref[...] = moved(k, nb_ref, tile, 0, 0).astype(BF16)
    left.send()
    right.ref[...] = moved(k, nb_ref, tile, tc - 1, 2).astype(BF16)
    right.send()


def moved(k, nb_ref, tile, i, o):
    own = k[:, i * tile : (i + 1) * tile]
    return rows_join(nt(own, nb_ref[i, o, 0]), nt(own, nb_ref[i, o, 1]))


def near_of(fields, nb_ref, i, offsets):
    p = q = None
    for o in offsets:
        pp, qq = nn(fields[i + o - 1], nb_ref[i, o, 0]), nn(fields[i + o - 1], nb_ref[i, o, 1])
        p, q = (pp, qq) if p is None else (p + pp, q + qq)
    return rows_join(p, q)


def inside_kernel(v_ref, k_ref, nb_ref, near, loc, *, tile, tc):
    v, k = v_ref[...], stacked(k_ref[...])
    fields = {i: v[:, i * tile : (i + 1) * tile] for i in range(tc)}
    for m in range(tc):
        cut = slice(m * tile, (m + 1) * tile)
        near.ref[:, cut] = near_of(fields, nb_ref, m, [o for o in range(3) if m + o - 1 in fields])
        total = None
        for o in range(3):
            i = m + 1 - o
            if 0 <= i < tc:
                part = moved(k, nb_ref, tile, i, o)
                total = part if total is None else total + part
        loc.ref[:, cut] = total


def second_near_kernel(*refs, tile, tc):
    fields = {i: refs[i][...] for i in range(tc)}
    hl_ref, hr_ref, nb_ref, base_ref, out = refs[tc:]
    fields[-1], fields[tc] = hl_ref[...], hr_ref[...]
    for i in range(tc):
        cut = slice(i * tile, (i + 1) * tile)
        out.ref[:, cut] = base_ref[:, cut] - DAMPING * near_of(fields, nb_ref, i, range(3))


def coupled_of(gathered, m_ref):
    turned = lanes_turn(gathered)
    coupled = nn(m_ref[0], gathered) + nn(m_ref[1], turned)
    return coupled.astype(BF16).astype(F32)


def update_kernel(got_ref, m_ref, near_ref, hl_ref, hr_ref, t_ref, e_ref, nb_ref, base, *tiles_out, tile, tc):
    n, lanes, _ = got_ref.ref.shape
    rows = base.ref.shape[0]
    coupled = coupled_of(got_ref[:, :, 0:rows].reshape(n * lanes, rows), m_ref)
    edges = {-1: hl_ref[...], tc: hr_ref[...]}
    for i in range(tc):
        cut = slice(i * tile, (i + 1) * tile)
        total = near_ref[:, cut] + expand(coupled, t_ref.get(), i)
        for o in range(3):
            if i + o - 1 in edges:
                total = total + near_of(edges, nb_ref, i, [o])
        start = stacked(e_ref[:, :, cut]).astype(F32)
        field = start - DAMPING * total
        tiles_out[i].ref[...] = field.astype(BF16)
        base.ref[:, cut] = (1.0 - DAMPING) * field + DAMPING * start
        base.send(slice(None), cut)


def focal_kernel(*refs, tile, tc):
    got_ref, loc_ref, gl_ref, gr_ref = refs[:4]
    fields = [ref[...] for ref in refs[4 : 4 + tc]]
    s_ref, k_ref, e_ref, out, side = refs[4 + tc :]
    n, _, rows = out.ref.shape
    focal = gl_ref.ref.shape[0] // 2
    back = jnp.sum(got_ref[:, :, rows:].astype(F32), axis=0).astype(BF16).astype(F32)
    k = stacked(k_ref[...])
    p = None
    for i in range(tc):
        cut = slice(i * tile, (i + 1) * tile)
        total = loc_ref[:, cut] + expand(back, s_ref.get(), i)
        if i == 0:
            total = total + gl_ref[...].astype(F32)
        if i == tc - 1:
            total = total + gr_ref[...].astype(F32)
        own = (-DAMPING * total).astype(BF16)
        side.ref[:, cut] = own
        start = stacked(e_ref[:, :, cut]).astype(F32)
        mix = ((1.0 - DAMPING) * fields[i].astype(F32) + DAMPING * start).astype(BF16)
        term = nt(k[:, cut], mix) + nt(own, fields[i])
        p = term if p is None else p + term
    half = rows // 2
    part = jnp.concatenate(
        [p[:focal, :half] - p[focal:, half:], p[:focal, half:] + p[focal:, :half]], axis=1
    ).astype(BF16)
    coeff = project(s_ref.get(), fields).astype(BF16)
    for d in range(n):
        out.ref[d, :focal] = part
        out.ref[d, focal:] = coeff


def eye(n):
    return lax.broadcasted_iota(jnp.int32, (n, n), 0) == lax.broadcasted_iota(jnp.int32, (n, n), 1)


def sum_kernel(got_ref, foc, power):
    focal = foc.ref.shape[0]
    half = foc.ref.shape[1] // 2
    total = jnp.sum(got_ref[:, 0:focal].astype(F32), axis=0)
    foc.ref[...] = total
    squares = total[:, :half] * total[:, :half] + total[:, half:] * total[:, half:]
    column = jnp.sum(squares, axis=1, keepdims=True)
    power.ref[...] = jnp.sum(jnp.where(eye(focal), column, 0.0), axis=0, keepdims=True)
    power.send()
    foc.send()


def last_kernel(a_ref, b_ref, c_ref, d_ref, foc_ref, side_ref, target_ref, owner_ref, k_ref, adj, res, *, sources, scale):
    focal = foc_ref.ref.shape[0]
    half = foc_ref.ref.shape[1] // 2
    intensity = (a_ref[...] + b_ref[...]) + (c_ref[...] + d_ref[...])
    row = jnp.tanh(intensity / (2.0 * sources)) - target_ref[...]
    diagonal = eye(focal)
    column = jnp.sum(jnp.where(diagonal, row, 0.0), axis=1, keepdims=True)
    owner = jnp.sum(jnp.where(diagonal, owner_ref[...], 0), axis=1, keepdims=True)
    slots = res.ref.shape[1]
    slot = lax.broadcasted_iota(jnp.int32, (focal, slots), 1) + lax.axis_index("tile") * slots
    res.ref[...] = jnp.sum(jnp.where(owner == slot, column, 0.0), axis=0, keepdims=True)
    res.send()
    re = column * foc_ref[:, :half]
    im = -column * foc_ref[:, half:]
    w = jnp.concatenate([re, im], axis=1).astype(BF16)
    turned = jnp.concatenate([-im, re], axis=1).astype(BF16)
    both = jnp.concatenate([w, turned], axis=0)
    k = stacked(k_ref[...])
    width = k.shape[1]
    tile = width // 2
    for at in range(0, width, tile):
        cut = slice(at, at + tile)
        out = scale * (tn(both, k[:, cut]) + tn(both, side_ref[:, cut]))
        adj.ref[0, :, cut] = out[:half]
        adj.ref[1, :, cut] = out[half:]
        adj.send(slice(None), slice(None), cut)


def field_kernel(got_ref, m_ref, near_ref, t_ref, out, *, tile, tc):
    n, _, rows = got_ref.ref.shape
    lanes = m_ref.ref.shape[1]
    half = rows // 2
    coupled = coupled_of(got_ref[:, -lanes:].reshape(n * lanes, rows), m_ref)
    for i in range(tc):
        cut = slice(i * tile, (i + 1) * tile)
        field = near_ref[:, cut] - DAMPING * expand(coupled, t_ref.get(), i)
        out.ref[0, :, cut] = field[:half]
        out.ref[1, :, cut] = field[half:]
        out.send(slice(None), slice(None), cut)


def edges_kernel(v_ref, left_ref, right_ref, sems):
    width, tile = v_ref.shape[1], left_ref.shape[1]
    copies = [
        pltpu.make_async_copy(v_ref.at[:, 0:tile], left_ref, sems.at[0]),
        pltpu.make_async_copy(v_ref.at[:, width - tile : width], right_ref, sems.at[1]),
    ]
    for copy in copies:
        copy.start()
    for copy in copies:
        copy.wait()


VM = pl.BlockSpec(memory_space=pltpu.VMEM)
FAR = pl.BlockSpec(memory_space=pltpu.HBM)


def in_hbm(x):
    return pltpu.with_memory_space_constraint(x, pltpu.HBM)


def padded(one):
    return math.prod(one.shape[:-1]) * -(-one.shape[-1] // 128) * 128 * jnp.dtype(one.dtype).itemsize


def call(kernel, outs, near, far=(), blocks=(), far_outs=()):
    far = [in_hbm(arg) for arg in far]
    held = [len(blocks) if arg.ndim == 5 and blocks else 0 for arg in far]
    scratch = [
        pltpu.VMEM((count,) + arg.shape[2:] if count else arg.shape, arg.dtype) for arg, count in zip(far, held)
    ]
    scratch += [pltpu.VMEM(*outs[o]) for o in far_outs]
    taken = sum(padded(one) for one in scratch) + 3 * sum(padded(jax.ShapeDtypeStruct(s, d)) for s, d in outs)
    taken += 2 * sum(padded(one) for one in near)
    scratch += [pltpu.SemaphoreType.DMA((sum(count or 1 for count in held) + 1,))]
    scratch += [pltpu.SemaphoreType.DMA((len(far_outs) + 1, 8))]

    def run(*refs):
        refs = list(refs)
        close = [Operand(None, refs.pop(0)) for _ in near]
        sources = [refs.pop(0) for _ in far]
        sinks = [refs.pop(0) for _ in outs]
        places = [refs.pop(0) for _ in far]
        stages = {o: refs.pop(0) for o in far_outs}
        ins, ends = refs
        operands, at = [], 0
        for source, place, count in zip(sources, places, held):
            if count:
                parts = {}
                for spot, block in enumerate(blocks):
                    copy = pltpu.make_async_copy(source.at[block], place.at[spot], ins.at[at])
                    copy.start()
                    at += 1
                    parts[block] = Operand(copy, place.at[spot])
                operands.append(Blocks(parts))
            else:
                copy = pltpu.make_async_copy(source, place, ins.at[at])
                copy.start()
                at += 1
                operands.append(Operand(copy, place))
        results = []
        for o, sink in enumerate(sinks):
            results.append(Result(stages[o], sink, ends.at[far_outs.index(o)]) if o in stages else Result(sink))
        kernel(*close, *operands, *results)
        for operand in operands:
            for one in operand.operands.values() if isinstance(operand, Blocks) else [operand]:
                one.get()
        for result in results:
            for copy in result.copies:
                copy.wait()

    return pl.pallas_call(
        run,
        out_shape=[jax.ShapeDtypeStruct(s, d) for s, d in outs],
        in_specs=[VM] * len(near) + [FAR] * len(far),
        out_specs=[FAR if o in far_outs else VM for o in range(len(outs))],
        scratch_shapes=scratch,
        compiler_params=pltpu.CompilerParams(vmem_limit_bytes=min(taken + (12 << 20), 60 * 1024 * 1024)),
    )(*near, *far)


def per_device(e, nb, sb, tb, coupling, pair_rank, far_link, fk, target, owner):
    tc, _, _, tile, _ = nb.shape
    rank = sb.shape[2]
    lanes = tc * rank
    half = e.shape[1]
    rows = 2 * half
    width = e.shape[2]
    tiles = pair_rank.shape[0]
    focal = target.shape[0]
    n = lax.axis_size("tile")
    groups = lax.axis_size("src")
    slots = focal // n
    edges = [(0, 0), (tc - 1, 2)]
    inside = [(i, o) for i in range(tc) for o in range(3) if (i, o) not in edges]
    sizes = dict(tile=tile, tc=tc)
    up = [(i, (i + 1) % n) for i in range(n)]
    down = [(j, i) for i, j in up]

    def exchange(to_left, to_right):
        return lax.ppermute(to_right, "tile", up), lax.ppermute(to_left, "tile", down)

    flat = stacked(e)
    every = [(i, o) for i in range(tc) for o in range(3)]
    el, er = pl.pallas_call(
        edges_kernel,
        out_shape=[jax.ShapeDtypeStruct((rows, tile), BF16)] * 2,
        in_specs=[FAR],
        out_specs=[VM, VM],
        scratch_shapes=[pltpu.SemaphoreType.DMA((2,))],
        compiler_params=pltpu.CompilerParams(vmem_limit_bytes=8 << 20),
        name="ends",
    )(in_hbm(flat))
    hl, hr = exchange(el, er)
    send, masked, gl, gr = call(
        first_kernel,
        [
            ((n, lanes, rows + 2 * focal), BF16),
            ((2, lanes, tiles * rank), BF16),
            ((2 * focal, tile), BF16),
            ((2 * focal, tile), BF16),
        ],
        [], [e, fk, sb, tb, jnp.swapaxes(coupling, 1, 2), pair_rank.T, far_link.T, nb], blocks=edges,
    )
    got = lax.all_to_all(send, "tile", split_axis=0, concat_axis=0, tiled=True)
    from_left, from_right = exchange(gl, gr)
    near, loc = call(
        functools.partial(inside_kernel, **sizes),
        [((rows, width), F32), ((2 * focal, width), F32)],
        [], [flat, fk, nb], blocks=inside,
    )
    base, *f1 = call(
        functools.partial(update_kernel, **sizes),
        [((rows, width), F32)] + [((rows, tile), BF16)] * tc,
        [got, masked, near, hl, hr], [tb, e, nb], blocks=edges, far_outs=(0,),
    )
    hl1, hr1 = exchange(f1[0], f1[-1])
    send1, side = call(
        functools.partial(focal_kernel, **sizes),
        [((n, focal + lanes, rows), BF16), ((2 * focal, width), BF16)],
        [got, loc, from_left, from_right, *f1], [sb, fk, e],
    )
    got1 = lax.all_to_all(send1, "tile", split_axis=0, concat_axis=0, tiled=True)
    (near1,) = call(
        functools.partial(second_near_kernel, **sizes), [((rows, width), F32)],
        [*f1, hl1, hr1], [nb, base], blocks=every,
    )
    foc, part = call(sum_kernel, [((focal, rows), F32), ((1, focal), F32)], [got1])
    parts = [part] + [lax.ppermute(part, "src", [(i, i ^ k) for i in range(groups)]) for k in (1, 2, 3)]
    adjoint, residual = call(
        functools.partial(last_kernel, sources=half * groups, scale=(tiles * tile / focal) ** 0.5),
        [((2, half, width), F32), ((1, slots), F32)],
        [*parts, foc, side], [target[None], owner[None], fk], far_outs=(0, 1),
    )
    (field,) = call(
        functools.partial(field_kernel, **sizes), [((2, half, width), F32)],
        [got1, masked, near1], [tb], far_outs=(0,),
    )
    return field, residual[0], adjoint


def solution(mesh):
    return jax.shard_map(
        per_device,
        mesh=mesh,
        in_specs=(
            P(None, "src", "tile"),
            P("tile", None, None, None, None),
            P("tile", None, None, None),
            P("tile", None, None, None),
            P(None, None, "tile"),
            P(None, "tile"),
            P(None, "tile"),
            P(None, None, "tile"),
            P(),
            P(),
        ),
        out_specs=(P(None, "src", "tile"), P("tile"), P(None, "src", "tile")),
        check_vma=False,
    )
```

time: 87 us -> 73.7 us (0.85)
  Pallas kernels: 36.1 us -> 27.1 us
  local copies, waits for them, and re-layouts: 7.95 us -> 0.01 us
  waiting for transfers between devices: 15.6 us -> 23.3 us
  blocking collectives: 6.58 us -> 0 us
  starting transfers between devices: 18.8 us -> 21.8 us
    pallas_call x8 -> x9, Pallas kernels: 36.1 us -> 27.1 us  [the longest x8 26.1 us: call(): pl.pallas_call(run, out_shape=[jax.ShapeDtypeStruct(s, d) for s, d in out...]
    unnamed x19 -> x2, local copies, waits for them, and re-layouts: 6.89 us -> 0.01 us
    psum x1 -> x0, blocking collectives: 6.58 us -> none  [per_device(): intensity = lax.psum(part, 'src')]
    all_to_all x1, waiting for transfers between devices: 10.5 us -> 14.4 us  [per_device(): lax.all_to_all(send1, 'tile', split_axis=0, concat_axis=0, tiled=True)]
    ppermute x3, waiting for transfers between devices: 5.08 us -> 8.89 us  [exchange(): lax.ppermute(to_right, 'tile', up)]
    ppermute x0 -> x3, starting transfers between devices: none -> 1.92 us  [per_device(): lax.ppermute(part, 'src', [(i, i ^ k) for i in range(groups)])]
    ppermute x3, starting transfers between devices: 2.42 us -> 0.99 us  [exchange(): lax.ppermute(to_left, 'tile', down)]
    ppermute x3, starting transfers between devices: 5.5 us -> 6.78 us  [exchange(): lax.ppermute(to_right, 'tile', up)]
  transfers between devices with their start and end apart: 8 -> 11, of which waited for: 2 -> 2; matrix products, arithmetic and copies ran while one was open for 1% -> 0% of each run, Pallas kernels for 24% -> 24%
where the time goes in v2:
time: 73.7 us; the launch traced here: 72.9 us
  Pallas kernels  27.1 us (37%)
  waiting for transfers between devices  23.3 us (32%)
  starting transfers between devices  21.8 us (30%)
  between operations  0.77 us (1%)
    pallas_call x8, Pallas kernels, call(): pl.pallas_call(run, out_shape=[jax.ShapeDtypeStruct(s, d) for s, d in out...  26.1 us
    all_to_all x1, waiting for transfers between devices, per_device(): lax.all_to_all(send1, 'tile', split_axis=0, concat_axis=0, tiled=True)  14.4 us
    ppermute x3, waiting for transfers between devices, exchange(): lax.ppermute(to_right, 'tile', up)  8.89 us
    ppermute x3, starting transfers between devices, exchange(): lax.ppermute(to_right, 'tile', up)  6.78 us
    all_to_all x1, starting transfers between devices, per_device(): got = lax.all_to_all(send, 'tile', split_axis=0, concat_axis=0, tiled=True)  6.35 us
    all_to_all x1, starting transfers between devices, per_device(): lax.all_to_all(send1, 'tile', split_axis=0, concat_axis=0, tiled=True)  5.73 us
    ppermute x3, starting transfers between devices, per_device(): lax.ppermute(part, 'src', [(i, i ^ k) for i in range(groups)])  1.92 us
  transfers between devices with their start and end apart: 11, of which 2 were waited for; matrix products, arithmetic and copies ran while one was open for 0% of the time, Pallas kernels for 24%

profile of v2, /device:TPU:6, one launch (start us, length us, event | category | flops | bytes accessed | tf_op | source)
XLA Modules:
  0.0 72.9 jit_solution(8263436547812494114)
XLA Ops:
  0.6 3.6 %shard_map.121 = (bf16[8,48,384]{2,1,0:T(8,128)(2,1)}, bf16[2,48,384]{2,1,0:T(8,128)(2,1)S(1)}, bf16[128,512]{1,0:T(8,128)(2,1)S(1)}, bf16[128,512]{1,0:T(8,128)(2,1)S(1)}) custom-call(bf16[2,128,1024]{2,1,0:T(8,128)(2,1)} %refs_8_.2, bf16[2,64,1024]{2,1,0:T(8,128)(2,1)} %refs_8_.3, bf16[2,2,24,512]{3,2,1,0:T(8,128)(2,1)} %refs_6_.3, ...), custom_call_target="tpu_custom_call" | custom-call | tf_op jit(solution)/shard_map/pallas_call | solution.py:359
  4.3 6.4 %all-to-all-start = ((bf16[8,48,384]{2,1,0:T(8,128)(2,1)}), bf16[8,48,384]{2,1,0:T(8,128)(2,1)S(1)}, u32[]{:S(2)}, u32[]{:S(2)}) async-start(bf16[8,48,384]{2,1,0:T(8,128)(2,1)} %get-tuple-element.20), calls=%async_computation | async-start | bytes 589824 | tf_op jit(solution)/shard_map/all_to_all | solution.py:412
  10.6 1.0 %ends.1 = (bf16[256,512]{1,0:T(8,128)(2,1)S(1)}, bf16[256,512]{1,0:T(8,128)(2,1)S(1)}) custom-call(bf16[256,1024]{1,0:T(8,128)(2,1)} %bitcast.7), custom_call_target="tpu_custom_call" | custom-call | tf_op jit(solution)/shard_map/ends/pallas_call | solution.py:392
  11.7 1.5 %collective-permute-start.2 = (bf16[256,512]{1,0:T(8,128)(2,1)S(1)}, bf16[256,512]{1,0:T(8,128)(2,1)S(1)}, u32[]{:S(2)}, u32[]{:S(2)}) collective-permute-start(bf16[256,512]{1,0:T(8,128)(2,1)S(1)} %get-tuple-element.26), channel_id=1, source_target_pairs={{0,4},{4,8},{8,12},{12,16},{16,20},{20,24},{24,28},{28,0},{1,5},{5... | collective-permute-start | bytes 786440 | tf_op jit(solution)/shard_map/ppermute | solution.py:388
  13.2 0.6 collective-permute-start.3
  13.7 2.4 %collective-permute-start = (bf16[128,512]{1,0:T(8,128)(2,1)S(1)}, bf16[128,512]{1,0:T(8,128)(2,1)S(1)}, u32[]{:S(2)}, u32[]{:S(2)}) collective-permute-start(bf16[128,512]{1,0:T(8,128)(2,1)S(1)} %get-tuple-element.22), channel_id=1, source_target_pairs={{0,4},{4,8},{8,12},{12,16},{16,20},{20,24},{24,28},{28,0},{1,5},{5... | collective-permute-start | bytes 393224 | tf_op jit(solution)/shard_map/ppermute | solution.py:388
  16.1 0.4 collective-permute-start.1
  16.5 4.7 %shard_map.122 = (f32[256,1024]{1,0:T(8,128)S(1)}, f32[128,1024]{1,0:T(8,128)S(1)}) custom-call(bf16[256,1024]{1,0:T(8,128)(2,1)} %bitcast.8, bf16[2,64,1024]{2,1,0:T(8,128)(2,1)} %refs_8_.3, bf16[2,3,2,512,512]{4,3,2,1,0:T(8,128)(2,1)} %refs_4_.1), custom_call_target="tpu_custom_call" | custom-call | tf_op jit(solution)/shard_map/pallas_call | solution.py:359
  21.2 8.9 %collective-permute-done.2.refs_3_ = bf16[256,512]{1,0:T(8,128)(2,1)S(1)} collective-permute-done((bf16[256,512]{1,0:T(8,128)(2,1)S(1)}, bf16[256,512]{1,0:T(8,128)(2,1)S(1)}, u32[]{:S(2)}, u32[]{:S(2)}) %collective-permute-start.2) | collective-permute-done | bytes 262176 | tf_op jit(solution)/shard_map/ppermute | solution.py:388
  30.1 0.0 collective-permute-done.3.refs_4_
  30.1 0.0 all-to-all-done.refs_0_
  30.1 3.6 %shard_map.123 = (f32[256,1024]{1,0:T(8,128)S(1)}, bf16[256,512]{1,0:T(8,128)(2,1)S(1)}, bf16[256,512]{1,0:T(8,128)(2,1)S(1)}) custom-call(bf16[8,48,384]{2,1,0:T(8,128)(2,1)S(1)} %all-to-all-done.refs_0_, bf16[2,48,384]{2,1,0:T(8,128)(2,1)S(1)} %get-tuple-element.24.refs_1_, f32[256,1024]{1,0:T(8,128)S(1)} %get-tuple-element.25.refs_2_, ...), custom_call_target="tpu_custom_call" | custom-call | tf_op jit(solution)/shard_map/pallas_call | solution.py:359
  33.7 0.0 copy-start
  33.8 0.0 collective-permute-done.refs_2_
  33.8 0.0 collective-permute-done.1.refs_3_
  33.8 3.4 %shard_map.124 = (bf16[8,112,256]{2,1,0:T(8,128)(2,1)}, bf16[128,1024]{1,0:T(8,128)(2,1)S(1)}) custom-call(bf16[8,48,384]{2,1,0:T(8,128)(2,1)S(1)} %all-to-all-done.refs_0_, f32[128,1024]{1,0:T(8,128)S(1)} %get-tuple-element.21.refs_1_, bf16[128,512]{1,0:T(8,128)(2,1)S(1)} %collective-permute-done.refs_2_, ...), custom_call_target="tpu_custom_call" | custom-call | tf_op jit(solution)/shard_map/pallas_call | solution.py:359
  37.2 0.0 copy-done
  37.2 5.7 %all-to-all-start.1 = ((bf16[8,112,256]{2,1,0:T(8,128)(2,1)}), bf16[8,112,256]{2,1,0:T(8,128)(2,1)S(1)}, u32[]{:S(2)}, u32[]{:S(2)}) async-start(bf16[8,112,256]{2,1,0:T(8,128)(2,1)} %get-tuple-element.30), calls=%async_computation.1 | async-start | bytes 917504 | tf_op jit(solution)/shard_map/all_to_all | solution.py:430
  42.9 0.0 collective-permute-start.5
  42.9 2.9 %collective-permute-start.4 = (bf16[256,512]{1,0:T(8,128)(2,1)S(1)}, bf16[256,512]{1,0:T(8,128)(2,1)S(1)}, u32[]{:S(2)}, u32[]{:S(2)}) collective-permute-start(bf16[256,512]{1,0:T(8,128)(2,1)S(1)} %get-tuple-element.29.refs_5_.refs_1_), channel_id=1, source_target_pairs={{0,4},{4,8},{8,12},{12,16},{16,20},{20,24},{24,28},{28,0},{1,5},{5... | collective-permute-start | bytes 786440 | tf_op jit(solution)/shard_map/ppermute | solution.py:388
  45.8 14.4 %all-to-all-done.1.refs_0_ = bf16[8,112,256]{2,1,0:T(8,128)(2,1)S(1)} async-done(((bf16[8,112,256]{2,1,0:T(8,128)(2,1)}), bf16[8,112,256]{2,1,0:T(8,128)(2,1)S(1)}, u32[]{:S(2)}, u32[]{:S(2)}) %all-to-all-start.1) | async-done | bytes 458784 | tf_op jit(solution)/shard_map/all_to_all | solution.py:430
  60.2 0.2 shard_map.127
  60.4 0.1 collective-permute-start.8
  60.5 0.6 collective-permute-start.7
  61.1 1.2 %collective-permute-start.6 = (f32[1,64]{1,0:T(1,128)S(1)}, f32[1,64]{1,0:T(1,128)S(1)}, u32[]{:S(2)}, u32[]{:S(2)}) collective-permute-start(f32[1,64]{1,0:T(1,128)S(1)} %get-tuple-element.32.refs_0_), channel_id=1, source_target_pairs={{0,1},{1,0},{2,3},{3,2},{4,5},{5,4},{6,7},{7,6},{8,9},{9,8},{10,11... | collective-permute-start | bytes 776 | tf_op jit(solution)/shard_map/ppermute | solution.py:436
  62.3 0.0 collective-permute-done.5.refs_3_
  62.3 0.0 collective-permute-done.4.refs_2_
  62.3 5.5 %shard_map.125.refs_2_ = f32[256,1024]{1,0:T(8,128)S(1)} custom-call(bf16[256,512]{1,0:T(8,128)(2,1)S(1)} %get-tuple-element.28.refs_4_.refs_0_, bf16[256,512]{1,0:T(8,128)(2,1)S(1)} %get-tuple-element.29.refs_5_.refs_1_, bf16[256,512]{1,0:T(8,128)(2,1)S(1)} %collective-permute-done.4.refs_2_, bf16[256,512]{1,0:T(8,128)(2,1)S(1)} %collective-permute-done.5.refs_3_, ...), custom_call_target="tpu_custom_call" | custom-call | tf_op jit(solution)/shard_map/pallas_call | solution.py:359
  67.9 2.5 %shard_map.126 = f32[2,128,1024]{2,1,0:T(8,128)} custom-call(bf16[8,112,256]{2,1,0:T(8,128)(2,1)S(1)} %all-to-all-done.1.refs_0_, bf16[2,48,384]{2,1,0:T(8,128)(2,1)S(1)} %get-tuple-element.24.refs_1_, f32[256,1024]{1,0:T(8,128)S(1)} %shard_map.125.refs_2_, bf16[2,2,24,512]{3,2,1,0:T(8,128)(2,1)} %refs_3_.3), custom_call_target="tpu_custom_call" | custom-call | tf_op jit(solution)/shard_map/pallas_call | solution.py:359
  70.4 0.0 collective-permute-done.8.refs_3_
  70.4 0.0 collective-permute-done.7.refs_2_
  70.4 0.0 collective-permute-done.6.refs_1_
  70.4 2.5 %shard_map.128 = (f32[2,128,1024]{2,1,0:T(8,128)}, f32[1,8]{1,0:T(1,128)}) custom-call(f32[1,64]{1,0:T(1,128)S(1)} %get-tuple-element.32.refs_0_, f32[1,64]{1,0:T(1,128)S(1)} %collective-permute-done.6.refs_1_, f32[1,64]{1,0:T(1,128)S(1)} %collective-permute-done.7.refs_2_, f32[1,64]{1,0:T(1,128)S(1)} %collective-permute-done.8.refs_3_, ...), custom_call_target="tpu_custom_call" | custom-call | tf_op jit(solution)/shard_map/pallas_call | solution.py:359
Async XLA Ops:
  4.3 25.9 %all-to-all-start = ((bf16[8,48,384]{2,1,0:T(8,128)(2,1)}), bf16[8,48,384]{2,1,0:T(8,128)(2,1)S(1)}, u32[]{:S(2)}, u32[]{:S(2)}) async-start(bf16[8,48,384]{2,1,0:T(8,128)(2,1)} %get-tuple-element.20), calls=%async_computation | async-start | bytes 589824 | tf_op jit(solution)/shard_map/all_to_all | solution.py:412
  11.7 18.5 %collective-permute-start.2 = (bf16[256,512]{1,0:T(8,128)(2,1)S(1)}, bf16[256,512]{1,0:T(8,128)(2,1)S(1)}, u32[]{:S(2)}, u32[]{:S(2)}) collective-permute-start(bf16[256,512]{1,0:T(8,128)(2,1)S(1)} %get-tuple-element.26), channel_id=1, source_target_pairs={{0,4},{4,8},{8,12},{12,16},{16,20},{20,24},{24,28},{28,0},{1,5},{5... | collective-permute-start | bytes 786440 | tf_op jit(solution)/shard_map/ppermute | solution.py:388
  13.2 16.9 %collective-permute-start.3 = (bf16[256,512]{1,0:T(8,128)(2,1)S(1)}, bf16[256,512]{1,0:T(8,128)(2,1)S(1)}, u32[]{:S(2)}, u32[]{:S(2)}) collective-permute-start(bf16[256,512]{1,0:T(8,128)(2,1)S(1)} %get-tuple-element.27), channel_id=1, source_target_pairs={{4,0},{8,4},{12,8},{16,12},{20,16},{24,20},{28,24},{0,28},{5,1},{9... | collective-permute-start | bytes 786440 | tf_op jit(solution)/shard_map/ppermute | solution.py:388
  13.7 20.0 %collective-permute-start = (bf16[128,512]{1,0:T(8,128)(2,1)S(1)}, bf16[128,512]{1,0:T(8,128)(2,1)S(1)}, u32[]{:S(2)}, u32[]{:S(2)}) collective-permute-start(bf16[128,512]{1,0:T(8,128)(2,1)S(1)} %get-tuple-element.22), channel_id=1, source_target_pairs={{0,4},{4,8},{8,12},{12,16},{16,20},{20,24},{24,28},{28,0},{1,5},{5... | collective-permute-start | bytes 393224 | tf_op jit(solution)/shard_map/ppermute | solution.py:388
  16.1 17.7 %collective-permute-start.1 = (bf16[128,512]{1,0:T(8,128)(2,1)S(1)}, bf16[128,512]{1,0:T(8,128)(2,1)S(1)}, u32[]{:S(2)}, u32[]{:S(2)}) collective-permute-start(bf16[128,512]{1,0:T(8,128)(2,1)S(1)} %get-tuple-element.23), channel_id=1, source_target_pairs={{4,0},{8,4},{12,8},{16,12},{20,16},{24,20},{28,24},{0,28},{5,1},{9... | collective-permute-start | bytes 393224 | tf_op jit(solution)/shard_map/ppermute | solution.py:388
  33.7 3.4 %copy-start = (f32[256,1024]{1,0:T(8,128)}, f32[256,1024]{1,0:T(8,128)S(1)}, u32[]{:S(2)}) copy-start(f32[256,1024]{1,0:T(8,128)S(1)} %get-tuple-element.31.refs_5_) | copy-start | bytes 3145732
  37.2 23.0 %all-to-all-start.1 = ((bf16[8,112,256]{2,1,0:T(8,128)(2,1)}), bf16[8,112,256]{2,1,0:T(8,128)(2,1)S(1)}, u32[]{:S(2)}, u32[]{:S(2)}) async-start(bf16[8,112,256]{2,1,0:T(8,128)(2,1)} %get-tuple-element.30), calls=%async_computation.1 | async-start | bytes 917504 | tf_op jit(solution)/shard_map/all_to_all | solution.py:430
  42.9 19.4 %collective-permute-start.5 = (bf16[256,512]{1,0:T(8,128)(2,1)S(1)}, bf16[256,512]{1,0:T(8,128)(2,1)S(1)}, u32[]{:S(2)}, u32[]{:S(2)}) collective-permute-start(bf16[256,512]{1,0:T(8,128)(2,1)S(1)} %get-tuple-element.28.refs_4_.refs_0_), channel_id=1, source_target_pairs={{4,0},{8,4},{12,8},{16,12},{20,16},{24,20},{28,24},{0,28},{5,1},{9... | collective-permute-start | bytes 786440 | tf_op jit(solution)/shard_map/ppermute | solution.py:388
  42.9 19.4 %collective-permute-start.4 = (bf16[256,512]{1,0:T(8,128)(2,1)S(1)}, bf16[256,512]{1,0:T(8,128)(2,1)S(1)}, u32[]{:S(2)}, u32[]{:S(2)}) collective-permute-start(bf16[256,512]{1,0:T(8,128)(2,1)S(1)} %get-tuple-element.29.refs_5_.refs_1_), channel_id=1, source_target_pairs={{0,4},{4,8},{8,12},{12,16},{16,20},{20,24},{24,28},{28,0},{1,5},{5... | collective-permute-start | bytes 786440 | tf_op jit(solution)/shard_map/ppermute | solution.py:388
  60.4 10.0 %collective-permute-start.8 = (f32[1,64]{1,0:T(1,128)S(1)}, f32[1,64]{1,0:T(1,128)S(1)}, u32[]{:S(2)}, u32[]{:S(2)}) collective-permute-start(f32[1,64]{1,0:T(1,128)S(1)} %get-tuple-element.32.refs_0_), channel_id=1, source_target_pairs={{0,3},{1,2},{2,1},{3,0},{4,7},{5,6},{6,5},{7,4},{8,11},{9,10},{10,... | collective-permute-start | bytes 776 | tf_op jit(solution)/shard_map/ppermute | solution.py:436
  60.5 9.9 %collective-permute-start.7 = (f32[1,64]{1,0:T(1,128)S(1)}, f32[1,64]{1,0:T(1,128)S(1)}, u32[]{:S(2)}, u32[]{:S(2)}) collective-permute-start(f32[1,64]{1,0:T(1,128)S(1)} %get-tuple-element.32.refs_0_), channel_id=1, source_target_pairs={{0,2},{1,3},{2,0},{3,1},{4,6},{5,7},{6,4},{7,5},{8,10},{9,11},{10,... | collective-permute-start | bytes 776 | tf_op jit(solution)/shard_map/ppermute | solution.py:436
  61.1 9.3 %collective-permute-start.6 = (f32[1,64]{1,0:T(1,128)S(1)}, f32[1,64]{1,0:T(1,128)S(1)}, u32[]{:S(2)}, u32[]{:S(2)}) collective-permute-start(f32[1,64]{1,0:T(1,128)S(1)} %get-tuple-element.32.refs_0_), channel_id=1, source_target_pairs={{0,1},{1,0},{2,3},{3,2},{4,5},{5,4},{6,7},{7,6},{8,9},{9,8},{10,11... | collective-permute-start | bytes 776 | tf_op jit(solution)/shard_map/ppermute | solution.py:436

commit v3 on v2

--- a/solution.py
+++ b/solution.py
@@ -10,6 +10,7 @@
 
 
 DAMPING = 0.8
+IN_FLIGHT = 16 << 20
 F32 = jnp.float32
 BF16 = jnp.bfloat16
 
@@ -41,18 +42,58 @@
     return jnp.concatenate([-x[:, h:], x[:, :h]], axis=1)
 
 
+def is_even():
+    return lax.rem(lax.axis_index("tile"), 2) == 0
+
+
+def put(near, far, left, right):
+    @pl.when(is_even())
+    def _():
+        near[...], far[...] = right, left
+
+    @pl.when(jnp.logical_not(is_even()))
+    def _():
+        near[...], far[...] = left, right
+
+
+def sides(near, far):
+    even = is_even()
+    return jnp.where(even, far, near), jnp.where(even, near, far)
+
+
 def stacked(x):
     return x.reshape(x.shape[0] * x.shape[1], x.shape[2])
 
 
+class Queue:
+    def __init__(self):
+        self.waiting, self.flying = [], 0
+
+    def add(self, copy, size):
+        self.waiting.append((copy, size))
+
+    def pump(self):
+        while self.waiting and self.flying < IN_FLIGHT:
+            copy, size = self.waiting.pop(0)
+            copy.start()
+            self.flying += size
+
+
 class Operand:
-    def __init__(self, copy, ref):
-        self.copy, self.ref = copy, ref
+    def __init__(self, ref, copy=None, queue=None):
+        self.ref, self.copy, self.queue = ref, copy, queue
+        if copy is not None:
+            queue.add(copy, padded(ref))
 
     def get(self):
         if self.copy is not None:
+            while any(copy is self.copy for copy, _ in self.queue.waiting):
+                self.queue.flying = 0
+                self.queue.pump()
             self.copy.wait()
             self.copy = None
+            self.queue.flying -= padded(self.ref)
+            self.queue.pump()
         return self.ref
 
     def __getitem__(self, index):
@@ -87,10 +128,13 @@
     return jnp.concatenate(parts, axis=0)
 
 
+def far_of(c, basis_re, basis_im):
+    return tn(c.astype(BF16), basis_re) + tn(lanes_turn(c).astype(BF16), basis_im)
+
+
 def expand(coeff_t, basis, i):
     rank = basis.shape[2]
-    c = coeff_t[i * rank : (i + 1) * rank]
-    return tn(c.astype(BF16), basis[i, 0]) + tn(lanes_turn(c).astype(BF16), basis[i, 1])
+    return far_of(coeff_t[i * rank : (i + 1) * rank], basis[i, 0], basis[i, 1])
 
 
 def first_kernel(e_ref, k_ref, s_ref, t_ref, c_ref, pr_ref, fl_ref, nb_ref, out, kept, left, right):
@@ -130,10 +174,25 @@
         out.ref[d, :, 0:rows] = coeff
         out.ref[d, :, rows:width] = back[d * lanes : (d + 1) * lanes].astype(BF16)
     out.send()
-    left.ref[...] = moved(k, nb_ref, tile, 0, 0).astype(BF16)
-    left.send()
-    right.ref[...] = moved(k, nb_ref, tile, tc - 1, 2).astype(BF16)
-    right.send()
+    pair = lax.rem(lax.axis_index("src"), 2)
+    part = k_ref.ref.shape[1] // 2
+    own = stacked(k_ref.get()[:, pl.ds(pl.multiple_of(pair * part, part), part), :])
+    sent = []
+    for i, o in ((0, 0), (tc - 1, 2)):
+        share = moved(own, nb_ref, tile, i, o).astype(BF16)
+        rows_of = [t_ref[i, 0].astype(F32), t_ref[i, 1].astype(F32)]
+        for at in range(0, columns, tile):
+            end = min(columns, at + tile)
+            for m in (m_re, m_im):
+                piece = m[:, at:end].astype(F32)[i * rank : (i + 1) * rank]
+                if end - at < tile:
+                    piece = jnp.concatenate([piece, jnp.zeros((rank, tile - end + at), F32)], axis=1)
+                rows_of.append(piece)
+        factors = jnp.concatenate(rows_of, axis=0)
+        half = factors.shape[0] // 2
+        factors = jnp.where(pair == 0, factors[:half], factors[half:]).astype(BF16)
+        sent.append(jnp.concatenate([share, factors], axis=0))
+    put(left.ref, right.ref, *sent)
 
 
 def moved(k, nb_ref, tile, i, o):
@@ -149,28 +208,49 @@
     return rows_join(p, q)
 
 
-def inside_kernel(v_ref, k_ref, nb_ref, near, loc, *, tile, tc):
+def inside_kernel(v_ref, k_ref, nb_ref, loc, near, early, *, tile, tc):
     v, k = v_ref[...], stacked(k_ref[...])
     fields = {i: v[:, i * tile : (i + 1) * tile] for i in range(tc)}
     for m in range(tc):
-        cut = slice(m * tile, (m + 1) * tile)
-        near.ref[:, cut] = near_of(fields, nb_ref, m, [o for o in range(3) if m + o - 1 in fields])
+        near.ref[:, m * tile : (m + 1) * tile] = near_of(fields, nb_ref, m, [o for o in range(3) if m + o - 1 in fields])
         total = None
         for o in range(3):
-            i = m + 1 - o
-            if 0 <= i < tc:
-                part = moved(k, nb_ref, tile, i, o)
+            if 0 <= m + 1 - o < tc:
+                part = moved(k, nb_ref, tile, m + 1 - o, o)
                 total = part if total is None else total + part
+        cut = slice(m * tile, (m + 1) * tile)
         loc.ref[:, cut] = total
+        loc.send(slice(None), cut)
+    early.ref[...] = DAMPING * nt(k, v)
+
+
+def edge_kernel(near_ref, hl_ref, hr_ref, v_ref, nb_ref, start, left, right, *, tile, tc):
+    fields = dict(zip((-1, tc), sides(hl_ref[...], hr_ref[...])))
+    v = v_ref[...]
+    ends = {}
+    for i in range(tc):
+        cut = slice(i * tile, (i + 1) * tile)
+        near = near_ref[:, cut]
+        for o in range(3):
+            if i + o - 1 in fields:
+                near = near + near_of(fields, nb_ref, i, [o])
+        value = v[:, cut].astype(F32) - DAMPING * near
+        start.ref[:, cut] = value
+        ends[i] = value.astype(BF16)
+    put(left.ref, right.ref, ends[0], ends[tc - 1])
 
 
 def second_near_kernel(*refs, tile, tc):
     fields = {i: refs[i][...] for i in range(tc)}
-    hl_ref, hr_ref, nb_ref, base_ref, out = refs[tc:]
-    fields[-1], fields[tc] = hl_ref[...], hr_ref[...]
+    hl_ref, hr_ref, edge_ref, bases_ref, e_ref, nb_ref, out = refs[tc:]
+    for at, (i, h) in enumerate(zip((-1, tc), sides(hl_ref[...], hr_ref[...]))):
+        far = far_of(edge_ref[at], bases_ref[at, 0], bases_ref[at, 1])
+        fields[i] = (h.astype(F32) - DAMPING * far).astype(BF16)
     for i in range(tc):
         cut = slice(i * tile, (i + 1) * tile)
-        out.ref[:, cut] = base_ref[:, cut] - DAMPING * near_of(fields, nb_ref, i, range(3))
+        near = near_of(fields, nb_ref, i, range(3))
+        start = (1.0 - DAMPING) * fields[i].astype(F32) + DAMPING * stacked(e_ref[:, :, cut]).astype(F32)
+        out.ref[:, cut] = start - DAMPING * near
 
 
 def coupled_of(gathered, m_ref):
@@ -179,73 +259,99 @@
     return coupled.astype(BF16).astype(F32)
 
 
-def update_kernel(got_ref, m_ref, near_ref, hl_ref, hr_ref, t_ref, e_ref, nb_ref, base, *tiles_out, tile, tc):
+def middle_kernel(*refs, tile, tc):
+    got_ref, m_ref, t_ref, start_ref, s_ref, gl_ref, ol_ref, gr_ref, or_ref, early_ref, loc_ref, k_ref = refs[:12]
+    tiles_out, (side, out, edge, bases) = refs[12 : 12 + tc], refs[12 + tc :]
     n, lanes, _ = got_ref.ref.shape
-    rows = base.ref.shape[0]
-    coupled = coupled_of(got_ref[:, :, 0:rows].reshape(n * lanes, rows), m_ref)
-    edges = {-1: hl_ref[...], tc: hr_ref[...]}
+    rows = out.ref.shape[1]
+    focal = k_ref.ref.shape[1]
+    rank = t_ref.ref.shape[2]
+    columns = n * lanes
+    first = lax.rem(lax.axis_index("src"), 2) == 0
+
+    def whole(own, other):
+        own, other = own.astype(F32), other.astype(F32)
+        low, high = jnp.where(first, own, other), jnp.where(first, other, own)
+        half = focal // 2
+        share = jnp.concatenate([low[:half], high[:half], low[half:focal], high[half:focal]], axis=0)
+        factors = jnp.concatenate([low[focal:], high[focal:]], axis=0)
+        basis = [factors[p * rank : (p + 1) * rank].astype(BF16) for p in range(2)]
+        turns = []
+        for p in range(2):
+            pieces = [
+                factors[(2 + 2 * c + p) * rank : (3 + 2 * c + p) * rank] for c in range(-(-columns // tile))
+            ]
+            turns.append((jnp.concatenate(pieces, axis=1) if len(pieces) > 1 else pieces[0])[:, :columns])
+        return share, basis, turns
+
+    (gl, gr), (ol, on_right) = sides(gl_ref[...], gr_ref[...]), sides(ol_ref[...], or_ref[...])
+    share_l, basis_l, turns_l = whole(gl, ol)
+    share_r, basis_r, turns_r = whole(gr, on_right)
+
+    gathered = got_ref[:, :, 0:rows].reshape(columns, rows)
+    stack = [
+        jnp.concatenate([turns_l[p], m_ref[p].astype(F32), turns_r[p]], axis=0).astype(BF16) for p in range(2)
+    ]
+    coupled = (nn(stack[0], gathered) + nn(stack[1], lanes_turn(gathered))).astype(BF16).astype(F32)
+    fields = []
     for i in range(tc):
-        cut = slice(i * tile, (i + 1) * tile)
-        total = near_ref[:, cut] + expand(coupled, t_ref.get(), i)
-        for o in range(3):
-            if i + o - 1 in edges:
-                total = total + near_of(edges, nb_ref, i, [o])
-        start = stacked(e_ref[:, :, cut]).astype(F32)
-        field = start - DAMPING * total
-        tiles_out[i].ref[...] = field.astype(BF16)
-        base.ref[:, cut] = (1.0 - DAMPING) * field + DAMPING * start
-        base.send(slice(None), cut)
-
-
-def focal_kernel(*refs, tile, tc):
-    got_ref, loc_ref, gl_ref, gr_ref = refs[:4]
-    fields = [ref[...] for ref in refs[4 : 4 + tc]]
-    s_ref, k_ref, e_ref, out, side = refs[4 + tc :]
-    n, _, rows = out.ref.shape
-    focal = gl_ref.ref.shape[0] // 2
+        far = far_of(coupled[(i + 1) * rank : (i + 2) * rank], t_ref[i, 0], t_ref[i, 1])
+        field = start_ref[:, i * tile : (i + 1) * tile] - DAMPING * far
+        fields.append(field.astype(BF16))
+        tiles_out[i].ref[...] = fields[i]
+    edge.ref[0], edge.ref[1] = coupled[:rank], coupled[(tc + 1) * rank :]
+    for p in range(2):
+        bases.ref[0, p], bases.ref[1, p] = basis_l[p], basis_r[p]
     back = jnp.sum(got_ref[:, :, rows:].astype(F32), axis=0).astype(BF16).astype(F32)
     k = stacked(k_ref[...])
-    p = None
+    p = early_ref[...]
+    half = rows // 2
     for i in range(tc):
         cut = slice(i * tile, (i + 1) * tile)
         total = loc_ref[:, cut] + expand(back, s_ref.get(), i)
         if i == 0:
-            total = total + gl_ref[...].astype(F32)
+            total = total + share_l
         if i == tc - 1:
-            total = total + gr_ref[...].astype(F32)
+            total = total + share_r
         own = (-DAMPING * total).astype(BF16)
         side.ref[:, cut] = own
-        start = stacked(e_ref[:, :, cut]).astype(F32)
-        mix = ((1.0 - DAMPING) * fields[i].astype(F32) + DAMPING * start).astype(BF16)
-        term = nt(k[:, cut], mix) + nt(own, fields[i])
-        p = term if p is None else p + term
+        side.send(slice(None), cut)
+        p = p + (1.0 - DAMPING) * nt(k[:, cut], fields[i]) + nt(own, fields[i])
     half = rows // 2
     part = jnp.concatenate(
         [p[:focal, :half] - p[focal:, half:], p[:focal, half:] + p[focal:, :half]], axis=1
     ).astype(BF16)
     coeff = project(s_ref.get(), fields).astype(BF16)
-    for d in range(n):
-        out.ref[d, :focal] = part
-        out.ref[d, focal:] = coeff
+    out.ref[:focal] = part
+    out.ref[focal:] = coeff
 
 
 def eye(n):
     return lax.broadcasted_iota(jnp.int32, (n, n), 0) == lax.broadcasted_iota(jnp.int32, (n, n), 1)
 
 
-def sum_kernel(got_ref, foc, power):
-    focal = foc.ref.shape[0]
+def pair_kernel(own_ref, other_ref, out, *, focal, group):
+    lanes = own_ref.ref.shape[0] - focal
+    first = lax.rem(lax.axis_index("tile") // group, 2) == 0
+    own, other = own_ref[...].astype(F32), other_ref[...].astype(F32)
+    out.ref[:focal] = (own[:focal] + other[:focal]).astype(BF16)
+    out.ref[focal : focal + lanes] = jnp.where(first, own[focal:], other[focal:]).astype(BF16)
+    out.ref[focal + lanes :] = jnp.where(first, other[focal:], own[focal:]).astype(BF16)
+
+
+def sum_kernel(*refs, focal):
+    gots, (foc, power) = refs[:-2], refs[-2:]
     half = foc.ref.shape[1] // 2
-    total = jnp.sum(got_ref[:, 0:focal].astype(F32), axis=0)
+    total = gots[0][:focal].astype(F32)
+    for got in gots[1:]:
+        total = total + got[:focal].astype(F32)
     foc.ref[...] = total
     squares = total[:, :half] * total[:, :half] + total[:, half:] * total[:, half:]
     column = jnp.sum(squares, axis=1, keepdims=True)
     power.ref[...] = jnp.sum(jnp.where(eye(focal), column, 0.0), axis=0, keepdims=True)
-    power.send()
-    foc.send()
-
-
-def last_kernel(a_ref, b_ref, c_ref, d_ref, foc_ref, side_ref, target_ref, owner_ref, k_ref, adj, res, *, sources, scale):
+
+
+def last_kernel(a_ref, b_ref, c_ref, d_ref, foc_ref, target_ref, owner_ref, k_ref, side_ref, adj, res, *, sources, scale):
     focal = foc_ref.ref.shape[0]
     half = foc_ref.ref.shape[1] // 2
     intensity = (a_ref[...] + b_ref[...]) + (c_ref[...] + d_ref[...])
@@ -273,11 +379,17 @@
         adj.send(slice(None), slice(None), cut)
 
 
-def field_kernel(got_ref, m_ref, near_ref, t_ref, out, *, tile, tc):
-    n, _, rows = got_ref.ref.shape
-    lanes = m_ref.ref.shape[1]
+def field_kernel(*refs, tile, tc, focal, group):
+    gots, (m_ref, near_ref, t_ref, out) = refs[:-5], refs[-5:-1]
+    all_ref = refs[-1]
+    rows = all_ref.shape[1]
     half = rows // 2
-    coupled = coupled_of(got_ref[:, -lanes:].reshape(n * lanes, rows), m_ref)
+    pair = gots[0].ref.shape[0] - focal
+    here = lax.axis_index("tile") // group
+    for k, got in enumerate(gots):
+        at = jnp.bitwise_xor(here, k)
+        all_ref[pl.ds(pl.multiple_of(at * pair, pair), pair), :] = got[focal:]
+    coupled = coupled_of(all_ref[...], m_ref)
     for i in range(tc):
         cut = slice(i * tile, (i + 1) * tile)
         field = near_ref[:, cut] - DAMPING * expand(coupled, t_ref.get(), i)
@@ -286,12 +398,13 @@
         out.send(slice(None), slice(None), cut)
 
 
-def edges_kernel(v_ref, left_ref, right_ref, sems):
-    width, tile = v_ref.shape[1], left_ref.shape[1]
-    copies = [
-        pltpu.make_async_copy(v_ref.at[:, 0:tile], left_ref, sems.at[0]),
-        pltpu.make_async_copy(v_ref.at[:, width - tile : width], right_ref, sems.at[1]),
-    ]
+def edges_kernel(v_ref, near_ref, far_ref, sems):
+    width, tile = v_ref.shape[1], near_ref.shape[1]
+    odd = lax.rem(lax.axis_index("tile"), 2)
+    copies = []
+    for at, (ref, side) in enumerate(((near_ref, 1 - odd), (far_ref, odd))):
+        begin = pl.multiple_of(side * (width - tile), 128)
+        copies.append(pltpu.make_async_copy(v_ref.at[:, pl.ds(begin, tile)], ref, sems.at[at]))
     for copy in copies:
         copy.start()
     for copy in copies:
@@ -310,13 +423,14 @@
     return math.prod(one.shape[:-1]) * -(-one.shape[-1] // 128) * 128 * jnp.dtype(one.dtype).itemsize
 
 
-def call(kernel, outs, near, far=(), blocks=(), far_outs=()):
+def call(kernel, outs, near, far=(), blocks=(), far_outs=(), extra=()):
     far = [in_hbm(arg) for arg in far]
     held = [len(blocks) if arg.ndim == 5 and blocks else 0 for arg in far]
     scratch = [
         pltpu.VMEM((count,) + arg.shape[2:] if count else arg.shape, arg.dtype) for arg, count in zip(far, held)
     ]
     scratch += [pltpu.VMEM(*outs[o]) for o in far_outs]
+    scratch += [pltpu.VMEM(*one) for one in extra]
     taken = sum(padded(one) for one in scratch) + 3 * sum(padded(jax.ShapeDtypeStruct(s, d)) for s, d in outs)
     taken += 2 * sum(padded(one) for one in near)
     scratch += [pltpu.SemaphoreType.DMA((sum(count or 1 for count in held) + 1,))]
@@ -324,31 +438,30 @@
 
     def run(*refs):
         refs = list(refs)
-        close = [Operand(None, refs.pop(0)) for _ in near]
+        close = [Operand(refs.pop(0)) for _ in near]
+        queue = Queue()
         sources = [refs.pop(0) for _ in far]
         sinks = [refs.pop(0) for _ in outs]
         places = [refs.pop(0) for _ in far]
         stages = {o: refs.pop(0) for o in far_outs}
-        ins, ends = refs
+        more, (ins, ends) = refs[: len(extra)], refs[len(extra) :]
         operands, at = [], 0
         for source, place, count in zip(sources, places, held):
             if count:
                 parts = {}
                 for spot, block in enumerate(blocks):
                     copy = pltpu.make_async_copy(source.at[block], place.at[spot], ins.at[at])
-                    copy.start()
                     at += 1
-                    parts[block] = Operand(copy, place.at[spot])
+                    parts[block] = Operand(place.at[spot], copy, queue)
                 operands.append(Blocks(parts))
             else:
-                copy = pltpu.make_async_copy(source, place, ins.at[at])
-                copy.start()
+                operands.append(Operand(place, pltpu.make_async_copy(source, place, ins.at[at]), queue))
                 at += 1
-                operands.append(Operand(copy, place))
+        queue.pump()
         results = []
         for o, sink in enumerate(sinks):
             results.append(Result(stages[o], sink, ends.at[far_outs.index(o)]) if o in stages else Result(sink))
-        kernel(*close, *operands, *results)
+        kernel(*close, *operands, *results, *more)
         for operand in operands:
             for one in operand.operands.values() if isinstance(operand, Blocks) else [operand]:
                 one.get()
@@ -358,7 +471,9 @@
 
     return pl.pallas_call(
         run,
-        out_shape=[jax.ShapeDtypeStruct(s, d) for s, d in outs],
+        out_shape=[
+            pltpu.HBM(s, d) if o in far_outs else jax.ShapeDtypeStruct(s, d) for o, (s, d) in enumerate(outs)
+        ],
         in_specs=[VM] * len(near) + [FAR] * len(far),
         out_specs=[FAR if o in far_outs else VM for o in range(len(outs))],
         scratch_shapes=scratch,
@@ -381,14 +496,14 @@
     edges = [(0, 0), (tc - 1, 2)]
     inside = [(i, o) for i in range(tc) for o in range(3) if (i, o) not in edges]
     sizes = dict(tile=tile, tc=tc)
-    up = [(i, (i + 1) % n) for i in range(n)]
-    down = [(j, i) for i, j in up]
-
-    def exchange(to_left, to_right):
-        return lax.ppermute(to_right, "tile", up), lax.ppermute(to_left, "tile", down)
+    every = [(i, o) for i in range(tc) for o in range(3)]
+    within = [(i, i ^ 1) for i in range(n)]
+    across = [(i, (i - 1 + 2 * (i % 2)) % n) for i in range(n)]
+
+    def exchange(near, far):
+        return lax.ppermute(near, "tile", within), lax.ppermute(far, "tile", across)
 
     flat = stacked(e)
-    every = [(i, o) for i in range(tc) for o in range(3)]
     el, er = pl.pallas_call(
         edges_kernel,
         out_shape=[jax.ShapeDtypeStruct((rows, tile), BF16)] * 2,
@@ -404,44 +519,63 @@
         [
             ((n, lanes, rows + 2 * focal), BF16),
             ((2, lanes, tiles * rank), BF16),
-            ((2 * focal, tile), BF16),
-            ((2 * focal, tile), BF16),
+            ((focal + rank * (1 + -(-tiles * rank // tile)), tile), BF16),
+            ((focal + rank * (1 + -(-tiles * rank // tile)), tile), BF16),
         ],
         [], [e, fk, sb, tb, jnp.swapaxes(coupling, 1, 2), pair_rank.T, far_link.T, nb], blocks=edges,
     )
     got = lax.all_to_all(send, "tile", split_axis=0, concat_axis=0, tiled=True)
     from_left, from_right = exchange(gl, gr)
-    near, loc = call(
+    loc, near, early = call(
         functools.partial(inside_kernel, **sizes),
-        [((rows, width), F32), ((2 * focal, width), F32)],
-        [], [flat, fk, nb], blocks=inside,
-    )
-    base, *f1 = call(
-        functools.partial(update_kernel, **sizes),
-        [((rows, width), F32)] + [((rows, tile), BF16)] * tc,
-        [got, masked, near, hl, hr], [tb, e, nb], blocks=edges, far_outs=(0,),
-    )
-    hl1, hr1 = exchange(f1[0], f1[-1])
-    send1, side = call(
-        functools.partial(focal_kernel, **sizes),
-        [((n, focal + lanes, rows), BF16), ((2 * focal, width), BF16)],
-        [got, loc, from_left, from_right, *f1], [sb, fk, e],
-    )
-    got1 = lax.all_to_all(send1, "tile", split_axis=0, concat_axis=0, tiled=True)
+        [((2 * focal, width), F32), ((rows, width), F32), ((2 * focal, rows), F32)],
+        [], [flat, fk, nb], blocks=inside, far_outs=(0,),
+    )
+    start, ql, qr = call(
+        functools.partial(edge_kernel, **sizes),
+        [((rows, width), F32), ((rows, tile), BF16), ((rows, tile), BF16)],
+        [near, hl, hr], [flat, nb], blocks=edges,
+    )
+    hl1, hr1 = exchange(ql, qr)
+    swap = [(i, i ^ 1) for i in range(groups)]
+    other_left, other_right = lax.ppermute(from_left, "src", swap), lax.ppermute(from_right, "src", swap)
+    *f1, side, send1, edge, bases = call(
+        functools.partial(middle_kernel, **sizes),
+        [((rows, tile), BF16)] * tc
+        + [
+            ((2 * focal, width), BF16),
+            ((focal + lanes, rows), BF16),
+            ((2, rank, rows), F32),
+            ((2, 2, rank, tile), BF16),
+        ],
+        [got, masked, tb, start, sb, from_left, other_left, from_right, other_right, early], [loc, fk],
+        far_outs=(tc,),
+    )
+    group = 1
+    while n // group > 4:
+        other = lax.ppermute(send1, "tile", [(i, i ^ group) for i in range(n)])
+        (send1,) = call(
+            functools.partial(pair_kernel, focal=focal, group=group),
+            [((focal + 2 * group * lanes, rows), BF16)], [send1, other],
+        )
+        group *= 2
+    gots = [send1]
+    for k in range(group, n, group):
+        gots.append(lax.ppermute(send1, "tile", [(i, i ^ k) for i in range(n)]))
     (near1,) = call(
         functools.partial(second_near_kernel, **sizes), [((rows, width), F32)],
-        [*f1, hl1, hr1], [nb, base], blocks=every,
-    )
-    foc, part = call(sum_kernel, [((focal, rows), F32), ((1, focal), F32)], [got1])
+        [*f1, hl1, hr1, edge, bases], [e, nb], blocks=every,
+    )
+    foc, part = call(functools.partial(sum_kernel, focal=focal), [((focal, rows), F32), ((1, focal), F32)], gots)
     parts = [part] + [lax.ppermute(part, "src", [(i, i ^ k) for i in range(groups)]) for k in (1, 2, 3)]
     adjoint, residual = call(
         functools.partial(last_kernel, sources=half * groups, scale=(tiles * tile / focal) ** 0.5),
         [((2, half, width), F32), ((1, slots), F32)],
-        [*parts, foc, side], [target[None], owner[None], fk], far_outs=(0, 1),
+        [*parts, foc], [target[None], owner[None], fk, side], far_outs=(0, 1),
     )
     (field,) = call(
-        functools.partial(field_kernel, **sizes), [((2, half, width), F32)],
-        [got1, masked, near1], [tb], far_outs=(0,),
+        functools.partial(field_kernel, focal=focal, group=group, **sizes), [((2, half, width), F32)],
+        [*gots, masked, near1, tb], far_outs=(0,), extra=[((n * lanes, rows), BF16)],
     )
     return field, residual[0], adjoint
 

time: 73.7 us -> 70.4 us (0.955)
  the two profiles are of different devices: /device:TPU:6 before, /device:TPU:0 now
where the time goes in v3:
time: 70.4 us; the launch traced here: 70.1 us
  starting transfers between devices  25.9 us (37%)
  Pallas kernels  24.9 us (35%)
  waiting for transfers between devices  18.5 us (26%)
  between operations  0.76 us (1%)
    pallas_call x9, Pallas kernels, call(): pl.pallas_call(run, out_shape=[pltpu.HBM(s, d) if o in far_outs else jax....  23.9 us
    ppermute x3, starting transfers between devices, exchange(): lax.ppermute(far, 'tile', across)  8.83 us
    all_to_all x1, starting transfers between devices, per_device(): got = lax.all_to_all(send, 'tile', split_axis=0, concat_axis=0, tiled=True)  7.32 us
    ppermute x3, waiting for transfers between devices, exchange(): lax.ppermute(near, 'tile', within)  6.52 us
    ppermute x3, waiting for transfers between devices, per_device(): gots.append(lax.ppermute(send1, 'tile', [(i, i ^ k) for i in range(n)]))  6.07 us
    ppermute x1, waiting for transfers between devices, per_device(): other = lax.ppermute(send1, 'tile', [(i, i ^ group) for i in range(n)])  4.92 us
    ppermute x3, starting transfers between devices, per_device(): gots.append(lax.ppermute(send1, 'tile', [(i, i ^ k) for i in range(n)]))  4.5 us
    ppermute x3, starting transfers between devices, exchange(): lax.ppermute(near, 'tile', within)  2.74 us
  transfers between devices with their start and end apart: 16, of which 7 were waited for; matrix products, arithmetic and copies ran while one was open for 0% of the time, Pallas kernels for 26%

profile of v3, /device:TPU:0, one launch (start us, length us, event | category | flops | bytes accessed | tf_op | source)
XLA Modules:
  0.0 70.1 jit_solution(15793204672524253321)
XLA Ops:
  0.6 4.0 %shard_map.121 = (bf16[8,48,384]{2,1,0:T(8,128)(2,1)}, bf16[2,48,384]{2,1,0:T(8,128)(2,1)S(1)}, bf16[112,512]{1,0:T(8,128)(2,1)S(1)}, bf16[112,512]{1,0:T(8,128)(2,1)S(1)}) custom-call(bf16[2,128,1024]{2,1,0:T(8,128)(2,1)} %refs_6_.2, bf16[2,64,1024]{2,1,0:T(8,128)(2,1)} %refs_7_.5, bf16[2,2,24,512]{3,2,1,0:T(8,128)(2,1)} %refs_4_.3, ...), custom_call_target="tpu_custom_call" | custom-call | tf_op jit(solution)/shard_map/pallas_call | solution.py:472
  4.7 7.3 %all-to-all-start = ((bf16[8,48,384]{2,1,0:T(8,128)(2,1)}), bf16[8,48,384]{2,1,0:T(8,128)(2,1)S(1)}, u32[]{:S(2)}, u32[]{:S(2)}) async-start(bf16[8,48,384]{2,1,0:T(8,128)(2,1)} %get-tuple-element.25), calls=%async_computation | async-start | bytes 589824 | tf_op jit(solution)/shard_map/all_to_all | solution.py:527
  12.0 1.0 %ends.1 = (bf16[256,512]{1,0:T(8,128)(2,1)S(1)}, bf16[256,512]{1,0:T(8,128)(2,1)S(1)}) custom-call(bf16[256,1024]{1,0:T(8,128)(2,1)} %bitcast.7), custom_call_target="tpu_custom_call" | custom-call | tf_op jit(solution)/shard_map/ends/pallas_call | solution.py:507
  13.1 2.1 %collective-permute-start = (bf16[256,512]{1,0:T(8,128)(2,1)S(1)}, bf16[256,512]{1,0:T(8,128)(2,1)S(1)}, u32[]{:S(2)}, u32[]{:S(2)}) collective-permute-start(bf16[256,512]{1,0:T(8,128)(2,1)S(1)} %get-tuple-element.28), channel_id=1, source_target_pairs={{0,4},{4,0},{8,12},{12,8},{16,20},{20,16},{24,28},{28,24},{1,5},{5... | collective-permute-start | bytes 786440 | tf_op jit(solution)/shard_map/ppermute | solution.py:504
  15.1 3.3 %collective-permute-start.1 = (bf16[256,512]{1,0:T(8,128)(2,1)S(1)}, bf16[256,512]{1,0:T(8,128)(2,1)S(1)}, u32[]{:S(2)}, u32[]{:S(2)}) collective-permute-start(bf16[256,512]{1,0:T(8,128)(2,1)S(1)} %get-tuple-element.29), channel_id=1, source_target_pairs={{0,28},{4,8},{8,4},{12,16},{16,12},{20,24},{24,20},{28,0},{1,29},{... | collective-permute-start | bytes 786440 | tf_op jit(solution)/shard_map/ppermute | solution.py:504
  18.4 0.0 collective-permute-start.2
  18.4 0.0 copy-start
  18.4 0.0 copy-start.1
  18.4 2.0 %collective-permute-start.4 = (bf16[112,512]{1,0:T(8,128)(2,1)S(1)}, bf16[112,512]{1,0:T(8,128)(2,1)S(1)}, u32[]{:S(2)}, u32[]{:S(2)}) collective-permute-start(bf16[112,512]{1,0:T(8,128)(2,1)S(1)} %get-tuple-element.32), channel_id=1, source_target_pairs={{0,28},{4,8},{8,4},{12,16},{16,12},{20,24},{24,20},{28,0},{1,29},{... | collective-permute-start | bytes 344072 | tf_op jit(solution)/shard_map/ppermute | solution.py:504
  20.4 5.6 %shard_map.122 = (f32[128,1024]{1,0:T(8,128)}, f32[256,1024]{1,0:T(8,128)S(1)}, f32[128,256]{1,0:T(8,128)S(1)}) custom-call(bf16[256,1024]{1,0:T(8,128)(2,1)} %bitcast.8, bf16[2,64,1024]{2,1,0:T(8,128)(2,1)} %refs_7_.5, bf16[2,3,2,512,512]{4,3,2,1,0:T(8,128)(2,1)} %refs_7_.4), custom_call_target="tpu_custom_call" | custom-call | tf_op jit(solution)/shard_map/pallas_call | solution.py:472
  26.1 6.5 %collective-permute-done.refs_1_ = bf16[256,512]{1,0:T(8,128)(2,1)S(1)} collective-permute-done((bf16[256,512]{1,0:T(8,128)(2,1)S(1)}, bf16[256,512]{1,0:T(8,128)(2,1)S(1)}, u32[]{:S(2)}, u32[]{:S(2)}) %collective-permute-start) | collective-permute-done | bytes 262176 | tf_op jit(solution)/shard_map/ppermute | solution.py:504
  32.6 0.0 collective-permute-done.1.refs_2_
  32.6 2.5 %shard_map.123 = (f32[256,1024]{1,0:T(8,128)S(1)}, bf16[256,512]{1,0:T(8,128)(2,1)S(1)}, bf16[256,512]{1,0:T(8,128)(2,1)S(1)}) custom-call(f32[256,1024]{1,0:T(8,128)S(1)} %get-tuple-element.27.refs_0_, bf16[256,512]{1,0:T(8,128)(2,1)S(1)} %collective-permute-done.refs_1_, bf16[256,512]{1,0:T(8,128)(2,1)S(1)} %collective-permute-done.1.refs_2_, ...), custom_call_target="tpu_custom_call" | custom-call | tf_op jit(solution)/shard_map/pallas_call | solution.py:472
  35.1 0.7 collective-permute-start.10
  35.8 3.5 %collective-permute-start.11 = (bf16[256,512]{1,0:T(8,128)(2,1)S(1)}, bf16[256,512]{1,0:T(8,128)(2,1)S(1)}, u32[]{:S(2)}, u32[]{:S(2)}) collective-permute-start(bf16[256,512]{1,0:T(8,128)(2,1)S(1)} %get-tuple-element.39), channel_id=1, source_target_pairs={{0,28},{4,8},{8,4},{12,16},{16,12},{20,24},{24,20},{28,0},{1,29},{... | collective-permute-start | bytes 786440 | tf_op jit(solution)/shard_map/ppermute | solution.py:504
  39.3 0.0 collective-permute-done.2.refs_5_
  39.3 0.0 collective-permute-start.3
  39.3 0.0 collective-permute-done.4.refs_7_
  39.3 0.5 collective-permute-start.5
  39.8 0.8 %collective-permute-done.3.refs_6_ = bf16[112,512]{1,0:T(8,128)(2,1)S(1)} collective-permute-done((bf16[112,512]{1,0:T(8,128)(2,1)S(1)}, bf16[112,512]{1,0:T(8,128)(2,1)S(1)}, u32[]{:S(2)}, u32[]{:S(2)}) %collective-permute-start.3) | collective-permute-done | bytes 114720 | tf_op jit(solution)/shard_map/ppermute | solution.py:541
  40.6 0.2 collective-permute-done.5.refs_8_
  40.8 0.0 all-to-all-done.refs_0_
  40.8 0.0 copy-done
  40.8 0.0 copy-done.1
  40.8 2.8 %shard_map.124 = (bf16[256,512]{1,0:T(8,128)(2,1)S(1)}, bf16[256,512]{1,0:T(8,128)(2,1)S(1)}, bf16[128,1024]{1,0:T(8,128)(2,1)}, bf16[112,256]{1,0:T(8,128)(2,1)...) custom-call(bf16[8,48,384]{2,1,0:T(8,128)(2,1)S(1)} %all-to-all-done.refs_0_, ...), custom_call_target="tpu_custom_call" | custom-call | tf_op jit(solution)/shard_map/pallas_call | solution.py:472
  43.6 0.1 collective-permute-start.6
  43.7 4.9 %collective-permute-done.6.refs_1_ = bf16[112,256]{1,0:T(8,128)(2,1)S(1)} collective-permute-done((bf16[112,256]{1,0:T(8,128)(2,1)S(1)}, bf16[112,256]{1,0:T(8,128)(2,1)S(1)}, u32[]{:S(2)}, u32[]{:S(2)}) %collective-permute-start.6) | collective-permute-done | bytes 57376 | tf_op jit(solution)/shard_map/ppermute | solution.py:556
  48.6 0.1 shard_map.125.refs_0_
  48.7 2.1 %collective-permute-start.7 = (bf16[160,256]{1,0:T(8,128)(2,1)S(1)}, bf16[160,256]{1,0:T(8,128)(2,1)S(1)}, u32[]{:S(2)}, u32[]{:S(2)}) collective-permute-start(bf16[160,256]{1,0:T(8,128)(2,1)S(1)} %shard_map.125.refs_0_), channel_id=1, source_target_pairs={{0,8},{4,12},{8,0},{12,4},{16,24},{20,28},{24,16},{28,20},{1,9},{5... | collective-permute-start | bytes 245768 | tf_op jit(solution)/shard_map/ppermute | solution.py:564
  50.8 2.2 %collective-permute-start.8 = (bf16[160,256]{1,0:T(8,128)(2,1)S(1)}, bf16[160,256]{1,0:T(8,128)(2,1)S(1)}, u32[]{:S(2)}, u32[]{:S(2)}) collective-permute-start(bf16[160,256]{1,0:T(8,128)(2,1)S(1)} %shard_map.125.refs_0_), channel_id=1, source_target_pairs={{0,16},{4,20},{8,24},{12,28},{16,0},{20,4},{24,8},{28,12},{1,17},{... | collective-permute-start | bytes 245768 | tf_op jit(solution)/shard_map/ppermute | solution.py:564
  52.9 0.3 collective-permute-start.9
  53.2 0.4 collective-permute-done.7.refs_1_
  53.6 4.7 %collective-permute-done.8.refs_2_ = bf16[160,256]{1,0:T(8,128)(2,1)S(1)} collective-permute-done((bf16[160,256]{1,0:T(8,128)(2,1)S(1)}, bf16[160,256]{1,0:T(8,128)(2,1)S(1)}, u32[]{:S(2)}, u32[]{:S(2)}) %collective-permute-start.8) | collective-permute-done | bytes 81952 | tf_op jit(solution)/shard_map/ppermute | solution.py:564
  58.3 1.0 %collective-permute-done.9.refs_3_ = bf16[160,256]{1,0:T(8,128)(2,1)S(1)} collective-permute-done((bf16[160,256]{1,0:T(8,128)(2,1)S(1)}, bf16[160,256]{1,0:T(8,128)(2,1)S(1)}, u32[]{:S(2)}, u32[]{:S(2)}) %collective-permute-start.9) | collective-permute-done | bytes 81952 | tf_op jit(solution)/shard_map/ppermute | solution.py:564
  59.3 0.2 shard_map.128
  59.5 0.1 collective-permute-start.12
  59.6 1.6 %collective-permute-start.13 = (f32[1,64]{1,0:T(1,128)S(1)}, f32[1,64]{1,0:T(1,128)S(1)}, u32[]{:S(2)}, u32[]{:S(2)}) collective-permute-start(f32[1,64]{1,0:T(1,128)S(1)} %get-tuple-element.42.refs_0_), channel_id=1, source_target_pairs={{0,2},{1,3},{2,0},{3,1},{4,6},{5,7},{6,4},{7,5},{8,10},{9,11},{10,... | collective-permute-start | bytes 776 | tf_op jit(solution)/shard_map/ppermute | solution.py:570
  61.1 0.3 collective-permute-start.14
  61.4 0.0 collective-permute-done.10.refs_2_
  61.4 0.0 collective-permute-done.11.refs_3_
  61.4 4.2 %shard_map.126.refs_5_ = f32[256,1024]{1,0:T(8,128)S(1)} custom-call(bf16[256,512]{1,0:T(8,128)(2,1)S(1)} %get-tuple-element.36.refs_0_, bf16[256,512]{1,0:T(8,128)(2,1)S(1)} %get-tuple-element.37.refs_1_, bf16[256,512]{1,0:T(8,128)(2,1)S(1)} %collective-permute-done.10.refs_2_, bf16[256,512]{1,0:T(8,128)(2,1)S(1)} %collective-permute-done.11.refs_3_, ...), custom_call_target="tpu_custom_call" | custom-call | tf_op jit(solution)/shard_map/pallas_call | solution.py:472
  65.6 1.8 %shard_map.127 = f32[2,128,1024]{2,1,0:T(8,128)} custom-call(bf16[160,256]{1,0:T(8,128)(2,1)S(1)} %shard_map.125.refs_0_, bf16[160,256]{1,0:T(8,128)(2,1)S(1)} %collective-permute-done.7.refs_1_, bf16[160,256]{1,0:T(8,128)(2,1)S(1)} %collective-permute-done.8.refs_2_, bf16[160,256]{1,0:T(8,128)(2,1)S(1)} %collective-permute-done.9.refs_3_, ...), custom_call_target="tpu_custom_call" | custom-call | tf_op jit(solution)/shard_map/pallas_call | solution.py:472
  67.4 0.0 collective-permute-done.12.refs_1_
  67.4 0.0 collective-permute-done.13.refs_2_
  67.5 0.0 collective-permute-done.14.refs_3_
  67.5 2.6 %shard_map.129 = (f32[2,128,1024]{2,1,0:T(8,128)}, f32[1,8]{1,0:T(1,128)}) custom-call(f32[1,64]{1,0:T(1,128)S(1)} %get-tuple-element.42.refs_0_, f32[1,64]{1,0:T(1,128)S(1)} %collective-permute-done.12.refs_1_, f32[1,64]{1,0:T(1,128)S(1)} %collective-permute-done.13.refs_2_, f32[1,64]{1,0:T(1,128)S(1)} %collective-permute-done.14.refs_3_, ...), custom_call_target="tpu_custom_call" | custom-call | tf_op jit(solution)/shard_map/pallas_call | solution.py:472
Async XLA Ops:
  4.7 36.1 %all-to-all-start = ((bf16[8,48,384]{2,1,0:T(8,128)(2,1)}), bf16[8,48,384]{2,1,0:T(8,128)(2,1)S(1)}, u32[]{:S(2)}, u32[]{:S(2)}) async-start(bf16[8,48,384]{2,1,0:T(8,128)(2,1)} %get-tuple-element.25), calls=%async_computation | async-start | bytes 589824 | tf_op jit(solution)/shard_map/all_to_all | solution.py:527
  13.1 19.5 %collective-permute-start = (bf16[256,512]{1,0:T(8,128)(2,1)S(1)}, bf16[256,512]{1,0:T(8,128)(2,1)S(1)}, u32[]{:S(2)}, u32[]{:S(2)}) collective-permute-start(bf16[256,512]{1,0:T(8,128)(2,1)S(1)} %get-tuple-element.28), channel_id=1, source_target_pairs={{0,4},{4,0},{8,12},{12,8},{16,20},{20,16},{24,28},{28,24},{1,5},{5... | collective-permute-start | bytes 786440 | tf_op jit(solution)/shard_map/ppermute | solution.py:504
  15.1 17.5 %collective-permute-start.1 = (bf16[256,512]{1,0:T(8,128)(2,1)S(1)}, bf16[256,512]{1,0:T(8,128)(2,1)S(1)}, u32[]{:S(2)}, u32[]{:S(2)}) collective-permute-start(bf16[256,512]{1,0:T(8,128)(2,1)S(1)} %get-tuple-element.29), channel_id=1, source_target_pairs={{0,28},{4,8},{8,4},{12,16},{16,12},{20,24},{24,20},{28,0},{1,29},{... | collective-permute-start | bytes 786440 | tf_op jit(solution)/shard_map/ppermute | solution.py:504
  18.4 20.9 %collective-permute-start.2 = (bf16[112,512]{1,0:T(8,128)(2,1)S(1)}, bf16[112,512]{1,0:T(8,128)(2,1)S(1)}, u32[]{:S(2)}, u32[]{:S(2)}) collective-permute-start(bf16[112,512]{1,0:T(8,128)(2,1)S(1)} %get-tuple-element.31), channel_id=1, source_target_pairs={{0,4},{4,0},{8,12},{12,8},{16,20},{20,16},{24,28},{28,24},{1,5},{5... | collective-permute-start | bytes 344072 | tf_op jit(solution)/shard_map/ppermute | solution.py:504
  18.4 22.4 %copy-start = (bf16[2,2,24,512]{3,2,1,0:T(8,128)(2,1)S(1)}, bf16[2,2,24,512]{3,2,1,0:T(8,128)(2,1)}, u32[]{:S(2)}) copy-start(bf16[2,2,24,512]{3,2,1,0:T(8,128)(2,1)} %refs_6_.3) | copy-start | bytes 294916
  18.4 22.4 %copy-start.1 = (bf16[2,2,24,512]{3,2,1,0:T(8,128)(2,1)S(1)}, bf16[2,2,24,512]{3,2,1,0:T(8,128)(2,1)}, u32[]{:S(2)}) copy-start(bf16[2,2,24,512]{3,2,1,0:T(8,128)(2,1)} %refs_4_.3) | copy-start | bytes 294916
  18.4 20.9 %collective-permute-start.4 = (bf16[112,512]{1,0:T(8,128)(2,1)S(1)}, bf16[112,512]{1,0:T(8,128)(2,1)S(1)}, u32[]{:S(2)}, u32[]{:S(2)}) collective-permute-start(bf16[112,512]{1,0:T(8,128)(2,1)S(1)} %get-tuple-element.32), channel_id=1, source_target_pairs={{0,28},{4,8},{8,4},{12,16},{16,12},{20,24},{24,20},{28,0},{1,29},{... | collective-permute-start | bytes 344072 | tf_op jit(solution)/shard_map/ppermute | solution.py:504
  35.1 26.3 %collective-permute-start.10 = (bf16[256,512]{1,0:T(8,128)(2,1)S(1)}, bf16[256,512]{1,0:T(8,128)(2,1)S(1)}, u32[]{:S(2)}, u32[]{:S(2)}) collective-permute-start(bf16[256,512]{1,0:T(8,128)(2,1)S(1)} %get-tuple-element.38), channel_id=1, source_target_pairs={{0,4},{4,0},{8,12},{12,8},{16,20},{20,16},{24,28},{28,24},{1,5},{5... | collective-permute-start | bytes 786440 | tf_op jit(solution)/shard_map/ppermute | solution.py:504
  35.8 25.7 %collective-permute-start.11 = (bf16[256,512]{1,0:T(8,128)(2,1)S(1)}, bf16[256,512]{1,0:T(8,128)(2,1)S(1)}, u32[]{:S(2)}, u32[]{:S(2)}) collective-permute-start(bf16[256,512]{1,0:T(8,128)(2,1)S(1)} %get-tuple-element.39), channel_id=1, source_target_pairs={{0,28},{4,8},{8,4},{12,16},{16,12},{20,24},{24,20},{28,0},{1,29},{... | collective-permute-start | bytes 786440 | tf_op jit(solution)/shard_map/ppermute | solution.py:504
  39.3 1.3 %collective-permute-start.3 = (bf16[112,512]{1,0:T(8,128)(2,1)S(1)}, bf16[112,512]{1,0:T(8,128)(2,1)S(1)}, u32[]{:S(2)}, u32[]{:S(2)}) collective-permute-start(bf16[112,512]{1,0:T(8,128)(2,1)S(1)} %collective-permute-done.2.refs_5_), channel_id=1, source_target_pairs={{0,1},{1,0},{2,3},{3,2},{4,5},{5,4},{6,7},{7,6},{8,9},{9,8},{10,11... | collective-permute-start | bytes 344072 | tf_op jit(solution)/shard_map/ppermute | solution.py:541
  39.3 1.5 %collective-permute-start.5 = (bf16[112,512]{1,0:T(8,128)(2,1)S(1)}, bf16[112,512]{1,0:T(8,128)(2,1)S(1)}, u32[]{:S(2)}, u32[]{:S(2)}) collective-permute-start(bf16[112,512]{1,0:T(8,128)(2,1)S(1)} %collective-permute-done.4.refs_7_), channel_id=1, source_target_pairs={{0,1},{1,0},{2,3},{3,2},{4,5},{5,4},{6,7},{7,6},{8,9},{9,8},{10,11... | collective-permute-start | bytes 344072 | tf_op jit(solution)/shard_map/ppermute | solution.py:541
  43.6 5.0 %collective-permute-start.6 = (bf16[112,256]{1,0:T(8,128)(2,1)S(1)}, bf16[112,256]{1,0:T(8,128)(2,1)S(1)}, u32[]{:S(2)}, u32[]{:S(2)}) collective-permute-start(bf16[112,256]{1,0:T(8,128)(2,1)S(1)} %get-tuple-element.35.refs_0_), channel_id=1, source_target_pairs={{0,4},{4,0},{8,12},{12,8},{16,20},{20,16},{24,28},{28,24},{1,5},{5... | collective-permute-start | bytes 172040 | tf_op jit(solution)/shard_map/ppermute | solution.py:556
  48.7 4.9 %collective-permute-start.7 = (bf16[160,256]{1,0:T(8,128)(2,1)S(1)}, bf16[160,256]{1,0:T(8,128)(2,1)S(1)}, u32[]{:S(2)}, u32[]{:S(2)}) collective-permute-start(bf16[160,256]{1,0:T(8,128)(2,1)S(1)} %shard_map.125.refs_0_), channel_id=1, source_target_pairs={{0,8},{4,12},{8,0},{12,4},{16,24},{20,28},{24,16},{28,20},{1,9},{5... | collective-permute-start | bytes 245768 | tf_op jit(solution)/shard_map/ppermute | solution.py:564
  50.8 7.5 %collective-permute-start.8 = (bf16[160,256]{1,0:T(8,128)(2,1)S(1)}, bf16[160,256]{1,0:T(8,128)(2,1)S(1)}, u32[]{:S(2)}, u32[]{:S(2)}) collective-permute-start(bf16[160,256]{1,0:T(8,128)(2,1)S(1)} %shard_map.125.refs_0_), channel_id=1, source_target_pairs={{0,16},{4,20},{8,24},{12,28},{16,0},{20,4},{24,8},{28,12},{1,17},{... | collective-permute-start | bytes 245768 | tf_op jit(solution)/shard_map/ppermute | solution.py:564
  52.9 6.3 %collective-permute-start.9 = (bf16[160,256]{1,0:T(8,128)(2,1)S(1)}, bf16[160,256]{1,0:T(8,128)(2,1)S(1)}, u32[]{:S(2)}, u32[]{:S(2)}) collective-permute-start(bf16[160,256]{1,0:T(8,128)(2,1)S(1)} %shard_map.125.refs_0_), channel_id=1, source_target_pairs={{0,24},{4,28},{8,16},{12,20},{16,8},{20,12},{24,0},{28,4},{1,25},{... | collective-permute-start | bytes 245768 | tf_op jit(solution)/shard_map/ppermute | solution.py:564
  59.5 8.0 %collective-permute-start.12 = (f32[1,64]{1,0:T(1,128)S(1)}, f32[1,64]{1,0:T(1,128)S(1)}, u32[]{:S(2)}, u32[]{:S(2)}) collective-permute-start(f32[1,64]{1,0:T(1,128)S(1)} %get-tuple-element.42.refs_0_), channel_id=1, source_target_pairs={{0,1},{1,0},{2,3},{3,2},{4,5},{5,4},{6,7},{7,6},{8,9},{9,8},{10,11... | collective-permute-start | bytes 776 | tf_op jit(solution)/shard_map/ppermute | solution.py:570
  59.6 7.9 %collective-permute-start.13 = (f32[1,64]{1,0:T(1,128)S(1)}, f32[1,64]{1,0:T(1,128)S(1)}, u32[]{:S(2)}, u32[]{:S(2)}) collective-permute-start(f32[1,64]{1,0:T(1,128)S(1)} %get-tuple-element.42.refs_0_), channel_id=1, source_target_pairs={{0,2},{1,3},{2,0},{3,1},{4,6},{5,7},{6,4},{7,5},{8,10},{9,11},{10,... | collective-permute-start | bytes 776 | tf_op jit(solution)/shard_map/ppermute | solution.py:570
  61.1 6.3 %collective-permute-start.14 = (f32[1,64]{1,0:T(1,128)S(1)}, f32[1,64]{1,0:T(1,128)S(1)}, u32[]{:S(2)}, u32[]{:S(2)}) collective-permute-start(f32[1,64]{1,0:T(1,128)S(1)} %get-tuple-element.42.refs_0_), channel_id=1, source_target_pairs={{0,3},{1,2},{2,1},{3,0},{4,7},{5,6},{6,5},{7,4},{8,11},{9,10},{10,... | collective-permute-start | bytes 776 | tf_op jit(solution)/shard_map/ppermute | solution.py:570

commit v4 on v3

--- a/solution.py
+++ b/solution.py
@@ -59,6 +59,52 @@
 def sides(near, far):
     even = is_even()
     return jnp.where(even, far, near), jnp.where(even, near, far)
+
+
+def bit_of(b):
+    return lax.rem(lax.axis_index("tile") // b, 2)
+
+
+def fold_bits(n):
+    return [1 << b for b in range(1, n.bit_length() - 2)]
+
+
+def spread_offsets(n):
+    return (1, n // 2, 1 + n // 2)
+
+
+def dealt(n):
+    spread = (0,) + spread_offsets(n)
+    order = [0]
+    for b in fold_bits(n):
+        order = [d + x for d in order for x in (0, b)]
+    return [d + x for d in order for x in spread]
+
+
+def pack(block, rows):
+    lanes, width = block.shape
+    if width < rows:
+        deep = lanes * width // rows
+        return jnp.concatenate([block[a : a + deep] for a in range(0, lanes, deep)], axis=1)
+    return jnp.concatenate([block[:, a : a + rows] for a in range(0, width, rows)], axis=0)
+
+
+def unpack(block, lanes):
+    deep, rows = block.shape
+    if deep < lanes:
+        width = deep * rows // lanes
+        return jnp.concatenate([block[:, a : a + width] for a in range(0, rows, width)], axis=0)
+    return jnp.concatenate([block[a : a + lanes] for a in range(0, deep, lanes)], axis=1)
+
+
+def place(all_ref, gots, n, lanes, skip=0):
+    bits = fold_bits(n)
+    for k, got in zip((0,) + spread_offsets(n), gots):
+        base = jnp.bitwise_and(jnp.bitwise_xor(lax.axis_index("tile"), k), n - 1 - sum(bits))
+        for j in range(1 << len(bits)):
+            device = base + sum(b for f, b in enumerate(bits) if (j >> f) & 1)
+            at = pl.multiple_of(device * lanes, lanes)
+            all_ref[pl.ds(at, lanes), :] = got[skip + j * lanes : skip + (j + 1) * lanes]
 
 
 def stacked(x):
@@ -137,12 +183,10 @@
     return far_of(coeff_t[i * rank : (i + 1) * rank], basis[i, 0], basis[i, 1])
 
 
-def first_kernel(e_ref, k_ref, s_ref, t_ref, c_ref, pr_ref, fl_ref, nb_ref, out, kept, left, right):
+def first_kernel(e_ref, k_ref, s_ref, t_ref, c_ref, pr_ref, fl_ref, nb_ref, out, mine, kept, left, right, keep, *, n):
     tc, tiles = pr_ref.ref.shape
     rank, tile = s_ref.ref.shape[2:]
     lanes = tc * rank
-    n = out.ref.shape[0]
-    width = out.ref.shape[2]
     rows = 2 * e_ref.ref.shape[1]
     columns = tiles * rank
     source = lax.broadcasted_iota(jnp.int32, (tiles, columns), 1) - rank * lax.broadcasted_iota(
@@ -170,10 +214,14 @@
     k = stacked(k_ref[...])
     proj = project(t_ref.get(), [k[:, i * tile : (i + 1) * tile] for i in range(tc)])
     back = tn(m_re, proj.astype(BF16)) + tn(m_im, lanes_turn(proj).astype(BF16))
-    for d in range(n):
-        out.ref[d, :, 0:rows] = coeff
-        out.ref[d, :, rows:width] = back[d * lanes : (d + 1) * lanes].astype(BF16)
-    out.send()
+    order = dealt(n)
+    parts = [back[d * lanes : (d + 1) * lanes] for d in order]
+    upper = bit_of(fold_bits(n)[0]) == 1
+    sent = [coeff.astype(F32)]
+    for low, high, at in zip(parts[: n // 2], parts[n // 2 :], range(n)):
+        mine.ref[at] = jnp.where(upper, high, low)
+        sent.append(pack(jnp.where(upper, low, high), rows))
+    out.ref[...] = jnp.concatenate(sent, axis=0).astype(BF16)
     pair = lax.rem(lax.axis_index("src"), 2)
     part = k_ref.ref.shape[1] // 2
     own = stacked(k_ref.get()[:, pl.ds(pl.multiple_of(pair * part, part), part), :])
@@ -195,6 +243,37 @@
     put(left.ref, right.ref, *sent)
 
 
+def deal_kernel(own_ref, other_ref, part_ref, *outs, n, fold):
+    bits = fold_bits(n)
+    rows = own_ref.ref.shape[1]
+    count, lanes, width = part_ref.ref.shape
+    deep = lanes * width // rows
+    size = own_ref.ref.shape[0] - count * deep
+    own, other = own_ref[...].astype(F32), other_ref[...].astype(F32)
+    upper = bit_of(bits[fold]) == 1
+    both = [jnp.where(upper, other[:size], own[:size]), jnp.where(upper, own[:size], other[:size])]
+    sums = []
+    for at in range(count):
+        begin = size + at * deep
+        sums.append(part_ref[at] + unpack(other[begin : begin + deep], lanes))
+    if fold + 1 < len(bits):
+        out, mine = outs
+        upper = bit_of(bits[fold + 1]) == 1
+        for low, high, at in zip(sums[: count // 2], sums[count // 2 :], range(count)):
+            mine.ref[at] = jnp.where(upper, high, low)
+            both.append(pack(jnp.where(upper, low, high), rows))
+        out.ref[...] = jnp.concatenate(both, axis=0).astype(BF16)
+        return
+    *sent, mine, held = outs
+    for at in range(4):
+        held[at] = sums[at]
+    here = bit_of(1) + 2 * bit_of(n // 2)
+    mine.ref[...] = held[here]
+    for k, out in zip((1, 2, 3), sent):
+        block = pack(held[jnp.bitwise_xor(here, k)], rows)
+        out.ref[...] = jnp.concatenate([*both, block], axis=0).astype(BF16)
+
+
 def moved(k, nb_ref, tile, i, o):
     own = k[:, i * tile : (i + 1) * tile]
     return rows_join(nt(own, nb_ref[i, o, 0]), nt(own, nb_ref[i, o, 1]))
@@ -208,33 +287,31 @@
     return rows_join(p, q)
 
 
-def inside_kernel(v_ref, k_ref, nb_ref, loc, near, early, *, tile, tc):
+def inside_kernel(nb_ref, v_ref, k_ref, start, loc, early, *, tile, tc):
     v, k = v_ref[...], stacked(k_ref[...])
     fields = {i: v[:, i * tile : (i + 1) * tile] for i in range(tc)}
+    early.ref[...] = DAMPING * nt(k, v)
     for m in range(tc):
-        near.ref[:, m * tile : (m + 1) * tile] = near_of(fields, nb_ref, m, [o for o in range(3) if m + o - 1 in fields])
+        cut = slice(m * tile, (m + 1) * tile)
+        inner = [o for o in range(3) if m + o - 1 in fields]
+        start.ref[:, cut] = fields[m].astype(F32) - DAMPING * near_of(fields, nb_ref, m, inner)
         total = None
         for o in range(3):
             if 0 <= m + 1 - o < tc:
                 part = moved(k, nb_ref, tile, m + 1 - o, o)
                 total = part if total is None else total + part
-        cut = slice(m * tile, (m + 1) * tile)
         loc.ref[:, cut] = total
-        loc.send(slice(None), cut)
-    early.ref[...] = DAMPING * nt(k, v)
-
-
-def edge_kernel(near_ref, hl_ref, hr_ref, v_ref, nb_ref, start, left, right, *, tile, tc):
+
+
+def edge_kernel(start_ref, hl_ref, hr_ref, nb_ref, start, left, right, *, tile, tc):
     fields = dict(zip((-1, tc), sides(hl_ref[...], hr_ref[...])))
-    v = v_ref[...]
     ends = {}
     for i in range(tc):
         cut = slice(i * tile, (i + 1) * tile)
-        near = near_ref[:, cut]
+        value = start_ref[:, cut]
         for o in range(3):
             if i + o - 1 in fields:
-                near = near + near_of(fields, nb_ref, i, [o])
-        value = v[:, cut].astype(F32) - DAMPING * near
+                value = value - DAMPING * near_of(fields, nb_ref, i, [o])
         start.ref[:, cut] = value
         ends[i] = value.astype(BF16)
     put(left.ref, right.ref, ends[0], ends[tc - 1])
@@ -242,7 +319,7 @@
 
 def second_near_kernel(*refs, tile, tc):
     fields = {i: refs[i][...] for i in range(tc)}
-    hl_ref, hr_ref, edge_ref, bases_ref, e_ref, nb_ref, out = refs[tc:]
+    hl_ref, hr_ref, edge_ref, bases_ref, nb_ref, e_ref, out = refs[tc:]
     for at, (i, h) in enumerate(zip((-1, tc), sides(hl_ref[...], hr_ref[...]))):
         far = far_of(edge_ref[at], bases_ref[at, 0], bases_ref[at, 1])
         fields[i] = (h.astype(F32) - DAMPING * far).astype(BF16)
@@ -260,9 +337,11 @@
 
 
 def middle_kernel(*refs, tile, tc):
-    got_ref, m_ref, t_ref, start_ref, s_ref, gl_ref, ol_ref, gr_ref, or_ref, early_ref, loc_ref, k_ref = refs[:12]
-    tiles_out, (side, out, edge, bases) = refs[12 : 12 + tc], refs[12 + tc :]
-    n, lanes, _ = got_ref.ref.shape
+    gots, refs = refs[:4], refs[4:]
+    mine_ref, m_ref, t_ref, start_ref, s_ref, gl_ref, ol_ref, gr_ref, or_ref, early_ref, loc_ref, k_ref = refs[:12]
+    tiles_out, (side, out, edge, bases, all_ref) = refs[12 : 12 + tc], refs[12 + tc :]
+    lanes = m_ref.ref.shape[1]
+    n = m_ref.ref.shape[2] // lanes
     rows = out.ref.shape[1]
     focal = k_ref.ref.shape[1]
     rank = t_ref.ref.shape[2]
@@ -288,7 +367,8 @@
     share_l, basis_l, turns_l = whole(gl, ol)
     share_r, basis_r, turns_r = whole(gr, on_right)
 
-    gathered = got_ref[:, :, 0:rows].reshape(columns, rows)
+    place(all_ref, gots, n, lanes)
+    gathered = all_ref[...]
     stack = [
         jnp.concatenate([turns_l[p], m_ref[p].astype(F32), turns_r[p]], axis=0).astype(BF16) for p in range(2)
     ]
@@ -302,7 +382,11 @@
     edge.ref[0], edge.ref[1] = coupled[:rank], coupled[(tc + 1) * rank :]
     for p in range(2):
         bases.ref[0, p], bases.ref[1, p] = basis_l[p], basis_r[p]
-    back = jnp.sum(got_ref[:, :, rows:].astype(F32), axis=0).astype(BF16).astype(F32)
+    back = mine_ref[...]
+    size = lanes << len(fold_bits(n))
+    for got in gots[1:]:
+        back = back + unpack(got[...][size:].astype(F32), lanes)
+    back = back.astype(BF16).astype(F32)
     k = stacked(k_ref[...])
     p = early_ref[...]
     half = rows // 2
@@ -330,9 +414,9 @@
     return lax.broadcasted_iota(jnp.int32, (n, n), 0) == lax.broadcasted_iota(jnp.int32, (n, n), 1)
 
 
-def pair_kernel(own_ref, other_ref, out, *, focal, group):
+def pair_kernel(own_ref, other_ref, out, *, focal, bit):
     lanes = own_ref.ref.shape[0] - focal
-    first = lax.rem(lax.axis_index("tile") // group, 2) == 0
+    first = bit_of(bit) == 0
     own, other = own_ref[...].astype(F32), other_ref[...].astype(F32)
     out.ref[:focal] = (own[:focal] + other[:focal]).astype(BF16)
     out.ref[focal : focal + lanes] = jnp.where(first, own[focal:], other[focal:]).astype(BF16)
@@ -351,7 +435,7 @@
     power.ref[...] = jnp.sum(jnp.where(eye(focal), column, 0.0), axis=0, keepdims=True)
 
 
-def last_kernel(a_ref, b_ref, c_ref, d_ref, foc_ref, target_ref, owner_ref, k_ref, side_ref, adj, res, *, sources, scale):
+def last_kernel(a_ref, b_ref, c_ref, d_ref, foc_ref, side_ref, k_ref, target_ref, owner_ref, adj, res, *, sources, scale):
     focal = foc_ref.ref.shape[0]
     half = foc_ref.ref.shape[1] // 2
     intensity = (a_ref[...] + b_ref[...]) + (c_ref[...] + d_ref[...])
@@ -379,16 +463,13 @@
         adj.send(slice(None), slice(None), cut)
 
 
-def field_kernel(*refs, tile, tc, focal, group):
+def field_kernel(*refs, tile, tc, focal):
     gots, (m_ref, near_ref, t_ref, out) = refs[:-5], refs[-5:-1]
     all_ref = refs[-1]
     rows = all_ref.shape[1]
     half = rows // 2
-    pair = gots[0].ref.shape[0] - focal
-    here = lax.axis_index("tile") // group
-    for k, got in enumerate(gots):
-        at = jnp.bitwise_xor(here, k)
-        all_ref[pl.ds(pl.multiple_of(at * pair, pair), pair), :] = got[focal:]
+    lanes = m_ref.ref.shape[1]
+    place(all_ref, gots, all_ref.shape[0] // lanes, lanes, focal)
     coupled = coupled_of(all_ref[...], m_ref)
     for i in range(tc):
         cut = slice(i * tile, (i + 1) * tile)
@@ -423,11 +504,12 @@
     return math.prod(one.shape[:-1]) * -(-one.shape[-1] // 128) * 128 * jnp.dtype(one.dtype).itemsize
 
 
-def call(kernel, outs, near, far=(), blocks=(), far_outs=(), extra=()):
+def call(kernel, outs, near, far=(), blocks=(), far_outs=(), extra=(), kept=None):
     far = [in_hbm(arg) for arg in far]
     held = [len(blocks) if arg.ndim == 5 and blocks else 0 for arg in far]
     scratch = [
-        pltpu.VMEM((count,) + arg.shape[2:] if count else arg.shape, arg.dtype) for arg, count in zip(far, held)
+        pltpu.VMEM((1, 128) if count and kept is not None else (count,) + arg.shape[2:] if count else arg.shape, arg.dtype)
+        for arg, count in zip(far, held)
     ]
     scratch += [pltpu.VMEM(*outs[o]) for o in far_outs]
     scratch += [pltpu.VMEM(*one) for one in extra]
@@ -450,9 +532,9 @@
             if count:
                 parts = {}
                 for spot, block in enumerate(blocks):
-                    copy = pltpu.make_async_copy(source.at[block], place.at[spot], ins.at[at])
+                    target = place.at[spot] if kept is None else sinks[kept].at[block]
+                    parts[block] = Operand(target, pltpu.make_async_copy(source.at[block], target, ins.at[at]), queue)
                     at += 1
-                    parts[block] = Operand(place.at[spot], copy, queue)
                 operands.append(Blocks(parts))
             else:
                 operands.append(Operand(place, pltpu.make_async_copy(source, place, ins.at[at]), queue))
@@ -496,7 +578,6 @@
     edges = [(0, 0), (tc - 1, 2)]
     inside = [(i, o) for i in range(tc) for o in range(3) if (i, o) not in edges]
     sizes = dict(tile=tile, tc=tc)
-    every = [(i, o) for i in range(tc) for o in range(3)]
     within = [(i, i ^ 1) for i in range(n)]
     across = [(i, (i - 1 + 2 * (i % 2)) % n) for i in range(n)]
 
@@ -514,27 +595,50 @@
         name="ends",
     )(in_hbm(flat))
     hl, hr = exchange(el, er)
-    send, masked, gl, gr = call(
-        first_kernel,
+    deep = lanes * 2 * focal // rows
+    share = focal + rank * (1 + -(-tiles * rank // tile))
+    send, part, masked, gl, gr, keep = call(
+        functools.partial(first_kernel, n=n),
         [
-            ((n, lanes, rows + 2 * focal), BF16),
+            ((lanes + n // 2 * deep, rows), BF16),
+            ((n // 2, lanes, 2 * focal), F32),
             ((2, lanes, tiles * rank), BF16),
-            ((focal + rank * (1 + -(-tiles * rank // tile)), tile), BF16),
-            ((focal + rank * (1 + -(-tiles * rank // tile)), tile), BF16),
+            ((share, tile), BF16),
+            ((share, tile), BF16),
+            (nb.shape, BF16),
         ],
-        [], [e, fk, sb, tb, jnp.swapaxes(coupling, 1, 2), pair_rank.T, far_link.T, nb], blocks=edges,
-    )
-    got = lax.all_to_all(send, "tile", split_axis=0, concat_axis=0, tiled=True)
+        [], [e, fk, sb, tb, jnp.swapaxes(coupling, 1, 2), pair_rank.T, far_link.T, nb],
+        blocks=edges + inside, kept=5,
+    )
+    bits = fold_bits(n)
+    for f, b in enumerate(bits):
+        other = lax.ppermute(send, "tile", [(i, i ^ b) for i in range(n)])
+        count = n >> (f + 1)
+        if f + 1 < len(bits):
+            outs = [
+                ((lanes * (2 << f) + count // 2 * deep, rows), BF16),
+                ((count // 2, lanes, 2 * focal), F32),
+            ]
+        else:
+            outs = [((lanes * (2 << f) + deep, rows), BF16)] * 3 + [((lanes, 2 * focal), F32)]
+        *sent, part = call(
+            functools.partial(deal_kernel, n=n, fold=f), outs, [send, other, part],
+            extra=[((4, lanes, 2 * focal), F32)] if f + 1 == len(bits) else [],
+        )
+        send = sent[0]
+    got = [send] + [
+        lax.ppermute(one, "tile", [(i, i ^ k) for i in range(n)]) for one, k in zip(sent, spread_offsets(n))
+    ]
     from_left, from_right = exchange(gl, gr)
-    loc, near, early = call(
+    start, loc, early = call(
         functools.partial(inside_kernel, **sizes),
-        [((2 * focal, width), F32), ((rows, width), F32), ((2 * focal, rows), F32)],
-        [], [flat, fk, nb], blocks=inside, far_outs=(0,),
+        [((rows, width), F32), ((2 * focal, width), F32), ((2 * focal, rows), F32)],
+        [keep], [flat, fk],
     )
     start, ql, qr = call(
         functools.partial(edge_kernel, **sizes),
         [((rows, width), F32), ((rows, tile), BF16), ((rows, tile), BF16)],
-        [near, hl, hr], [flat, nb], blocks=edges,
+        [start, hl, hr, keep],
     )
     hl1, hr1 = exchange(ql, qr)
     swap = [(i, i ^ 1) for i in range(groups)]
@@ -548,33 +652,30 @@
             ((2, rank, rows), F32),
             ((2, 2, rank, tile), BF16),
         ],
-        [got, masked, tb, start, sb, from_left, other_left, from_right, other_right, early], [loc, fk],
-        far_outs=(tc,),
-    )
-    group = 1
-    while n // group > 4:
-        other = lax.ppermute(send1, "tile", [(i, i ^ group) for i in range(n)])
+        [*got, part, masked, tb, start, sb, from_left, other_left, from_right, other_right, early, loc, fk],
+        extra=[((n * lanes, rows), BF16)],
+    )
+    for f, b in enumerate(fold_bits(n)):
+        other = lax.ppermute(send1, "tile", [(i, i ^ b) for i in range(n)])
         (send1,) = call(
-            functools.partial(pair_kernel, focal=focal, group=group),
-            [((focal + 2 * group * lanes, rows), BF16)], [send1, other],
+            functools.partial(pair_kernel, focal=focal, bit=b),
+            [((focal + (2 << f) * lanes, rows), BF16)], [send1, other],
         )
-        group *= 2
     gots = [send1]
-    for k in range(group, n, group):
-        gots.append(lax.ppermute(send1, "tile", [(i, i ^ k) for i in range(n)]))
+    gots += [lax.ppermute(send1, "tile", [(i, i ^ k) for i in range(n)]) for k in spread_offsets(n)]
     (near1,) = call(
         functools.partial(second_near_kernel, **sizes), [((rows, width), F32)],
-        [*f1, hl1, hr1, edge, bases], [e, nb], blocks=every,
+        [*f1, hl1, hr1, edge, bases, keep], [e],
     )
     foc, part = call(functools.partial(sum_kernel, focal=focal), [((focal, rows), F32), ((1, focal), F32)], gots)
     parts = [part] + [lax.ppermute(part, "src", [(i, i ^ k) for i in range(groups)]) for k in (1, 2, 3)]
     adjoint, residual = call(
         functools.partial(last_kernel, sources=half * groups, scale=(tiles * tile / focal) ** 0.5),
         [((2, half, width), F32), ((1, slots), F32)],
-        [*parts, foc], [target[None], owner[None], fk, side], far_outs=(0, 1),
+        [*parts, foc, side, fk], [target[None], owner[None]], far_outs=(0, 1),
     )
     (field,) = call(
-        functools.partial(field_kernel, focal=focal, group=group, **sizes), [((2, half, width), F32)],
+        functools.partial(field_kernel, focal=focal, **sizes), [((2, half, width), F32)],
         [*gots, masked, near1, tb], far_outs=(0,), extra=[((n * lanes, rows), BF16)],
     )
     return field, residual[0], adjoint

time: 70.4 us -> 69.1 us (0.982)
  Pallas kernels: 24.9 us -> 17.8 us
  waiting for transfers between devices: 18.5 us -> 25.2 us
    ppermute x4 -> x8, waiting for transfers between devices: 11 us -> 20.6 us  [the longest x3 8.46 us: per_device(): lax.ppermute(one, 'tile', [(i, i ^ k) for i in range(n)])]
    all_to_all x1 -> x0, starting transfers between devices: 7.32 us -> none  [per_device(): got = lax.all_to_all(send, 'tile', split_axis=0, concat_axis=0, tiled=True)]
    pallas_call x9 -> x10, Pallas kernels: 23.9 us -> 16.7 us  [call(): pl.pallas_call(run, out_shape=[pltpu.HBM(s, d) if o in far_outs else jax....]
    ppermute x4 -> x8, starting transfers between devices: 4.57 us -> 10.3 us  [the longest x3 5.69 us: per_device(): lax.ppermute(one, 'tile', [(i, i ^ k) for i in range(n)])]
    ppermute x3, waiting for transfers between devices: 6.52 us -> 1.9 us  [exchange(): lax.ppermute(near, 'tile', within)]
    ppermute x3, starting transfers between devices: 2.74 us -> 5.71 us  [exchange(): lax.ppermute(near, 'tile', within)]
    ppermute x3, waiting for transfers between devices: 0.01 us -> 2.7 us  [per_device(): lax.ppermute(part, 'src', [(i, i ^ k) for i in range(groups)])]
    ppermute x3, starting transfers between devices: 8.83 us -> 6.75 us  [exchange(): lax.ppermute(far, 'tile', across)]
  transfers between devices with their start and end apart: 16 -> 19, of which waited for: 7 -> 9; matrix products, arithmetic and copies ran while one was open for 0% -> 0% of each run, Pallas kernels for 26% -> 18%
where the time goes in v4:
time: 69.1 us; the launch traced here: 69 us
  starting transfers between devices  25.2 us (36%)
  waiting for transfers between devices  25.2 us (36%)
  Pallas kernels  17.8 us (26%)
  between operations  0.8 us (1%)
    pallas_call x10, Pallas kernels, call(): pl.pallas_call(run, out_shape=[pltpu.HBM(s, d) if o in far_outs else jax....  16.7 us
    ppermute x3, waiting for transfers between devices, per_device(): lax.ppermute(one, 'tile', [(i, i ^ k) for i in range(n)])  8.46 us
    ppermute x3, starting transfers between devices, exchange(): lax.ppermute(far, 'tile', across)  6.75 us
    ppermute x3, waiting for transfers between devices, per_device(): lax.ppermute(send1, 'tile', [(i, i ^ k) for i in range(n)])  5.83 us
    ppermute x3, starting transfers between devices, exchange(): lax.ppermute(near, 'tile', within)  5.71 us
    ppermute x3, starting transfers between devices, per_device(): lax.ppermute(one, 'tile', [(i, i ^ k) for i in range(n)])  5.69 us
    ppermute x3, starting transfers between devices, per_device(): lax.ppermute(send1, 'tile', [(i, i ^ k) for i in range(n)])  4.44 us
    ppermute x1, waiting for transfers between devices, per_device(): other = lax.ppermute(send1, 'tile', [(i, i ^ b) for i in range(n)])  4.16 us
  transfers between devices with their start and end apart: 19, of which 9 were waited for; matrix products, arithmetic and copies ran while one was open for 0% of the time, Pallas kernels for 18%

profile of v4, /device:TPU:0, one launch (start us, length us, event | category | flops | bytes accessed | tf_op | source)
XLA Modules:
  0.0 69.0 jit_solution(10225919179947521283)
XLA Ops:
  0.6 1.1 %ends.1 = (bf16[256,512]{1,0:T(8,128)(2,1)S(1)}, bf16[256,512]{1,0:T(8,128)(2,1)S(1)}) custom-call(bf16[256,1024]{1,0:T(8,128)(2,1)} %bitcast.7), custom_call_target="tpu_custom_call" | custom-call | tf_op jit(solution)/shard_map/ends/pallas_call | solution.py:588
  1.7 3.1 %collective-permute-start.4 = (bf16[256,512]{1,0:T(8,128)(2,1)S(1)}, bf16[256,512]{1,0:T(8,128)(2,1)S(1)}, u32[]{:S(2)}, u32[]{:S(2)}) collective-permute-start(bf16[256,512]{1,0:T(8,128)(2,1)S(1)} %get-tuple-element.40), channel_id=1, source_target_pairs={{0,4},{4,0},{8,12},{12,8},{16,20},{20,16},{24,28},{28,24},{1,5},{5... | collective-permute-start | bytes 786440 | tf_op jit(solution)/shard_map/ppermute | solution.py:585
  4.8 3.5 %collective-permute-start.5 = (bf16[256,512]{1,0:T(8,128)(2,1)S(1)}, bf16[256,512]{1,0:T(8,128)(2,1)S(1)}, u32[]{:S(2)}, u32[]{:S(2)}) collective-permute-start(bf16[256,512]{1,0:T(8,128)(2,1)S(1)} %get-tuple-element.41), channel_id=1, source_target_pairs={{0,28},{4,8},{8,4},{12,16},{16,12},{20,24},{24,20},{28,0},{1,29},{... | collective-permute-start | bytes 786440 | tf_op jit(solution)/shard_map/ppermute | solution.py:585
  8.3 3.4 %shard_map.121 = (bf16[144,256]{1,0:T(8,128)(2,1)S(1)}, f32[4,48,128]{2,1,0:T(8,128)S(1)}, bf16[2,48,384]{2,1,0:T(8,128)(2,1)S(1)}, bf16[112,512]{1,0:T(8,128)(2...) custom-call(bf16[2,128,1024]{2,1,0:T(8,128)(2,1)} %refs_7_.3, ...), custom_call_target="tpu_custom_call" | custom-call | tf_op jit(solution)/shard_map/pallas_call | solution.py:554
  11.7 0.1 collective-permute-start
  11.8 1.1 %collective-permute-start.6 = (bf16[112,512]{1,0:T(8,128)(2,1)S(1)}, bf16[112,512]{1,0:T(8,128)(2,1)S(1)}, u32[]{:S(2)}, u32[]{:S(2)}) collective-permute-start(bf16[112,512]{1,0:T(8,128)(2,1)S(1)} %get-tuple-element.43), channel_id=1, source_target_pairs={{0,4},{4,0},{8,12},{12,8},{16,20},{20,16},{24,28},{28,24},{1,5},{5... | collective-permute-start | bytes 344072 | tf_op jit(solution)/shard_map/ppermute | solution.py:585
  12.8 1.9 %collective-permute-start.8 = (bf16[112,512]{1,0:T(8,128)(2,1)S(1)}, bf16[112,512]{1,0:T(8,128)(2,1)S(1)}, u32[]{:S(2)}, u32[]{:S(2)}) collective-permute-start(bf16[112,512]{1,0:T(8,128)(2,1)S(1)} %get-tuple-element.44), channel_id=1, source_target_pairs={{0,28},{4,8},{8,4},{12,16},{16,12},{20,24},{24,20},{28,0},{1,29},{... | collective-permute-start | bytes 344072 | tf_op jit(solution)/shard_map/ppermute | solution.py:585
  14.7 2.1 %collective-permute-done.refs_1_ = bf16[144,256]{1,0:T(8,128)(2,1)S(1)} collective-permute-done((bf16[144,256]{1,0:T(8,128)(2,1)S(1)}, bf16[144,256]{1,0:T(8,128)(2,1)S(1)}, u32[]{:S(2)}, u32[]{:S(2)}) %collective-permute-start) | collective-permute-done | bytes 73760 | tf_op jit(solution)/shard_map/ppermute | solution.py:615
  16.9 0.1 shard_map.122
  17.0 0.6 collective-permute-start.1
  17.6 1.9 %collective-permute-done.4.refs_1_ = bf16[256,512]{1,0:T(8,128)(2,1)S(1)} collective-permute-done((bf16[256,512]{1,0:T(8,128)(2,1)S(1)}, bf16[256,512]{1,0:T(8,128)(2,1)S(1)}, u32[]{:S(2)}, u32[]{:S(2)}) %collective-permute-start.4) | collective-permute-done | bytes 262176 | tf_op jit(solution)/shard_map/ppermute | solution.py:585
  19.5 3.6 %collective-permute-start.2 = (bf16[120,256]{1,0:T(8,128)(2,1)S(1)}, bf16[120,256]{1,0:T(8,128)(2,1)S(1)}, u32[]{:S(2)}, u32[]{:S(2)}) collective-permute-start(bf16[120,256]{1,0:T(8,128)(2,1)S(1)} %get-tuple-element.34), channel_id=1, source_target_pairs={{0,16},{4,20},{8,24},{12,28},{16,0},{20,4},{24,8},{28,12},{1,17},{... | collective-permute-start | bytes 184328 | tf_op jit(solution)/shard_map/ppermute | solution.py:630
  23.1 0.0 copy-start
  23.1 0.0 copy-start.1
  23.1 0.0 copy-start.2
  23.1 3.8 %shard_map.123 = (f32[256,1024]{1,0:T(8,128)S(1)}, f32[128,1024]{1,0:T(8,128)S(1)}, f32[128,256]{1,0:T(8,128)S(1)}) custom-call(bf16[2,3,2,512,512]{4,3,2,1,0:T(8,128)(2,1)S(1)} %get-tuple-element.38.refs_0_.refs_3_.refs_6_, bf16[256,1024]{1,0:T(8,128)(2,1)} %bitcast.8, bf16[2,64,1024]{2,1,0:T(8,128)(2,1)} %refs_6_.5), custom_call_target="tpu_custom_call" | custom-call | tf_op jit(solution)/shard_map/pallas_call | solution.py:554
  26.9 0.0 collective-permute-done.5.refs_2_
  26.9 0.9 %shard_map.124 = (f32[256,1024]{1,0:T(8,128)S(1)}, bf16[256,512]{1,0:T(8,128)(2,1)S(1)}, bf16[256,512]{1,0:T(8,128)(2,1)S(1)}) custom-call(f32[256,1024]{1,0:T(8,128)S(1)} %get-tuple-element.39.refs_0_, bf16[256,512]{1,0:T(8,128)(2,1)S(1)} %collective-permute-done.4.refs_1_, bf16[256,512]{1,0:T(8,128)(2,1)S(1)} %collective-permute-done.5.refs_2_, ...), custom_call_target="tpu_custom_call" | custom-call | tf_op jit(solution)/shard_map/pallas_call | solution.py:554
  27.8 1.6 %collective-permute-start.14 = (bf16[256,512]{1,0:T(8,128)(2,1)S(1)}, bf16[256,512]{1,0:T(8,128)(2,1)S(1)}, u32[]{:S(2)}, u32[]{:S(2)}) collective-permute-start(bf16[256,512]{1,0:T(8,128)(2,1)S(1)} %get-tuple-element.50), channel_id=1, source_target_pairs={{0,4},{4,0},{8,12},{12,8},{16,20},{20,16},{24,28},{28,24},{1,5},{5... | collective-permute-start | bytes 786440 | tf_op jit(solution)/shard_map/ppermute | solution.py:585
  29.4 0.0 collective-permute-done.6.refs_9_
  29.4 1.3 %collective-permute-start.15 = (bf16[256,512]{1,0:T(8,128)(2,1)S(1)}, bf16[256,512]{1,0:T(8,128)(2,1)S(1)}, u32[]{:S(2)}, u32[]{:S(2)}) collective-permute-start(bf16[256,512]{1,0:T(8,128)(2,1)S(1)} %get-tuple-element.51), channel_id=1, source_target_pairs={{0,28},{4,8},{8,4},{12,16},{16,12},{20,24},{24,20},{28,0},{1,29},{... | collective-permute-start | bytes 786440 | tf_op jit(solution)/shard_map/ppermute | solution.py:585
  30.7 0.0 collective-permute-done.8.refs_11_
  30.7 0.0 collective-permute-start.7
  30.7 0.0 collective-permute-done.1.refs_1_
  30.7 0.5 collective-permute-start.9
  31.2 0.0 collective-permute-done.2.refs_2_
  31.2 1.5 %collective-permute-start.3 = (bf16[120,256]{1,0:T(8,128)(2,1)S(1)}, bf16[120,256]{1,0:T(8,128)(2,1)S(1)}, u32[]{:S(2)}, u32[]{:S(2)}) collective-permute-start(bf16[120,256]{1,0:T(8,128)(2,1)S(1)} %get-tuple-element.35), channel_id=1, source_target_pairs={{0,20},{4,16},{8,28},{12,24},{16,4},{20,0},{24,12},{28,8},{1,21},{... | collective-permute-start | bytes 184328 | tf_op jit(solution)/shard_map/ppermute | solution.py:630
  32.7 8.5 %collective-permute-done.3.refs_3_ = bf16[120,256]{1,0:T(8,128)(2,1)S(1)} collective-permute-done((bf16[120,256]{1,0:T(8,128)(2,1)S(1)}, bf16[120,256]{1,0:T(8,128)(2,1)S(1)}, u32[]{:S(2)}, u32[]{:S(2)}) %collective-permute-start.3) | collective-permute-done | bytes 61472 | tf_op jit(solution)/shard_map/ppermute | solution.py:630
  41.2 0.0 collective-permute-done.7.refs_10_
  41.2 0.0 collective-permute-done.9.refs_12_
  41.2 0.0 copy-done
  41.2 0.0 copy-done.1
  41.2 0.0 copy-done.2
  41.2 1.6 %shard_map.125 = (bf16[256,512]{1,0:T(8,128)(2,1)S(1)}, bf16[256,512]{1,0:T(8,128)(2,1)S(1)}, bf16[128,1024]{1,0:T(8,128)(2,1)S(1)}, bf16[112,256]{1,0:T(8,128)(...) custom-call(bf16[120,256]{1,0:T(8,128)(2,1)S(1)} %get-tuple-element.33.refs_0_, ...), custom_call_target="tpu_custom_call" | custom-call | tf_op jit(solution)/shard_map/pallas_call | solution.py:554
  42.9 0.1 collective-permute-start.10
  42.9 4.2 %collective-permute-done.10.refs_1_ = bf16[112,256]{1,0:T(8,128)(2,1)S(1)} collective-permute-done((bf16[112,256]{1,0:T(8,128)(2,1)S(1)}, bf16[112,256]{1,0:T(8,128)(2,1)S(1)}, u32[]{:S(2)}, u32[]{:S(2)}) %collective-permute-start.10) | collective-permute-done | bytes 57376 | tf_op jit(solution)/shard_map/ppermute | solution.py:659
  47.1 0.1 shard_map.126.refs_0_
  47.2 0.1 collective-permute-start.11
  47.3 0.4 collective-permute-start.12
  47.7 4.0 %collective-permute-start.13 = (bf16[160,256]{1,0:T(8,128)(2,1)S(1)}, bf16[160,256]{1,0:T(8,128)(2,1)S(1)}, u32[]{:S(2)}, u32[]{:S(2)}) collective-permute-start(bf16[160,256]{1,0:T(8,128)(2,1)S(1)} %shard_map.126.refs_0_), channel_id=1, source_target_pairs={{0,20},{4,16},{8,28},{12,24},{16,4},{20,0},{24,12},{28,8},{1,21},{... | collective-permute-start | bytes 245768 | tf_op jit(solution)/shard_map/ppermute | solution.py:665
  51.7 0.1 collective-permute-done.11.refs_1_
  51.7 3.3 %collective-permute-done.12.refs_2_ = bf16[160,256]{1,0:T(8,128)(2,1)S(1)} collective-permute-done((bf16[160,256]{1,0:T(8,128)(2,1)S(1)}, bf16[160,256]{1,0:T(8,128)(2,1)S(1)}, u32[]{:S(2)}, u32[]{:S(2)}) %collective-permute-start.12) | collective-permute-done | bytes 81952 | tf_op jit(solution)/shard_map/ppermute | solution.py:665
  55.0 2.4 %collective-permute-done.13.refs_3_ = bf16[160,256]{1,0:T(8,128)(2,1)S(1)} collective-permute-done((bf16[160,256]{1,0:T(8,128)(2,1)S(1)}, bf16[160,256]{1,0:T(8,128)(2,1)S(1)}, u32[]{:S(2)}, u32[]{:S(2)}) %collective-permute-start.13) | collective-permute-done | bytes 81952 | tf_op jit(solution)/shard_map/ppermute | solution.py:665
  57.5 0.2 shard_map.129
  57.7 0.1 collective-permute-start.16
  57.8 1.6 %collective-permute-start.17 = (f32[1,64]{1,0:T(1,128)S(1)}, f32[1,64]{1,0:T(1,128)S(1)}, u32[]{:S(2)}, u32[]{:S(2)}) collective-permute-start(f32[1,64]{1,0:T(1,128)S(1)} %get-tuple-element.54.refs_0_), channel_id=1, source_target_pairs={{0,2},{1,3},{2,0},{3,1},{4,6},{5,7},{6,4},{7,5},{8,10},{9,11},{10,... | collective-permute-start | bytes 776 | tf_op jit(solution)/shard_map/ppermute | solution.py:671
  59.3 0.3 collective-permute-start.18
  59.6 0.0 collective-permute-done.16.refs_1_
  59.6 1.8 %collective-permute-done.17.refs_2_ = f32[1,64]{1,0:T(1,128)S(1)} collective-permute-done((f32[1,64]{1,0:T(1,128)S(1)}, f32[1,64]{1,0:T(1,128)S(1)}, u32[]{:S(2)}, u32[]{:S(2)}) %collective-permute-start.17) | collective-permute-done | bytes 288 | tf_op jit(solution)/shard_map/ppermute | solution.py:671
  61.4 0.9 %collective-permute-done.18.refs_3_ = f32[1,64]{1,0:T(1,128)S(1)} collective-permute-done((f32[1,64]{1,0:T(1,128)S(1)}, f32[1,64]{1,0:T(1,128)S(1)}, u32[]{:S(2)}, u32[]{:S(2)}) %collective-permute-start.18) | collective-permute-done | bytes 288 | tf_op jit(solution)/shard_map/ppermute | solution.py:671
  62.3 2.3 %shard_map.130 = (f32[2,128,1024]{2,1,0:T(8,128)}, f32[1,8]{1,0:T(1,128)}) custom-call(f32[1,64]{1,0:T(1,128)S(1)} %get-tuple-element.54.refs_0_, f32[1,64]{1,0:T(1,128)S(1)} %collective-permute-done.16.refs_1_, f32[1,64]{1,0:T(1,128)S(1)} %collective-permute-done.17.refs_2_, f32[1,64]{1,0:T(1,128)S(1)} %collective-permute-done.18.refs_3_, ...), custom_call_target="tpu_custom_call" | custom-call | tf_op jit(solution)/shard_map/pallas_call | solution.py:554
  64.6 0.0 collective-permute-done.14.refs_2_
  64.6 0.0 collective-permute-done.15.refs_3_
  64.6 2.5 %shard_map.127.refs_5_ = f32[256,1024]{1,0:T(8,128)S(1)} custom-call(bf16[256,512]{1,0:T(8,128)(2,1)S(1)} %get-tuple-element.48.refs_0_, bf16[256,512]{1,0:T(8,128)(2,1)S(1)} %get-tuple-element.49.refs_1_, bf16[256,512]{1,0:T(8,128)(2,1)S(1)} %collective-permute-done.14.refs_2_, bf16[256,512]{1,0:T(8,128)(2,1)S(1)} %collective-permute-done.15.refs_3_, ...), custom_call_target="tpu_custom_call" | custom-call | tf_op jit(solution)/shard_map/pallas_call | solution.py:554
  67.1 1.8 %shard_map.128 = f32[2,128,1024]{2,1,0:T(8,128)} custom-call(bf16[160,256]{1,0:T(8,128)(2,1)S(1)} %shard_map.126.refs_0_, bf16[160,256]{1,0:T(8,128)(2,1)S(1)} %collective-permute-done.11.refs_1_, bf16[160,256]{1,0:T(8,128)(2,1)S(1)} %collective-permute-done.12.refs_2_, bf16[160,256]{1,0:T(8,128)(2,1)S(1)} %collective-permute-done.13.refs_3_, ...), custom_call_target="tpu_custom_call" | custom-call | tf_op jit(solution)/shard_map/pallas_call | solution.py:554
Async XLA Ops:
  1.7 17.8 %collective-permute-start.4 = (bf16[256,512]{1,0:T(8,128)(2,1)S(1)}, bf16[256,512]{1,0:T(8,128)(2,1)S(1)}, u32[]{:S(2)}, u32[]{:S(2)}) collective-permute-start(bf16[256,512]{1,0:T(8,128)(2,1)S(1)} %get-tuple-element.40), channel_id=1, source_target_pairs={{0,4},{4,0},{8,12},{12,8},{16,20},{20,16},{24,28},{28,24},{1,5},{5... | collective-permute-start | bytes 786440 | tf_op jit(solution)/shard_map/ppermute | solution.py:585
  4.8 22.2 %collective-permute-start.5 = (bf16[256,512]{1,0:T(8,128)(2,1)S(1)}, bf16[256,512]{1,0:T(8,128)(2,1)S(1)}, u32[]{:S(2)}, u32[]{:S(2)}) collective-permute-start(bf16[256,512]{1,0:T(8,128)(2,1)S(1)} %get-tuple-element.41), channel_id=1, source_target_pairs={{0,28},{4,8},{8,4},{12,16},{16,12},{20,24},{24,20},{28,0},{1,29},{... | collective-permute-start | bytes 786440 | tf_op jit(solution)/shard_map/ppermute | solution.py:585
  11.7 5.2 %collective-permute-start = (bf16[144,256]{1,0:T(8,128)(2,1)S(1)}, bf16[144,256]{1,0:T(8,128)(2,1)S(1)}, u32[]{:S(2)}, u32[]{:S(2)}) collective-permute-start(bf16[144,256]{1,0:T(8,128)(2,1)S(1)} %get-tuple-element.31.refs_0_), channel_id=1, source_target_pairs={{0,8},{4,12},{8,0},{12,4},{16,24},{20,28},{24,16},{28,20},{1,9},{5... | collective-permute-start | bytes 221192 | tf_op jit(solution)/shard_map/ppermute | solution.py:615
  11.8 17.6 %collective-permute-start.6 = (bf16[112,512]{1,0:T(8,128)(2,1)S(1)}, bf16[112,512]{1,0:T(8,128)(2,1)S(1)}, u32[]{:S(2)}, u32[]{:S(2)}) collective-permute-start(bf16[112,512]{1,0:T(8,128)(2,1)S(1)} %get-tuple-element.43), channel_id=1, source_target_pairs={{0,4},{4,0},{8,12},{12,8},{16,20},{20,16},{24,28},{28,24},{1,5},{5... | collective-permute-start | bytes 344072 | tf_op jit(solution)/shard_map/ppermute | solution.py:585
  12.8 17.9 %collective-permute-start.8 = (bf16[112,512]{1,0:T(8,128)(2,1)S(1)}, bf16[112,512]{1,0:T(8,128)(2,1)S(1)}, u32[]{:S(2)}, u32[]{:S(2)}) collective-permute-start(bf16[112,512]{1,0:T(8,128)(2,1)S(1)} %get-tuple-element.44), channel_id=1, source_target_pairs={{0,28},{4,8},{8,4},{12,16},{16,12},{20,24},{24,20},{28,0},{1,29},{... | collective-permute-start | bytes 344072 | tf_op jit(solution)/shard_map/ppermute | solution.py:585
  17.0 13.7 %collective-permute-start.1 = (bf16[120,256]{1,0:T(8,128)(2,1)S(1)}, bf16[120,256]{1,0:T(8,128)(2,1)S(1)}, u32[]{:S(2)}, u32[]{:S(2)}) collective-permute-start(bf16[120,256]{1,0:T(8,128)(2,1)S(1)} %get-tuple-element.33.refs_0_), channel_id=1, source_target_pairs={{0,4},{4,0},{8,12},{12,8},{16,20},{20,16},{24,28},{28,24},{1,5},{5... | collective-permute-start | bytes 184328 | tf_op jit(solution)/shard_map/ppermute | solution.py:630
  19.5 11.7 %collective-permute-start.2 = (bf16[120,256]{1,0:T(8,128)(2,1)S(1)}, bf16[120,256]{1,0:T(8,128)(2,1)S(1)}, u32[]{:S(2)}, u32[]{:S(2)}) collective-permute-start(bf16[120,256]{1,0:T(8,128)(2,1)S(1)} %get-tuple-element.34), channel_id=1, source_target_pairs={{0,16},{4,20},{8,24},{12,28},{16,0},{20,4},{24,8},{28,12},{1,17},{... | collective-permute-start | bytes 184328 | tf_op jit(solution)/shard_map/ppermute | solution.py:630
  23.1 18.1 %copy-start = (bf16[2,64,1024]{2,1,0:T(8,128)(2,1)S(1)}, bf16[2,64,1024]{2,1,0:T(8,128)(2,1)}, u32[]{:S(2)}) copy-start(bf16[2,64,1024]{2,1,0:T(8,128)(2,1)} %refs_6_.5) | copy-start | bytes 786436
  23.1 18.1 %copy-start.1 = (bf16[2,2,24,512]{3,2,1,0:T(8,128)(2,1)S(1)}, bf16[2,2,24,512]{3,2,1,0:T(8,128)(2,1)}, u32[]{:S(2)}) copy-start(bf16[2,2,24,512]{3,2,1,0:T(8,128)(2,1)} %refs_6_.4) | copy-start | bytes 294916
  23.1 18.1 %copy-start.2 = (bf16[2,2,24,512]{3,2,1,0:T(8,128)(2,1)S(1)}, bf16[2,2,24,512]{3,2,1,0:T(8,128)(2,1)}, u32[]{:S(2)}) copy-start(bf16[2,2,24,512]{3,2,1,0:T(8,128)(2,1)} %refs_8_.1) | copy-start | bytes 294916
  27.8 36.8 %collective-permute-start.14 = (bf16[256,512]{1,0:T(8,128)(2,1)S(1)}, bf16[256,512]{1,0:T(8,128)(2,1)S(1)}, u32[]{:S(2)}, u32[]{:S(2)}) collective-permute-start(bf16[256,512]{1,0:T(8,128)(2,1)S(1)} %get-tuple-element.50), channel_id=1, source_target_pairs={{0,4},{4,0},{8,12},{12,8},{16,20},{20,16},{24,28},{28,24},{1,5},{5... | collective-permute-start | bytes 786440 | tf_op jit(solution)/shard_map/ppermute | solution.py:585
  29.4 35.2 %collective-permute-start.15 = (bf16[256,512]{1,0:T(8,128)(2,1)S(1)}, bf16[256,512]{1,0:T(8,128)(2,1)S(1)}, u32[]{:S(2)}, u32[]{:S(2)}) collective-permute-start(bf16[256,512]{1,0:T(8,128)(2,1)S(1)} %get-tuple-element.51), channel_id=1, source_target_pairs={{0,28},{4,8},{8,4},{12,16},{16,12},{20,24},{24,20},{28,0},{1,29},{... | collective-permute-start | bytes 786440 | tf_op jit(solution)/shard_map/ppermute | solution.py:585
  30.7 10.5 %collective-permute-start.7 = (bf16[112,512]{1,0:T(8,128)(2,1)S(1)}, bf16[112,512]{1,0:T(8,128)(2,1)S(1)}, u32[]{:S(2)}, u32[]{:S(2)}) collective-permute-start(bf16[112,512]{1,0:T(8,128)(2,1)S(1)} %collective-permute-done.6.refs_9_), channel_id=1, source_target_pairs={{0,1},{1,0},{2,3},{3,2},{4,5},{5,4},{6,7},{7,6},{8,9},{9,8},{10,11... | collective-permute-start | bytes 344072 | tf_op jit(solution)/shard_map/ppermute | solution.py:645
  30.7 10.5 %collective-permute-start.9 = (bf16[112,512]{1,0:T(8,128)(2,1)S(1)}, bf16[112,512]{1,0:T(8,128)(2,1)S(1)}, u32[]{:S(2)}, u32[]{:S(2)}) collective-permute-start(bf16[112,512]{1,0:T(8,128)(2,1)S(1)} %collective-permute-done.8.refs_11_), channel_id=1, source_target_pairs={{0,1},{1,0},{2,3},{3,2},{4,5},{5,4},{6,7},{7,6},{8,9},{9,8},{10,11... | collective-permute-start | bytes 344072 | tf_op jit(solution)/shard_map/ppermute | solution.py:645
  31.2 10.0 %collective-permute-start.3 = (bf16[120,256]{1,0:T(8,128)(2,1)S(1)}, bf16[120,256]{1,0:T(8,128)(2,1)S(1)}, u32[]{:S(2)}, u32[]{:S(2)}) collective-permute-start(bf16[120,256]{1,0:T(8,128)(2,1)S(1)} %get-tuple-element.35), channel_id=1, source_target_pairs={{0,20},{4,16},{8,28},{12,24},{16,4},{20,0},{24,12},{28,8},{1,21},{... | collective-permute-start | bytes 184328 | tf_op jit(solution)/shard_map/ppermute | solution.py:630
  42.9 4.2 %collective-permute-start.10 = (bf16[112,256]{1,0:T(8,128)(2,1)S(1)}, bf16[112,256]{1,0:T(8,128)(2,1)S(1)}, u32[]{:S(2)}, u32[]{:S(2)}) collective-permute-start(bf16[112,256]{1,0:T(8,128)(2,1)S(1)} %get-tuple-element.47.refs_0_), channel_id=1, source_target_pairs={{0,8},{4,12},{8,0},{12,4},{16,24},{20,28},{24,16},{28,20},{1,9},{5... | collective-permute-start | bytes 172040 | tf_op jit(solution)/shard_map/ppermute | solution.py:659
  47.2 4.5 %collective-permute-start.11 = (bf16[160,256]{1,0:T(8,128)(2,1)S(1)}, bf16[160,256]{1,0:T(8,128)(2,1)S(1)}, u32[]{:S(2)}, u32[]{:S(2)}) collective-permute-start(bf16[160,256]{1,0:T(8,128)(2,1)S(1)} %shard_map.126.refs_0_), channel_id=1, source_target_pairs={{0,4},{4,0},{8,12},{12,8},{16,20},{20,16},{24,28},{28,24},{1,5},{5... | collective-permute-start | bytes 245768 | tf_op jit(solution)/shard_map/ppermute | solution.py:665
  47.3 7.8 %collective-permute-start.12 = (bf16[160,256]{1,0:T(8,128)(2,1)S(1)}, bf16[160,256]{1,0:T(8,128)(2,1)S(1)}, u32[]{:S(2)}, u32[]{:S(2)}) collective-permute-start(bf16[160,256]{1,0:T(8,128)(2,1)S(1)} %shard_map.126.refs_0_), channel_id=1, source_target_pairs={{0,16},{4,20},{8,24},{12,28},{16,0},{20,4},{24,8},{28,12},{1,17},{... | collective-permute-start | bytes 245768 | tf_op jit(solution)/shard_map/ppermute | solution.py:665
  47.7 9.8 %collective-permute-start.13 = (bf16[160,256]{1,0:T(8,128)(2,1)S(1)}, bf16[160,256]{1,0:T(8,128)(2,1)S(1)}, u32[]{:S(2)}, u32[]{:S(2)}) collective-permute-start(bf16[160,256]{1,0:T(8,128)(2,1)S(1)} %shard_map.126.refs_0_), channel_id=1, source_target_pairs={{0,20},{4,16},{8,28},{12,24},{16,4},{20,0},{24,12},{28,8},{1,21},{... | collective-permute-start | bytes 245768 | tf_op jit(solution)/shard_map/ppermute | solution.py:665
  57.7 1.9 %collective-permute-start.16 = (f32[1,64]{1,0:T(1,128)S(1)}, f32[1,64]{1,0:T(1,128)S(1)}, u32[]{:S(2)}, u32[]{:S(2)}) collective-permute-start(f32[1,64]{1,0:T(1,128)S(1)} %get-tuple-element.54.refs_0_), channel_id=1, source_target_pairs={{0,1},{1,0},{2,3},{3,2},{4,5},{5,4},{6,7},{7,6},{8,9},{9,8},{10,11... | collective-permute-start | bytes 776 | tf_op jit(solution)/shard_map/ppermute | solution.py:671
  57.8 3.6 %collective-permute-start.17 = (f32[1,64]{1,0:T(1,128)S(1)}, f32[1,64]{1,0:T(1,128)S(1)}, u32[]{:S(2)}, u32[]{:S(2)}) collective-permute-start(f32[1,64]{1,0:T(1,128)S(1)} %get-tuple-element.54.refs_0_), channel_id=1, source_target_pairs={{0,2},{1,3},{2,0},{3,1},{4,6},{5,7},{6,4},{7,5},{8,10},{9,11},{10,... | collective-permute-start | bytes 776 | tf_op jit(solution)/shard_map/ppermute | solution.py:671
  59.3 3.0 %collective-permute-start.18 = (f32[1,64]{1,0:T(1,128)S(1)}, f32[1,64]{1,0:T(1,128)S(1)}, u32[]{:S(2)}, u32[]{:S(2)}) collective-permute-start(f32[1,64]{1,0:T(1,128)S(1)} %get-tuple-element.54.refs_0_), channel_id=1, source_target_pairs={{0,3},{1,2},{2,1},{3,0},{4,7},{5,6},{6,5},{7,4},{8,11},{9,10},{10,... | collective-permute-start | bytes 776 | tf_op jit(solution)/shard_map/ppermute | solution.py:671
